TPU v7x, 128 devices: a whole 4x4x4 slice. The times are simulated.
128 devices in a mesh: axial: 4 (over x), azim: 32 (over z, y, core).
Axes of the slice: x: 4, y: 4, z: 4, core: 2. Of those that a mesh axis runs over, the one named last changes fastest.
Arguments:
- density: float32 [64, 256, 512], P(None, 'azim', 'axial'), may hold values from 0.5 to 2
- velocity: float32 [3, 64, 256, 512], P(None, None, 'azim', 'axial'), may hold values from -3 to 3
- pressure: float32 [64, 256, 512], P(None, 'azim', 'axial'), may hold values from 0.4 to 1.5
- axial_metric: float32 [3, 64, 256, 512], P(None, None, 'azim', 'axial'), may hold values from -4 to 4
- azim_metric: float32 [3, 64, 256, 512], P(None, None, 'azim', 'axial'), may hold values from -4 to 4
- volume: float32 [64, 256, 512], P(None, 'azim', 'axial'), may hold values from 0.5 to 2
- radial_term: float32 [5, 64, 256, 512], P(None, None, 'azim', 'axial'), may hold values from -6 to 6
- panel_area: float32 [256, 512], P('azim', 'axial'), may hold values from 0.5 to 2
- observer_ids: int32 [4, 256, 512], P(None, 'azim', 'axial'), may hold values from 0 to 511
- bin_ids: int32 [4, 256, 512], P(None, 'azim', 'axial'), may hold values from 0 to 127
- weight_ids: int32 [4, 256, 512], P(None, 'azim', 'axial'), may hold values from 0 to 255
- bin_weights: float32 [256], replicated, may hold values from 0.2 to 1
Outputs:
- new_state: float32 [5, 64, 256, 512], P(None, None, 'azim', 'axial')
- signals: float32 [512, 128], P(('axial', 'azim'))
All inputs are finite; a program needn't handle non-finite values.
Results may differ from a plain program's by a relative error of at most 0.0003.
Values sent between devices are 32-bit elements; how exact they have to be, the bound alone decides.
A program may use at most 128 MiB of HBM per device.

v0:
```python
import math

import jax
import jax.numpy as jnp
from jax import lax
from jax.sharding import PartitionSpec as P

OBSERVERS = 512
TIME_BINS = 128


GAMMA = 1.4
SECTION = 0.25
DERIV_ALPHA = 1.0 / 3.0
FILTER_ALPHA = 0.499
DERIV_A = 14.0 / 9.0
DERIV_B = 1.0 / 9.0
HIGHEST = lax.Precision.HIGHEST


def padded(cells, sides, width, closed):
    for axis, dim in sides:
        count = lax.axis_size(axis)
        ends = count if closed else count - 1
        head = lax.slice_in_dim(cells, 0, width, axis=dim)
        tail = lax.slice_in_dim(cells, cells.shape[dim] - width, cells.shape[dim], axis=dim)
        cells = jnp.concatenate(
            [
                lax.ppermute(tail, axis, [(i, (i + 1) % count) for i in range(ends)]),
                cells,
                lax.ppermute(head, axis, [((i + 1) % count, i) for i in range(ends)]),
            ],
            axis=dim,
        )
    return cells


def decay_root(alpha):
    return (-1.0 + math.sqrt(1.0 - 4.0 * alpha * alpha)) / (2.0 * alpha)


def signed_power(base, exponent):
    exponent = jnp.asarray(exponent)
    parity = jnp.where(exponent % 2 == 0, 1.0, -1.0)
    return parity * jnp.exp(exponent.astype(jnp.float32) * math.log(-base))


def deriv_side(extended, dim):
    length = extended.shape[dim] - 6

    def cells(offset):
        return lax.slice_in_dim(extended, 3 + offset, 3 + offset + length, axis=dim)

    return 0.5 * DERIV_A * (cells(1) - cells(-1)) + 0.25 * DERIV_B * (cells(2) - cells(-2))


def filter_side(extended, dim):
    length = extended.shape[dim] - 6

    def cells(offset):
        return lax.slice_in_dim(extended, 3 + offset, 3 + offset + length, axis=dim)

    beta = FILTER_ALPHA
    coeffs = [
        (11.0 + 10.0 * beta) / 16.0,
        (15.0 + 34.0 * beta) / 32.0,
        (-3.0 + 6.0 * beta) / 16.0,
        (1.0 - 2.0 * beta) / 32.0,
    ]
    total = coeffs[0] * cells(0)
    for shift in range(1, 4):
        total = total + 0.5 * coeffs[shift] * (cells(shift) + cells(-shift))
    return total


def fluxes(density, velocity, pressure, energy, metric, volume):
    contra = metric[0] * velocity[0] + metric[1] * velocity[1] + metric[2] * velocity[2]
    mass_flow = density * contra
    pieces = [volume * mass_flow]
    for comp in range(3):
        pieces.append(volume * (mass_flow * velocity[comp] + metric[comp] * pressure))
    pieces.append(volume * (energy + pressure) * contra)
    return jnp.stack(pieces)


def pad_axial(field):
    return padded(field, (("axial", 3),), 3, False)


def pad_azimuth(field):
    return padded(field, (("azim", 2),), 3, True)


def open_line(rhs, alpha):
    base = decay_root(alpha)
    factor_g = -alpha / base
    scale = 1.0 / (factor_g * (1.0 - base * base))
    width_here = rhs.shape[3]
    group_size = lax.axis_size("axial")
    device_pos = lax.axis_index("axial")
    total_len = width_here * group_size
    offsets = jnp.arange(width_here, dtype=jnp.int32)
    local_matrix = signed_power(base, jnp.abs(offsets[:, None] - offsets[None, :]))
    local_part = jnp.einsum("vraj,ij->vrai", rhs, local_matrix, precision=HIGHEST)
    first_moment = jnp.einsum(
        "vraj,j->vra", rhs, signed_power(base, width_here - 1 - offsets), precision=HIGHEST
    )
    last_moment = jnp.einsum("vraj,j->vra", rhs, signed_power(base, offsets), precision=HIGHEST)
    moments = jnp.stack([first_moment, last_moment])[None]
    piece = lax.all_gather(moments, "axial", axis=0, tiled=True)
    others = jnp.arange(piece.shape[0], dtype=jnp.int32)
    gap_up = device_pos - others
    w_left = jnp.where(
        gap_up > 0, signed_power(base, width_here * jnp.maximum(gap_up - 1, 0) + 1), 0.0
    )
    w_right = jnp.where(
        gap_up < 0, signed_power(base, width_here * jnp.maximum(-gap_up - 1, 0) + 1), 0.0
    )
    w_end = signed_power(base, width_here * (group_size - 1 - others))
    left_sum = jnp.einsum("k,kvra->vra", w_left, piece[:, 0], precision=HIGHEST)
    right_sum = jnp.einsum("k,kvra->vra", w_right, piece[:, 1], precision=HIGHEST)
    end_sum = jnp.einsum("k,kvra->vra", w_end, piece[:, 0], precision=HIGHEST)
    left_sum, right_sum, end_sum = (left_sum, right_sum, end_sum)
    position = device_pos * width_here + offsets
    result = local_part + signed_power(base, offsets) * left_sum[..., None]
    result = result + signed_power(base, width_here - 1 - offsets) * right_sum[..., None]
    result = result - signed_power(base, total_len + 1 - position) * end_sum[..., None]
    return scale * result


def cycle_line(rhs, alpha):
    base = decay_root(alpha)
    factor_g = -alpha / base
    width_here = rhs.shape[2]
    group_size = lax.axis_size("azim")
    device_pos = lax.axis_index("azim")
    total_len = width_here * group_size
    scale = 1.0 / (factor_g * (1.0 - base * base) * (1.0 - base**total_len))
    offsets = jnp.arange(width_here, dtype=jnp.int32)
    gap = jnp.abs(offsets[:, None] - offsets[None, :])
    local_matrix = scale * (signed_power(base, gap) + signed_power(base, total_len - gap))
    local_part = jnp.einsum("vrjx,ij->vrix", rhs, local_matrix, precision=HIGHEST)
    first_moment = jnp.einsum(
        "vrjx,j->vrx", rhs, signed_power(base, width_here - 1 - offsets), precision=HIGHEST
    )
    last_moment = jnp.einsum("vrjx,j->vrx", rhs, signed_power(base, offsets), precision=HIGHEST)
    moments = jnp.stack([first_moment, last_moment])[None]
    piece = lax.all_gather(moments, "azim", axis=0, tiled=True)
    others = jnp.arange(piece.shape[0], dtype=jnp.int32)
    shift = (device_pos - others) % group_size
    w_first = jnp.where(
        shift > 0, signed_power(base, width_here * jnp.maximum(shift - 1, 0) + 1), 0.0
    )
    w_last = jnp.where(
        shift > 0, signed_power(base, width_here * jnp.maximum(group_size - shift - 1, 0) + 1), 0.0
    )
    first_sum = jnp.einsum("k,kvrx->vrx", w_first, piece[:, 0], precision=HIGHEST)
    last_sum = jnp.einsum("k,kvrx->vrx", w_last, piece[:, 1], precision=HIGHEST)
    outer = signed_power(base, offsets)[:, None] * first_sum[:, :, None, :]
    outer = outer + signed_power(base, width_here - 1 - offsets)[:, None] * last_sum[:, :, None, :]
    return local_part + scale * outer


def per_device(
    density,
    velocity,
    pressure,
    axial_metric,
    azim_metric,
    volume,
    radial_term,
    panel_area,
    observer_ids,
    bin_ids,
    weight_ids,
    bin_weights,
):
    energy = pressure / (GAMMA - 1.0) + 0.5 * density * (
        velocity[0] ** 2 + velocity[1] ** 2 + velocity[2] ** 2
    )
    state = jnp.concatenate([density[None], density[None] * velocity, energy[None]], axis=0)
    axial_flux = fluxes(density, velocity, pressure, energy, axial_metric, volume)
    azim_flux = fluxes(density, velocity, pressure, energy, azim_metric, volume)
    axial_deriv = open_line(deriv_side(pad_axial(axial_flux), 3), DERIV_ALPHA)
    azim_deriv = cycle_line(deriv_side(pad_azimuth(azim_flux), 2), DERIV_ALPHA)
    sectioned = state + SECTION * (radial_term - (axial_deriv + azim_deriv) / volume)
    smoothed = open_line(filter_side(pad_axial(sectioned), 3), FILTER_ALPHA)
    new_state = cycle_line(filter_side(pad_azimuth(smoothed), 2), FILTER_ALPHA)
    surface = new_state[:, 0]
    source = panel_area * (surface[2] + surface[0] - 1.0)
    table_size = bin_weights.shape[0]
    one_hot = (
        weight_ids.reshape(-1)[:, None] == jnp.arange(table_size, dtype=jnp.int32)[None, :]
    ).astype(jnp.float32)
    entry_weight = jnp.dot(one_hot, bin_weights, precision=HIGHEST)
    values = entry_weight * jnp.broadcast_to(source[None], weight_ids.shape).reshape(-1)
    bucket = (observer_ids * TIME_BINS + bin_ids).reshape(-1)
    partial_signals = jax.ops.segment_sum(
        values, bucket, num_segments=OBSERVERS * TIME_BINS
    ).reshape(OBSERVERS, TIME_BINS)
    signals = lax.psum_scatter(partial_signals, ("axial", "azim"), scatter_dimension=0, tiled=True)
    return (new_state, signals)


def solution(mesh):
    placed = (
        P(None, "azim", "axial"),
        P(None, None, "azim", "axial"),
        P(None, "azim", "axial"),
        P(None, None, "azim", "axial"),
        P(None, None, "azim", "axial"),
        P(None, "azim", "axial"),
        P(None, None, "azim", "axial"),
        P("azim", "axial"),
        P(None, "azim", "axial"),
        P(None, "azim", "axial"),
        P(None, "azim", "axial"),
        P(),
    )
    return jax.shard_map(
        per_device,
        mesh=mesh,
        in_specs=placed,
        out_specs=(P(None, None, "azim", "axial"), P(("axial", "azim"), None)),
        check_vma=False,
    )
```

profile of v0, /device:TPU:1, one launch (start us, length us, event | category | flops | bytes accessed | tf_op | source)
XLA Modules:
  0.0 457.6 jit_solution(16983114548345051890)
XLA Ops:
  7.3 2.7 bitcast_dynamic-update-slice_fusion.4
  15.6 6.4 %collective-permute-done.2 = f32[5,64,3,128]{3,1,2,0:T(8,128)S(1)} collective-permute-done((f32[5,64,3,128]{3,1,2,0:T(8,128)S(1)}, f32[5,64,3,128]{3,1,2,0:T(8,128)S(1)}, u32[]{:S(2)}, u32[]{:S(2)}) %collective-permute-start.2) | collective-permute-done | bytes 491552 | tf_op jit(solution)/shard_map/ppermute | solution.py:31
  28.7 1.8 copy.14
  32.8 4.5 collective-permute-start.1
  37.9 1.9 broadcast_multiply_fusion.1
  39.9 1.6 copy.15
  43.0 5.7 %fusion.30 = f32[5,64,8,128]{3,2,1,0:T(8,128)S(1)} fusion(f32[5,64,8,3]{3,2,1,0:T(8,128)} %copy.17, f32[5,64,8,128]{3,2,1,0:T(8,128)S(1)} %bitcast_dynamic-update-slice_fusion.5, f32[5,64,8,3]{3,2,1,0:T(8,128)} %copy.15), kind=kLoop, calls=%fused_computation.64 | loop fusion | flops 2949120 | bytes 2682880 | tf_op jit(solution)/shard_map/add | solution.py:54
  48.7 17.3 %fusion.215 = f32[1,5,64,8]{3,0,2,1:T(1,128)S(1)} fusion(f32[5,64,8,128]{3,2,1,0:T(8,128)S(1)} %fusion.30), kind=kOutput, calls=%fused_computation.350 | convolution fusion | flops 3934336 | bytes 1320960 | tf_op jit(solution)/shard_map/vraj,j->vra/dot_general | solution.py:105
  66.1 17.5 %fusion.213 = f32[1,5,64,8]{3,0,2,1:T(1,128)S(1)} fusion(f32[5,64,8,128]{3,2,1,0:T(8,128)S(1)} %fusion.30), kind=kOutput, calls=%fused_computation.348 | convolution fusion | flops 3933568 | bytes 1320960 | tf_op jit(solution)/shard_map/vraj,j->vra/dot_general | solution.py:108
  83.7 9.9 %all-gather = f32[8,5,64,8]{2,3,1,0:T(8,128)S(1)} all-gather(f32[2,5,64,8]{2,3,1,0:T(8,128)S(1)} %pad_maximum_fusion.10), channel_id=2, replica_groups=mesh['axial'=4,'azim'=32] {'axial'}, dimensions={0}, use_global_device_ids=true | all-gather | bytes 102400 | tf_op jit(solution)/shard_map/all_gather | solution.py:110
  94.9 2.5 fusion.19
  97.4 5.2 %slice_bitcast_fusion.3 = (f32[32,5,64,128]{3,2,1,0:T(8,128)S(1)}, f32[32,5,64,128]{3,2,1,0:T(8,128)S(1)}) fusion(f32[32,2,5,64,128]{4,3,2,1,0:T(8,128)} %bitcast.355), kind=kLoop, calls=%fused_computation.4 | loop fusion | bytes 20971520 | tf_op jit(solution)/shard_map/squeeze | solution.py:157
  102.6 5.4 %fusion.6 = f32[1,5,64,128]{3,0,2,1:T(1,128)S(1)} fusion(f32[32,5,64,128]{3,2,1,0:T(8,128)S(1)} %get-tuple-element.12, s32[]{:T(128)S(6)} %axis_index.33), kind=kOutput, calls=%fused_computation.11 | convolution fusion | flops 15729728 | bytes 5406724 | tf_op jit(solution)/shard_map/k,kvrx->vrx/dot_general | solution.py:157
  108.1 5.8 %fusion.4 = f32[1,5,64,128]{3,0,2,1:T(1,128)S(1)} fusion(f32[32,5,64,128]{3,2,1,0:T(8,128)S(1)} %get-tuple-element.13, s32[]{:T(128)S(6)} %axis_index.33), kind=kOutput, calls=%fused_computation.9 | convolution fusion | flops 15729728 | bytes 5406724 | tf_op jit(solution)/shard_map/k,kvrx->vrx/dot_general | solution.py:158
  114.0 1.8 fusion.21
  117.3 1.8 copy.22
  120.8 4.0 collective-permute-start.5
  128.0 6.2 %fusion.47 = f32[5,64,8,128]{3,2,1,0:T(8,128)S(1)} fusion(f32[5,64,8,3]{3,2,1,0:T(8,128)} %copy.25, f32[5,64,8,128]{3,2,1,0:T(8,128)S(1)} %fusion.21, f32[5,64,8,3]{3,2,1,0:T(8,128)} %copy.23), kind=kLoop, calls=%fused_computation.81 | loop fusion | flops 5242880 | bytes 2682880 | tf_op jit(solution)/shard_map/add | solution.py:72
  134.2 17.3 %fusion.204 = f32[1,5,64,8]{3,0,2,1:T(1,128)S(1)} fusion(f32[5,64,8,128]{3,2,1,0:T(8,128)S(1)} %fusion.47), kind=kOutput, calls=%fused_computation.339 | convolution fusion | flops 3934336 | bytes 1320960 | tf_op jit(solution)/shard_map/vraj,j->vra/dot_general | solution.py:105
  151.5 17.5 %fusion.202 = f32[1,5,64,8]{3,0,2,1:T(1,128)S(1)} fusion(f32[5,64,8,128]{3,2,1,0:T(8,128)S(1)} %fusion.47), kind=kOutput, calls=%fused_computation.337 | convolution fusion | flops 3933568 | bytes 1320960 | tf_op jit(solution)/shard_map/vraj,j->vra/dot_general | solution.py:108
  169.2 9.2 %all-gather.2 = f32[8,5,64,8]{2,3,1,0:T(8,128)S(1)} all-gather(f32[2,5,64,8]{2,3,1,0:T(8,128)S(1)} %pad_maximum_fusion.11), channel_id=4, replica_groups=mesh['axial'=4,'azim'=32] {'axial'}, dimensions={0}, use_global_device_ids=true | all-gather | bytes 102400 | tf_op jit(solution)/shard_map/all_gather | solution.py:110
  179.6 1.7 broadcast_multiply_fusion
  181.5 16.4 %collective-permute-start.6 = (f32[5,64,3,128]{3,1,2,0:T(8,128)S(1)}, f32[5,64,3,128]{3,1,2,0:T(8,128)S(1)}, u32[]{:S(2)}, u32[]{:S(2)}) collective-permute-start(f32[5,64,3,128]{3,1,2,0:T(8,128)S(1)} %copy.26), channel_id=1, source_target_pairs={{1,0},{2,1},{3,2},{4,3},{5,4},{6,5},{7,6},{8,7},{9,8},{10,9},{11,1... | collective-permute-start | bytes 1474568 | tf_op jit(solution)/shard_map/ppermute | solution.py:31
  199.7 4.1 collective-permute-done.7
  204.2 1.7 fusion.36
  209.2 2.3 fusion.8
  211.6 56.8 %all-gather.9.cloned.1.call-done = f32[64,5,64,128]{3,2,1,0:T(8,128)} async-done(((f32[2,5,64,128]{3,2,1,0:T(8,128)}), f32[64,5,64,128]{3,2,1,0:T(8,128)}) %all-gather.9.cloned.1.call-update) | async-done | bytes 10485776 | tf_op jit(solution)/shard_map/all_gather | solution.py:148
  268.4 5.2 %slice_bitcast_fusion.1 = (f32[32,5,64,128]{3,2,1,0:T(8,128)S(1)}, f32[32,5,64,128]{3,2,1,0:T(8,128)S(1)}) fusion(f32[32,2,5,64,128]{4,3,2,1,0:T(8,128)} %bitcast.356), kind=kLoop, calls=%fused_computation.2 | loop fusion | bytes 20971520 | tf_op jit(solution)/shard_map/squeeze | solution.py:157
  273.6 5.4 %fusion.2 = f32[1,5,64,128]{3,0,2,1:T(1,128)S(1)} fusion(f32[32,5,64,128]{3,2,1,0:T(8,128)S(1)} %get-tuple-element.10, s32[]{:T(128)S(6)} %axis_index.33), kind=kOutput, calls=%fused_computation.7 | convolution fusion | flops 15729728 | bytes 5406724 | tf_op jit(solution)/shard_map/k,kvrx->vrx/dot_general | solution.py:157
  279.0 5.7 %fusion = f32[1,5,64,128]{3,0,2,1:T(1,128)S(1)} fusion(f32[32,5,64,128]{3,2,1,0:T(8,128)S(1)} %get-tuple-element.11, s32[]{:T(128)S(6)} %axis_index.33), kind=kOutput, calls=%fused_computation.5 | convolution fusion | flops 15729728 | bytes 5406724 | tf_op jit(solution)/shard_map/k,kvrx->vrx/dot_general | solution.py:158
  286.2 22.6 %scatter_custom_fusion = f32[65536]{0:T(1024)} fusion(s32[4096]{0:T(1024)S(1)} %add_bitcast_fusion, f32[4096]{0:T(1024)S(1)} %bitcast_multiply_fusion.21, f32[]{:T(128)} %constant.254.clone.1), kind=kCustom, calls=%fused_computation.160 | custom fusion | flops 4096 | bytes 262148 | tf_op jit(solution)/shard_map/scatter-add | solution.py:198
  308.8 140.8 %all-reduce.3.cloned.1.call-done = f32[512,128]{1,0:T(8,128)} async-done(((f32[512,128]{1,0:T(8,128)}), f32[512,128]{1,0:T(8,128)}) %all-reduce.3.cloned.1.call-update) | async-done | bytes 262160
  (124 shorter events, 34.4 us)
Async XLA Ops:
  7.2 202.1 %copy-start = (f32[256]{0:T(256)S(1)}, f32[256]{0:T(256)}, u32[]{:S(2)}) copy-start(f32[256]{0:T(256)} %param.23) | copy-start | bytes 3076
  7.2 2.8 copy-start.1
  7.2 2.8 copy-start.8
  7.2 2.8 copy-start.4
  7.2 2.8 copy-start.6
  7.2 90.2 %all-gather.7.cloned.1.call-start = ((), (), s32[]{:S(2)}) async-start(), calls=%async_computation | async-start | bytes 10813440 | tf_op jit(solution)/shard_map/all_gather | solution.py:148
  12.4 14.7 %copy-start.12 = (f32[64,8,128]{2,1,0:T(8,128)}, f32[64,8,128]{2,1,0:T(8,128)S(1)}, u32[]{:S(2)}) copy-start(f32[64,8,128]{2,1,0:T(8,128)S(1)} %get-tuple-element.3) | copy-start | bytes 786436
  12.7 9.3 %collective-permute-start.2 = (f32[5,64,3,128]{3,1,2,0:T(8,128)S(1)}, f32[5,64,3,128]{3,1,2,0:T(8,128)S(1)}, u32[]{:S(2)}, u32[]{:S(2)}) collective-permute-start(f32[5,64,3,128]{3,1,2,0:T(8,128)S(1)} %copy.18), channel_id=1, source_target_pairs={{1,0},{2,1},{3,2},{4,3},{5,4},{6,5},{7,6},{8,7},{9,8},{10,9},{11,1... | collective-permute-start | bytes 1474568 | tf_op jit(solution)/shard_map/ppermute | solution.py:31
  14.2 8.1 %collective-permute-start.3 = (f32[5,64,3,128]{3,1,2,0:T(8,128)S(1)}, f32[5,64,3,128]{3,1,2,0:T(8,128)S(1)}, u32[]{:S(2)}, u32[]{:S(2)}) collective-permute-start(f32[5,64,3,128]{3,1,2,0:T(8,128)S(1)} %copy.20), channel_id=1, source_target_pairs={{0,1},{1,2},{2,3},{3,4},{4,5},{5,6},{6,7},{7,8},{8,9},{9,10},{10,1... | collective-permute-start | bytes 1474568 | tf_op jit(solution)/shard_map/ppermute | solution.py:29
  23.8 2.5 copy-start.2
  25.0 2.1 copy-start.14
  27.1 241.4 %all-gather.9.cloned.1.call-start = ((), (), s32[]{:S(2)}) async-start(), calls=%async_computation.1 | async-start | bytes 10813440 | tf_op jit(solution)/shard_map/all_gather | solution.py:148
  30.4 9.4 %collective-permute-start = (f32[5,64,8,3]{1,2,3,0:T(8,128)S(1)}, f32[5,64,8,3]{1,2,3,0:T(8,128)S(1)}, u32[]{:S(2)}, u32[]{:S(2)}) collective-permute-start(f32[5,64,8,3]{1,2,3,0:T(8,128)S(1)} %copy.14), channel_id=1, source_target_pairs={{32,0},{64,32},{96,64},{33,1},{65,33},{97,65},{34,2},{66,34},{98,6... | collective-permute-start | bytes 92168 | tf_op jit(solution)/shard_map/ppermute | solution.py:31
  32.8 8.6 %collective-permute-start.1 = (f32[5,64,8,3]{1,2,3,0:T(8,128)}, f32[5,64,8,3]{1,2,3,0:T(8,128)S(1)}, u32[]{:S(2)}, u32[]{:S(2)}) collective-permute-start(f32[5,64,8,3]{1,2,3,0:T(8,128)} %copy.16), channel_id=1, source_target_pairs={{0,32},{32,64},{64,96},{1,33},{33,65},{65,97},{2,34},{34,66},{66,9... | collective-permute-start | bytes 92168 | tf_op jit(solution)/shard_map/ppermute | solution.py:29
  102.6 11.3 %copy-start.22 = (f32[5,64,8,128]{3,2,1,0:T(8,128)S(1)}, f32[5,64,8,128]{3,2,1,0:T(8,128)}, u32[]{:S(2)}) copy-start(f32[5,64,8,128]{3,2,1,0:T(8,128)} %fusion.19) | copy-start | bytes 3932164
  108.0 5.9 %copy-start.3 = (f32[5,64,8,128]{3,2,1,0:T(8,128)S(1)}, f32[5,64,8,128]{3,2,1,0:T(8,128)}, u32[]{:S(2)}) copy-start(f32[5,64,8,128]{3,2,1,0:T(8,128)} %copy-done.2) | copy-start | bytes 3932164
  108.0 5.9 %copy-start.5 = (f32[64,8,128]{2,1,0:T(8,128)S(1)}, f32[64,8,128]{2,1,0:T(8,128)}, u32[]{:S(2)}) copy-start(f32[64,8,128]{2,1,0:T(8,128)} %param.17) | copy-start | bytes 786436
  108.0 5.9 %copy-start.10 = (f32[64,8,128]{2,1,0:T(8,128)S(1)}, f32[64,8,128]{2,1,0:T(8,128)}, u32[]{:S(2)}) copy-start(f32[64,8,128]{2,1,0:T(8,128)} %param.12) | copy-start | bytes 786436
  108.0 5.9 %copy-start.13 = (f32[64,8,128]{2,1,0:T(8,128)S(1)}, f32[64,8,128]{2,1,0:T(8,128)}, u32[]{:S(2)}) copy-start(f32[64,8,128]{2,1,0:T(8,128)} %copy-done.12) | copy-start | bytes 786436
  108.1 5.9 %copy-start.15 = (f32[3,64,8,128]{3,2,1,0:T(8,128)S(1)}, f32[3,64,8,128]{3,2,1,0:T(8,128)}, u32[]{:S(2)}) copy-start(f32[3,64,8,128]{3,2,1,0:T(8,128)} %broadcast_multiply_fusion.1) | copy-start | bytes 2359300
  108.1 5.9 %copy-start.19 = (f32[5,64,8,128]{3,2,1,0:T(8,128)S(1)}, f32[5,64,8,128]{3,2,1,0:T(8,128)}, u32[]{:S(2)}) copy-start(f32[5,64,8,128]{3,2,1,0:T(8,128)} %param.18) | copy-start | bytes 3932164
  108.1 5.9 %copy-start.21 = (f32[8]{0:T(128)S(1)}, f32[8]{0:T(128)}, u32[]{:S(2)}) copy-start(f32[8]{0:T(128)} %get-tuple-element.39) | copy-start | bytes 100
  119.1 5.8 %collective-permute-start.4 = (f32[5,64,8,3]{1,2,3,0:T(8,128)S(1)}, f32[5,64,8,3]{1,2,3,0:T(8,128)S(1)}, u32[]{:S(2)}, u32[]{:S(2)}) collective-permute-start(f32[5,64,8,3]{1,2,3,0:T(8,128)S(1)} %copy.22), channel_id=1, source_target_pairs={{32,0},{64,32},{96,64},{33,1},{65,33},{97,65},{34,2},{66,34},{98,6... | collective-permute-start | bytes 92168 | tf_op jit(solution)/shard_map/ppermute | solution.py:31
  120.8 5.6 %collective-permute-start.5 = (f32[5,64,8,3]{1,2,3,0:T(8,128)S(1)}, f32[5,64,8,3]{1,2,3,0:T(8,128)S(1)}, u32[]{:S(2)}, u32[]{:S(2)}) collective-permute-start(f32[5,64,8,3]{1,2,3,0:T(8,128)S(1)} %copy.24), channel_id=1, source_target_pairs={{0,32},{32,64},{64,96},{1,33},{33,65},{65,97},{2,34},{34,66},{66,9... | collective-permute-start | bytes 92168 | tf_op jit(solution)/shard_map/ppermute | solution.py:29
  181.5 17.9 %collective-permute-start.6 = (f32[5,64,3,128]{3,1,2,0:T(8,128)S(1)}, f32[5,64,3,128]{3,1,2,0:T(8,128)S(1)}, u32[]{:S(2)}, u32[]{:S(2)}) collective-permute-start(f32[5,64,3,128]{3,1,2,0:T(8,128)S(1)} %copy.26), channel_id=1, source_target_pairs={{1,0},{2,1},{3,2},{4,3},{5,4},{6,5},{7,6},{8,7},{9,8},{10,9},{11,1... | collective-permute-start | bytes 1474568 | tf_op jit(solution)/shard_map/ppermute | solution.py:31
  198.0 5.8 %collective-permute-start.7 = (f32[5,64,3,128]{3,1,2,0:T(8,128)S(1)}, f32[5,64,3,128]{3,1,2,0:T(8,128)S(1)}, u32[]{:S(2)}, u32[]{:S(2)}) collective-permute-start(f32[5,64,3,128]{3,1,2,0:T(8,128)S(1)} %copy.28), channel_id=1, source_target_pairs={{0,1},{1,2},{2,3},{3,4},{4,5},{5,6},{6,7},{7,8},{8,9},{9,10},{10,1... | collective-permute-start | bytes 1474568 | tf_op jit(solution)/shard_map/ppermute | solution.py:29
  207.1 2.1 copy-start.20
  208.4 3.2 copy-start.16
  208.4 3.2 copy-start.17
  209.2 240.4 %all-reduce.3.cloned.1.call-start = ((), (), s32[]{:S(2)}) async-start(), calls=%async_computation.2 | async-start | bytes 524288
  284.7 1.5 copy-start.18
  286.2 164.7 %copy-start.11 = (f32[5,64,8,128]{3,2,1,0:T(8,128)}, f32[5,64,8,128]{3,2,1,0:T(8,128)S(1)}, u32[]{:S(2)}) copy-start(f32[5,64,8,128]{3,2,1,0:T(8,128)S(1)} %fusion.17) | copy-start | bytes 3932164
  (2 other events, 2.1 us)
Sparse Core Ops, SparseCore 0:
  27.2 63.5 all-gather.6
  209.3 59.0 all-gather.8
  308.9 140.6 all-reduce.2
where the time goes:
time: 464 us; the launch traced here: 458 us
  waiting for transfers between devices  209 us (45%)
  matrix products  108 us (23%)
  other arithmetic  44.7 us (10%)
  local copies, waits for them, and re-layouts  30.9 us (7%)
  starting transfers between devices  30.5 us (7%)
  blocking collectives  19.1 us (4%)
  between operations  14.8 us (3%)
    unnamed x4, waiting for transfers between devices  141 us
    all_gather x2, waiting for transfers between devices, cycle_line(): piece = lax.all_gather(moments, 'azim', axis=0, tiled=True)  56.8 us
    dot_general x2, matrix products, open_line(): jnp.einsum('vraj,j->vra', rhs, signed_power(base, offsets), precision=HIG...  34.9 us
    dot_general x2, matrix products, open_line(): jnp.einsum('vraj,j->vra', rhs, signed_power(base, width_here - 1 - offset...  34.6 us
    scatter-add x1, other arithmetic, per_device(): jax.ops.segment_sum(values, bucket, num_segments=OBSERVERS * TIME_BINS)  22.6 us
    ppermute x4, starting transfers between devices, padded(): lax.ppermute(head, axis, [((i + 1) % count, i) for i in range(ends)])  20.4 us
    all_gather x2, blocking collectives, open_line(): piece = lax.all_gather(moments, 'axial', axis=0, tiled=True)  19.1 us
    dot_general x2, matrix products, cycle_line(): last_sum = jnp.einsum('k,kvrx->vrx', w_last, piece[:, 1], precision=HIGHEST)  11.5 us
  transfers between devices with their start and end apart: 11, of which 5 were waited for; matrix products, arithmetic and copies ran while one was open for 13% of the time, Pallas kernels for 0%

commit v1 on v0

v1 whole, which is shorter than its diff:
```python
import functools
import math

import jax
import jax.numpy as jnp
import ml_dtypes
import numpy as np
from jax import lax
from jax.experimental import pallas as pl
from jax.experimental.pallas import tpu as pltpu
from jax.sharding import PartitionSpec as P

F32 = jnp.float32
BF16 = jnp.bfloat16
MESH = pl.DeviceIdType.MESH

PLANES = 64
FIELDS = 5
ROWS = 8
LANES = 128
AXIAL = 4
AZIM = 32
NA = AXIAL * LANES
NAZ = AZIM * ROWS
SLAB = FIELDS * PLANES
LINES = ROWS * SLAB
BLOCKS = PLANES // 8
SLOTS = 2 * BLOCKS
TILE_ROWS = 8 * FIELDS
HALF = LINES // 2
ENTRY_ROWS = 32
OBSERVERS = 512
TIME_BINS = 128
PEERS = (AZIM - 1) + 2 * (AXIAL - 1)

SECTION = 0.25
DERIV_ALPHA = 1.0 / 3.0
BETA = 0.499


def decay_root(alpha):
    return (-1.0 + math.sqrt(1.0 - 4.0 * alpha * alpha)) / (2.0 * alpha)


DL = decay_root(DERIV_ALPHA)
FL = decay_root(BETA)
C1 = (1.0 / 36.0) / DERIV_ALPHA
DS = 1.0 / math.sqrt(1.0 - 4.0 * DERIV_ALPHA**2)
DK = (7.0 / 9.0 - C1) * DS * (1.0 / DL - DL)
FC = [
    (11.0 + 10.0 * BETA) / 16.0,
    (15.0 + 34.0 * BETA) / 32.0,
    (-3.0 + 6.0 * BETA) / 16.0,
    (1.0 - 2.0 * BETA) / 32.0,
]
FS = 1.0 / math.sqrt(1.0 - 4.0 * BETA**2)
E2 = FC[3] / (2.0 * BETA)
E1 = (FC[2] / 2.0 - E2) / BETA
E0 = (FC[1] / 2.0 - E1 - BETA * E2) / BETA
FK = (FC[0] - E0 - 2.0 * BETA * E1) * FS


def split(values):
    high = values.astype(ml_dtypes.bfloat16)
    low = (values - high.astype(np.float64)).astype(ml_dtypes.bfloat16)
    return high, low


def axial_tables(root, scale, band):
    n, w = NA, LANES
    index = np.arange(n)
    green = scale * (
        np.power(root, np.abs(index[:, None] - index[None, :]))
        - np.power(root, 2 * n - index[:, None] - index[None, :])
    )
    side = np.zeros((n, n))
    for shift, value in band.items():
        side += value * np.eye(n, k=shift)
    whole = green @ side
    left = np.zeros((AXIAL, w))
    right = np.zeros((AXIAL, w))
    for k in range(AXIAL):
        cols = slice(k * w, (k + 1) * w)
        lo, hi = max(0, k * w - 3), min(n, (k + 1) * w + 3)
        m = np.arange(lo, hi)
        left[k] = np.power(root, ((k + 1) * w - m).astype(np.float64)) @ side[lo:hi, cols]
        right[k] = (
            np.power(root, (m - k * w + 1).astype(np.float64))
            - np.power(root, (2 * n - m - k * w + 1).astype(np.float64))
        ) @ side[lo:hi, cols]
    t = np.arange(w)
    own = np.zeros((AXIAL, w, 2 * w), ml_dtypes.bfloat16)
    sent = np.zeros((AXIAL, 2, 32, 2 * w), ml_dtypes.bfloat16)
    taken = np.zeros((AXIAL, 2, 64, 2 * w), ml_dtypes.bfloat16)
    for d in range(AXIAL):
        high, low = split(whole[d * w : (d + 1) * w, d * w : (d + 1) * w].T)
        own[d] = np.concatenate([high, low], axis=1)
        for half in range(2):
            rows = np.zeros((16, w))
            base = half * 4
            rows[base] = left[d]
            rows[base + 1, w - 1] = 1.0
            rows[base + 2, w - 2] = 1.0
            rows[8 + base] = right[d]
            rows[8 + base + 1, 0] = 1.0
            rows[8 + base + 2, 1] = 1.0
            high, low = split(rows)
            sent[d, half] = np.concatenate(
                [np.concatenate([high, high], axis=1), np.concatenate([low, low], axis=1)], axis=0
            )
            rows = np.zeros((32, w))
            for k in range(AXIAL):
                row = k * 8 + half * 4
                i = d * w + t
                if k < d:
                    rows[row] = scale * (
                        np.power(root, (i - (k + 1) * w).astype(np.float64))
                        - np.power(root, (2 * n - i - (k + 1) * w).astype(np.float64))
                    )
                    if k == d - 1:
                        for edge in range(2):
                            col = d * w - 1 - edge
                            for near in range(2 - edge):
                                rows[row + 1 + edge, near] = (
                                    whole[d * w + near, col] - rows[row, near] * left[k, col - k * w]
                                )
                if k > d:
                    rows[row] = scale * np.power(root, (k * w - 1 - i).astype(np.float64))
                    if k == d + 1:
                        for edge in range(2):
                            col = k * w + edge
                            for near in range(2 - edge):
                                rows[row + 1 + edge, w - 1 - near] = (
                                    whole[k * w - 1 - near, col] - rows[row, w - 1 - near] * right[k, edge]
                                )
            high, low = split(rows)
            pair = np.concatenate([high, low], axis=1)
            taken[d, half] = np.concatenate([pair, pair], axis=0)
    return own, sent, taken


def both_tables():
    deriv = axial_tables(DL, DS, {1: 7.0 / 9.0, -1: -7.0 / 9.0, 2: 1.0 / 36.0, -2: -1.0 / 36.0})
    band = {0: FC[0]}
    for shift in range(1, 4):
        band[shift] = band[-shift] = FC[shift] / 2.0
    smooth = axial_tables(FL, FS, band)
    return [np.stack(pair, axis=1) for pair in zip(deriv, smooth)]


def two_terms(value):
    high = value.astype(BF16)
    low = (value - high.astype(F32)).astype(BF16)
    return high, low


def dot_last(left, right):
    return lax.dot_general(left, right, (((1,), (1,)), ((), ())), preferred_element_type=F32)


def dot_first(left, right):
    return lax.dot_general(left, right, (((0,), (0,)), ((), ())), preferred_element_type=F32)


def kernel(
    own_hbm,
    sent_hbm,
    taken_hbm,
    density_hbm,
    velocity_hbm,
    pressure_hbm,
    axial_hbm,
    azim_hbm,
    volume_hbm,
    radial_hbm,
    area_ref,
    observer_ref,
    bin_ref,
    weight_ref,
    table_ref,
    state_hbm,
    signal_ref,
    own,
    sent,
    taken,
    density,
    velocity,
    pressure,
    axial_metric,
    azim_metric,
    volume,
    radial,
    azim_flux,
    base,
    ratio,
    cells,
    lined,
    final,
    edge_send,
    edge_recv,
    moment_send,
    moment_recv,
    start_send,
    start_recv,
    deriv_halo,
    filter_halo,
    observer_hot,
    bin_hot,
    partial,
    part_recv,
    owner_send,
    owner_recv,
    load_sem,
    store_sem,
    edge_send_sem,
    edge_recv_sem,
    moment_send_sem,
    moment_recv_sem,
    start_send_sem,
    start_recv_sem,
    halo_send_sem,
    halo_recv_sem,
    part_send_sem,
    part_recv_sem,
    owner_send_sem,
    owner_recv_sem,
):
    me_a = lax.axis_index("axial")
    me_z = lax.axis_index("azim")
    core = lax.rem(me_z, 2)
    chip = me_z // 2
    twin = me_z + 1 - 2 * core
    reducer = core == 0
    after = lax.rem(me_z + 1, AZIM)
    before = lax.rem(me_z + AZIM - 1, AZIM)

    loads = [
        pltpu.make_async_copy(density_hbm, density, load_sem.at[0]),
        pltpu.make_async_copy(velocity_hbm, velocity, load_sem.at[1]),
        pltpu.make_async_copy(pressure_hbm, pressure, load_sem.at[2]),
        pltpu.make_async_copy(axial_hbm, axial_metric, load_sem.at[3]),
        pltpu.make_async_copy(azim_hbm, azim_metric, load_sem.at[4]),
        pltpu.make_async_copy(volume_hbm, volume, load_sem.at[5]),
        pltpu.make_async_copy(radial_hbm, radial, load_sem.at[6]),
    ]
    for which in range(2):
        loads.append(
            pltpu.make_async_copy(
                own_hbm.at[me_a, which], own.at[which, pl.ds(0, LANES)], load_sem.at[7 + 4 * which]
            )
        )
        loads.append(
            pltpu.make_async_copy(
                own_hbm.at[me_a, which], own.at[which, pl.ds(LANES, LANES)], load_sem.at[8 + 4 * which]
            )
        )
        loads.append(pltpu.make_async_copy(sent_hbm.at[me_a, which], sent.at[which], load_sem.at[9 + 4 * which]))
        loads.append(pltpu.make_async_copy(taken_hbm.at[me_a, which], taken.at[which], load_sem.at[10 + 4 * which]))
    for load in loads:
        load.start()

    barrier = pltpu.get_barrier_semaphore()

    def greet_azim(step, carry):
        other = lax.rem(me_z + step, AZIM)
        pl.semaphore_signal(barrier, inc=1, device_id=(me_a, other), device_id_type=MESH)
        return carry

    lax.fori_loop(1, AZIM, greet_azim, 0)

    def greet_axial(step, carry):
        other = lax.rem(me_a + step, AXIAL)
        pl.semaphore_signal(barrier, inc=1, device_id=(other, me_z), device_id_type=MESH)
        pl.semaphore_signal(barrier, inc=1, device_id=(other, twin), device_id_type=MESH)
        return carry

    lax.fori_loop(1, AXIAL, greet_axial, 0)

    edge_recv[0, pl.ds(me_a, 1)] = jnp.zeros((1, 8, HALF), F32)
    edge_recv[1, pl.ds(me_a, 1)] = jnp.zeros((1, 8, HALF), F32)

    for load in loads:
        load.wait()
    pl.semaphore_wait(barrier, PEERS)

    def send_moments(which, slot):
        target = 2 * slot

        @pl.when(target != me_z)
        def _():
            pltpu.make_async_remote_copy(
                src_ref=moment_send.at[which, slot],
                dst_ref=moment_recv.at[which, me_z],
                send_sem=moment_send_sem.at[which],
                recv_sem=moment_recv_sem.at[which],
                device_id=(me_a, target),
                device_id_type=MESH,
            ).start()

        @pl.when(target == me_z)
        def _():
            pltpu.make_async_copy(
                moment_send.at[which, slot], moment_recv.at[which, me_z], moment_recv_sem.at[which]
            ).start()

    def wait_moment_sends(which):
        @pl.when(reducer)
        def _():
            part = moment_send.at[which, pl.ds(0, SLOTS - 1)]
            pltpu.make_async_copy(part, part, moment_send_sem.at[which]).wait()

        @pl.when(jnp.logical_not(reducer))
        def _():
            part = moment_send.at[which]
            pltpu.make_async_copy(part, part, moment_send_sem.at[which]).wait()

    def reduce_moments(which, root):
        factor = root**ROWS
        wrap = 1.0 / (1.0 - root**NAZ)

        @pl.when(reducer)
        def _():
            part = moment_recv.at[which]
            pltpu.make_async_copy(part, part, moment_recv_sem.at[which]).wait()
            side = lax.rem(chip, 2)

            def place(step):
                return step + side * (AZIM - 1 - 2 * step)

            def gather(step, total):
                return factor * total + moment_recv[which, place(step)]

            first = lax.fori_loop(0, AZIM, gather, jnp.zeros((TILE_ROWS, LANES), F32)) * wrap

            def hand_out(step, now):
                other = place(step)
                start_send[which, other] = now

                @pl.when(other != me_z)
                def _():
                    pltpu.make_async_remote_copy(
                        src_ref=start_send.at[which, other],
                        dst_ref=start_recv.at[which, chip],
                        send_sem=start_send_sem.at[which],
                        recv_sem=start_recv_sem.at[which],
                        device_id=(me_a, other),
                        device_id_type=MESH,
                    ).start()

                @pl.when(other == me_z)
                def _():
                    pltpu.make_async_copy(
                        start_send.at[which, other], start_recv.at[which, chip], start_recv_sem.at[which]
                    ).start()

                return factor * now + moment_recv[which, other]

            lax.fori_loop(0, AZIM, hand_out, first)

    def wait_starts(which):
        part = start_recv.at[which]
        pltpu.make_async_copy(part, part, start_recv_sem.at[which]).wait()

    def wait_start_sends(which):
        @pl.when(reducer)
        def _():
            part = start_send.at[which, pl.ds(0, AZIM - 1)]
            pltpu.make_async_copy(part, part, start_send_sem.at[which]).wait()

    def moments_of(values, root):
        up = root * values[0]
        for row in range(1, ROWS):
            up = root * (up + values[row])
        down = root * values[ROWS - 1]
        for row in range(ROWS - 2, -1, -1):
            down = root * (down + values[row])
        return up, down

    def keep_moments(which, group, field, values, root):
        up, down = moments_of(values, root)
        for half in range(2):
            for side, value in ((0, up), (1, down)):
                moment_send[which, 4 * group + 2 * half + side, pl.ds(8 * field, 8)] = value[8 * half : 8 * half + 8]

    def start_of(which, group, field, side):
        return jnp.concatenate(
            [start_recv[which, 4 * group + 2 * half + side, pl.ds(8 * field, 8)] for half in range(2)], axis=0
        )

    def halo_copies(which, halo, source, depth):
        return (
            pltpu.make_async_remote_copy(
                src_ref=source.at[pl.ds(ROWS - depth, depth)],
                dst_ref=halo.at[0],
                send_sem=halo_send_sem.at[which, 0],
                recv_sem=halo_recv_sem.at[which, 0],
                device_id=(me_a, after),
                device_id_type=MESH,
            ),
            pltpu.make_async_remote_copy(
                src_ref=source.at[pl.ds(0, depth)],
                dst_ref=halo.at[1],
                send_sem=halo_send_sem.at[which, 1],
                recv_sem=halo_recv_sem.at[which, 1],
                device_id=(me_a, before),
                device_id_type=MESH,
            ),
        )

    def edge_copy(which, step):
        other = lax.rem(me_a + step, AXIAL)
        down = jnp.where(other < me_a, 1, 0)
        return pltpu.make_async_remote_copy(
            src_ref=edge_send.at[which, down],
            dst_ref=edge_recv.at[which, me_a],
            send_sem=edge_send_sem.at[which, step - 1],
            recv_sem=edge_recv_sem.at[which, step - 1],
            device_id=(other, me_z),
            device_id_type=MESH,
        )

    def send_edges(which):
        def piece(step, carry):
            at = pl.multiple_of(step * 640, 640)
            total = dot_last(sent[which, 0], cells[which, pl.ds(at, 640)]) + dot_last(
                sent[which, 1], cells[which, pl.ds(HALF + at, 640)]
            )
            total = total[:16] + total[16:]
            edge_send[which, 0, :, pl.ds(at, 640)] = total[:8]
            edge_send[which, 1, :, pl.ds(at, 640)] = total[8:]
            return carry

        lax.fori_loop(0, 2, piece, 0)
        for step in range(1, AXIAL):
            edge_copy(which, step).start()

    def own_part(which):
        def piece(row, carry):
            at = pl.multiple_of(row * SLAB, SLAB)
            total = jnp.dot(cells[which, pl.ds(at, SLAB)], own[which], preferred_element_type=F32)
            lined[row] = total[:, :LANES] + total[:, LANES:]
            return carry

        lax.fori_loop(0, ROWS, piece, 0)

    def add_edges(which):
        for step in range(1, AXIAL):
            edge_copy(which, step).wait_recv()

        def piece(step, carry):
            at = pl.multiple_of(lax.rem(step, 2) * 640, 640)
            received = edge_recv[which, :, :, pl.ds(at, 640)].reshape(32, 640)
            high, low = two_terms(received)
            total = dot_first(jnp.concatenate([high, low], axis=0), taken[which, step // 2])
            total = (total[:, :LANES] + total[:, LANES:]).reshape(2, SLAB, LANES)
            lined[pl.ds(2 * step, 2)] = lined[pl.ds(2 * step, 2)] + total
            return carry

        lax.fori_loop(0, 4, piece, 0)

    def wait_edge_sends(which):
        for step in range(1, AXIAL):
            edge_copy(which, step).wait_send()

    def keep_cells(which, row, field, group, value):
        high, low = two_terms(value)
        at = pl.multiple_of(row * SLAB + field * PLANES + group * 16, 16)
        cells[which, pl.ds(at, 16), pl.ds(0, LANES)] = high
        cells[which, pl.ds(at, 16), pl.ds(LANES, LANES)] = low

    def flux_group(group, carry):
        flux = [[None] * ROWS for _ in range(FIELDS)]
        for row in range(ROWS):
            at = pl.ds(group * 128 + row, 16, stride=ROWS)
            rho, prs, vol = density[at], pressure[at], volume[at]
            vel = [velocity[comp, at] for comp in range(3)]
            energy = 2.5 * prs + 0.5 * rho * (vel[0] * vel[0] + vel[1] * vel[1] + vel[2] * vel[2])
            state = [rho, rho * vel[0], rho * vel[1], rho * vel[2], energy]
            here = pl.ds(pl.multiple_of(group * 16, 16), 16)
            ratio[row, here] = SECTION / vol
            for field in range(FIELDS):
                base[row, pl.ds(pl.multiple_of(field * PLANES + group * 16, 16), 16)] = (
                    state[field] + SECTION * radial[field, at]
                )
            heat = energy + prs
            for metric, azimuthal in ((axial_metric, False), (azim_metric, True)):
                grad = [metric[comp, at] for comp in range(3)]
                contra = vol * (grad[0] * vel[0] + grad[1] * vel[1] + grad[2] * vel[2])
                flow = rho * contra
                push = vol * prs
                parts = [flow] + [flow * vel[comp] + grad[comp] * push for comp in range(3)] + [heat * contra]
                for field in range(FIELDS):
                    if azimuthal:
                        flux[field][row] = parts[field]
                        azim_flux[row, pl.ds(pl.multiple_of(field * PLANES + group * 16, 16), 16)] = parts[field]
                    else:
                        keep_cells(0, row, field, group, parts[field])
        for field in range(FIELDS):
            keep_moments(0, group, field, flux[field], DL)
        for quarter in range(4):
            send_moments(0, 4 * group + quarter)
        return carry

    lax.fori_loop(0, BLOCKS // 2, flux_group, 0)
    for copy in halo_copies(0, deriv_halo, azim_flux, 1):
        copy.start()
    send_edges(0)

    ids = observer_ref[...]
    order = (
        lax.shift_right_logical(ids, 7) * 128
        + (lax.shift_right_logical(ids, 2) & 1) * 64
        + (lax.shift_right_logical(ids, 3) & 15) * 4
        + (ids & 3)
    )
    partial[pl.ds(0, ENTRY_ROWS)] = order.astype(F32)

    def hot_row(row, carry):
        wanted = partial[pl.ds(row, 1)].astype(jnp.int32)
        rows = lax.broadcasted_iota(jnp.int32, (OBSERVERS, LANES), 0)
        at = pl.multiple_of(row * LANES, LANES)
        observer_hot[:, pl.ds(at, LANES)] = jnp.where(rows == wanted, 1.0, 0.0).astype(BF16)
        return carry

    lax.fori_loop(0, ENTRY_ROWS, hot_row, 0)

    own_part(0)
    reduce_moments(0, DL)
    add_edges(0)
    wait_starts(0)
    for copy in halo_copies(0, deriv_halo, azim_flux, 1):
        copy.wait_recv()

    def section_group(group, carry):
        for field in range(FIELDS):
            at = pl.ds(pl.multiple_of(field * PLANES + group * 16, 16), 16)
            here = pl.ds(pl.multiple_of(group * 16, 16), 16)
            flux = [deriv_halo[0, 0, at]] + [azim_flux[row, at] for row in range(ROWS)] + [deriv_halo[1, 0, at]]
            up = [start_of(0, group, field, 0)]
            for row in range(ROWS - 1):
                up.append(DL * (flux[row + 1] + up[-1]))
            down = [start_of(0, group, field, 1)]
            for row in range(ROWS - 1, 0, -1):
                down.append(DL * (flux[row + 1] + down[-1]))
            down = down[::-1]
            for row in range(ROWS):
                deriv = DK * (down[row] - up[row]) + C1 * (flux[row + 2] - flux[row])
                value = base[row, at] - ratio[row, here] * (lined[row, at] + deriv)
                keep_cells(1, row, field, group, value)
        return carry

    lax.fori_loop(0, BLOCKS // 2, section_group, 0)
    send_edges(1)
    own_part(1)
    add_edges(1)
    for copy in halo_copies(1, filter_halo, lined, 2):
        copy.start()

    def moment_group(group, carry):
        for field in range(FIELDS):
            at = pl.ds(pl.multiple_of(field * PLANES + group * 16, 16), 16)
            keep_moments(1, group, field, [lined[row, at] for row in range(ROWS)], FL)
        for quarter in range(4):
            send_moments(1, 4 * group + quarter)
        return carry

    lax.fori_loop(0, BLOCKS // 2, moment_group, 0)
    reduce_moments(1, FL)
    wait_starts(1)
    for copy in halo_copies(1, filter_halo, lined, 2):
        copy.wait_recv()

    def store_copy(group):
        planes = pl.ds(pl.multiple_of(group * 128, 128), 128)
        return pltpu.make_async_copy(final.at[:, planes], state_hbm.at[:, planes], store_sem.at[group])

    def final_group(group, carry):
        for field in range(FIELDS):
            at = pl.ds(pl.multiple_of(field * PLANES + group * 16, 16), 16)
            value = [filter_halo[0, 0, at], filter_halo[0, 1, at]]
            value += [lined[row, at] for row in range(ROWS)]
            value += [filter_halo[1, 0, at], filter_halo[1, 1, at]]
            up = [start_of(1, group, field, 0)]
            for row in range(ROWS - 1):
                up.append(FL * (value[row + 2] + up[-1]))
            down = [start_of(1, group, field, 1)]
            for row in range(ROWS - 1, 0, -1):
                down.append(FL * (value[row + 2] + down[-1]))
            down = down[::-1]
            for row in range(ROWS):
                near = E1 * (value[row + 1] + value[row + 3]) + E2 * (value[row] + value[row + 4])
                result = FK * (up[row] + down[row]) + (FK + E0) * value[row + 2] + near
                final[field, pl.ds(group * 128 + row, 16, stride=ROWS)] = result
        return carry

    def final_step(group, carry):
        final_group(group, carry)
        store_copy(group).start()
        return carry

    lax.fori_loop(0, BLOCKS // 2, final_step, 0)

    source = area_ref[...] * (final[2, pl.ds(0, ROWS)] + final[0, pl.ds(0, ROWS)] - 1.0)
    picks = weight_ref[...]
    low_half = jnp.take_along_axis(
        jnp.broadcast_to(table_ref[pl.ds(0, 1)], (ENTRY_ROWS, LANES)), picks & 127, axis=1
    )
    high_half = jnp.take_along_axis(
        jnp.broadcast_to(table_ref[pl.ds(1, 1)], (ENTRY_ROWS, LANES)), picks & 127, axis=1
    )
    weights = jnp.where(picks < LANES, low_half, high_half)
    values = weights * jnp.concatenate([source] * 4, axis=0)
    high, low = two_terms(values)
    partial[pl.ds(0, ENTRY_ROWS)] = high.astype(F32)
    partial[pl.ds(ENTRY_ROWS, ENTRY_ROWS)] = low.astype(F32)

    def bin_row(row, carry):
        same = lax.broadcasted_iota(jnp.int32, (TIME_BINS, LANES), 0) == bin_ref[pl.ds(row, 1)]
        at = pl.multiple_of(row * LANES, LANES)
        bin_hot[pl.ds(0, TIME_BINS), pl.ds(at, LANES)] = jnp.where(same, partial[pl.ds(row, 1)], 0.0).astype(BF16)
        bin_hot[pl.ds(TIME_BINS, TIME_BINS), pl.ds(at, LANES)] = jnp.where(
            same, partial[pl.ds(ENTRY_ROWS + row, 1)], 0.0
        ).astype(BF16)
        return carry

    lax.fori_loop(0, ENTRY_ROWS, bin_row, 0)

    def sum_rows(step, carry):
        at = pl.ds(pl.multiple_of(step * 128, 128), 128)
        total = dot_last(observer_hot[at], bin_hot[...])
        partial[at] = total[:, :TIME_BINS] + total[:, TIME_BINS:]
        return carry

    lax.fori_loop(0, OBSERVERS // 128, sum_rows, 0)

    mine = me_a * 2 + core

    def part_copy(step):
        other = lax.rem(mine + step, 8)
        other_z = me_z - core + lax.rem(other, 2)
        return pltpu.make_async_remote_copy(
            src_ref=partial.at[pl.ds(pl.multiple_of(other * 64, 64), 64)],
            dst_ref=part_recv.at[step - 1],
            send_sem=part_send_sem.at[step - 1],
            recv_sem=part_recv_sem.at[step - 1],
            device_id=(other // 2, other_z),
            device_id_type=MESH,
        )

    for step in range(1, 8):
        part_copy(step).start()
    total = partial[pl.ds(pl.multiple_of(mine * 64, 64), 64)]
    for step in range(1, 8):
        part_copy(step).wait_recv()
        total = total + part_recv[step - 1]
    for owner in range(16):
        owner_send[owner, pl.ds(0, 4)] = total[4 * owner : 4 * owner + 4]
        owner_send[owner, pl.ds(4, 4)] = jnp.zeros((4, LANES), F32)

    def owner_copy(step):
        other = lax.rem(chip + step, 16)
        return pltpu.make_async_remote_copy(
            src_ref=owner_send.at[other],
            dst_ref=owner_recv.at[step - 1],
            send_sem=owner_send_sem.at[step - 1],
            recv_sem=owner_recv_sem.at[step - 1],
            device_id=(me_a, 2 * other + core),
            device_id_type=MESH,
        )

    for step in range(1, 16):
        owner_copy(step).start()
    result = owner_send[chip]
    for step in range(1, 16):
        owner_copy(step).wait_recv()
        result = result + owner_recv[step - 1]
    signal_ref[...] = result[:4]

    for group in range(BLOCKS // 2):
        store_copy(group).wait()
    for which, halo, source_ref, depth in ((0, deriv_halo, azim_flux, 1), (1, filter_halo, lined, 2)):
        wait_moment_sends(which)
        wait_start_sends(which)
        wait_edge_sends(which)
        for copy in halo_copies(which, halo, source_ref, depth):
            copy.wait_send()
    for step in range(1, 8):
        part_copy(step).wait_send()
    for step in range(1, 16):
        owner_copy(step).wait_send()


def per_device(
    density,
    velocity,
    pressure,
    axial_metric,
    azim_metric,
    volume,
    radial_term,
    panel_area,
    observer_ids,
    bin_ids,
    weight_ids,
    bin_weights,
):
    own, sent, taken = both_tables()
    rows = PLANES * ROWS
    hbm = pl.BlockSpec(memory_space=pl.ANY)
    vmem = pl.BlockSpec(memory_space=pltpu.VMEM)
    dma = pltpu.SemaphoreType.DMA
    state, signals = pl.pallas_call(
        kernel,
        out_shape=(
            jax.ShapeDtypeStruct((FIELDS, rows, LANES), F32),
            jax.ShapeDtypeStruct((4, TIME_BINS), F32),
        ),
        in_specs=[hbm] * 10 + [vmem] * 5,
        out_specs=(hbm, vmem),
        scratch_shapes=[
            pltpu.VMEM((2, 2 * LANES, 2 * LANES), BF16),
            pltpu.VMEM((2, 2, 32, 2 * LANES), BF16),
            pltpu.VMEM((2, 2, 64, 2 * LANES), BF16),
            pltpu.VMEM((rows, LANES), F32),
            pltpu.VMEM((3, rows, LANES), F32),
            pltpu.VMEM((rows, LANES), F32),
            pltpu.VMEM((3, rows, LANES), F32),
            pltpu.VMEM((3, rows, LANES), F32),
            pltpu.VMEM((rows, LANES), F32),
            pltpu.VMEM((FIELDS, rows, LANES), F32),
            pltpu.VMEM((ROWS, SLAB, LANES), F32),
            pltpu.VMEM((ROWS, SLAB, LANES), F32),
            pltpu.VMEM((ROWS, PLANES, LANES), F32),
            pltpu.VMEM((2, LINES, 2 * LANES), BF16),
            pltpu.VMEM((ROWS, SLAB, LANES), F32),
            pltpu.VMEM((FIELDS, rows, LANES), F32),
            pltpu.VMEM((2, 2, 8, HALF), F32),
            pltpu.VMEM((2, AXIAL, 8, HALF), F32),
            pltpu.VMEM((2, SLOTS, TILE_ROWS, LANES), F32),
            pltpu.VMEM((2, AZIM, TILE_ROWS, LANES), F32),
            pltpu.VMEM((2, AZIM, TILE_ROWS, LANES), F32),
            pltpu.VMEM((2, SLOTS, TILE_ROWS, LANES), F32),
            pltpu.VMEM((2, 1, SLAB, LANES), F32),
            pltpu.VMEM((2, 2, SLAB, LANES), F32),
            pltpu.VMEM((OBSERVERS, ENTRY_ROWS * LANES), BF16),
            pltpu.VMEM((2 * TIME_BINS, ENTRY_ROWS * LANES), BF16),
            pltpu.VMEM((OBSERVERS, TIME_BINS), F32),
            pltpu.VMEM((7, 64, TIME_BINS), F32),
            pltpu.VMEM((16, 8, TIME_BINS), F32),
            pltpu.VMEM((15, 8, TIME_BINS), F32),
            dma((15,)),
            dma((BLOCKS // 2,)),
            dma((2, 3)),
            dma((2, 3)),
            dma((2,)),
            dma((2,)),
            dma((2,)),
            dma((2,)),
            dma((2, 2)),
            dma((2, 2)),
            dma((7,)),
            dma((7,)),
            dma((15,)),
            dma((15,)),
        ],
        compiler_params=pltpu.CompilerParams(
            collective_id=0, has_side_effects=True, vmem_limit_bytes=48 * 1024 * 1024
        ),
    )(
        jnp.asarray(own),
        jnp.asarray(sent),
        jnp.asarray(taken),
        density.reshape(rows, LANES),
        velocity.reshape(3, rows, LANES),
        pressure.reshape(rows, LANES),
        axial_metric.reshape(3, rows, LANES),
        azim_metric.reshape(3, rows, LANES),
        volume.reshape(rows, LANES),
        radial_term.reshape(FIELDS, rows, LANES),
        panel_area,
        observer_ids.reshape(ENTRY_ROWS, LANES),
        bin_ids.reshape(ENTRY_ROWS, LANES),
        weight_ids.reshape(ENTRY_ROWS, LANES),
        bin_weights.reshape(2, LANES),
    )
    return state.reshape(FIELDS, PLANES, ROWS, LANES), signals


def solution(mesh):
    placed = (
        P(None, "azim", "axial"),
        P(None, None, "azim", "axial"),
        P(None, "azim", "axial"),
        P(None, None, "azim", "axial"),
        P(None, None, "azim", "axial"),
        P(None, "azim", "axial"),
        P(None, None, "azim", "axial"),
        P("azim", "axial"),
        P(None, "azim", "axial"),
        P(None, "azim", "axial"),
        P(None, "azim", "axial"),
        P(),
    )
    return jax.shard_map(
        per_device,
        mesh=mesh,
        in_specs=placed,
        out_specs=(P(None, None, "azim", "axial"), P(("axial", "azim"), None)),
        check_vma=False,
    )
```

time: 464 us -> 79.8 us (0.17); the launches traced: 458 us -> 79.1 us
  waiting for transfers between devices: 209 us -> 0 us
  matrix products: 108 us -> 0 us
  Pallas kernels: 0 us -> 64 us
  other arithmetic: 44.7 us -> 0 us
  starting transfers between devices: 30.5 us -> 0 us
  blocking collectives: 19.1 us -> 0 us
  local copies, waits for them, and re-layouts: 30.9 us -> 14.4 us
  between operations: 14.8 us -> 0.67 us
    unnamed x4 -> x0, waiting for transfers between devices: 141 us -> none
    dot_general x23 -> x0, matrix products: 108 us -> none  [the longest x2 34.9 us: open_line(): jnp.einsum('vraj,j->vra', rhs, signed_power(base, offsets), precision=HIG...]
    pallas_call x0 -> x1, Pallas kernels: none -> 64 us  [per_device(): pl.pallas_call(kernel, out_shape=(jax.ShapeDtypeStruct((FIELDS, rows, LAN...]
    all_gather x2 -> x0, waiting for transfers between devices: 56.8 us -> none  [cycle_line(): piece = lax.all_gather(moments, 'azim', axis=0, tiled=True)]
    ppermute x8 -> x0, starting transfers between devices: 30.4 us -> none  [the longest x4 20.4 us: padded(): lax.ppermute(head, axis, [((i + 1) % count, i) for i in range(ends)])]
    scatter-add x1 -> x0, other arithmetic: 22.6 us -> none  [per_device(): jax.ops.segment_sum(values, bucket, num_segments=OBSERVERS * TIME_BINS)]
    all_gather x2 -> x0, blocking collectives: 19.1 us -> none  [open_line(): piece = lax.all_gather(moments, 'axial', axis=0, tiled=True)]
    add x4 -> x0, other arithmetic: 14.7 us -> none  [the longest x2 7.91 us: filter_side(): total = total + 0.5 * coeffs[shift] * (cells(shift) + cells(-shift))]
  transfers between devices with their start and end apart: 11 -> 0, of which waited for: 5 -> 0; matrix products, arithmetic and copies ran while one was open for 13% -> 0% of each run, Pallas kernels for 0% -> 0%
where the time goes in v1:
time: 79.8 us; the launch traced here: 79.1 us
  Pallas kernels  64 us (80%)
  local copies, waits for them, and re-layouts  14.4 us (18%)
    pallas_call x1, Pallas kernels, per_device(): pl.pallas_call(kernel, out_shape=(jax.ShapeDtypeStruct((FIELDS, rows, LAN...  64 us
    unnamed x30, local copies, waits for them, and re-layouts  14.4 us

profile of v1, /device:TPU:1, one launch (start us, length us, event | category | flops | bytes accessed | tf_op | source)
XLA Modules:
  0.0 79.1 jit_solution(15219374000186739893)
XLA Ops:
  0.6 0.0 copy-start
  0.6 1.1 %copy-done = f32[3,64,8,128]{3,2,1,0:T(8,128)S(1)} copy-done((f32[3,64,8,128]{3,2,1,0:T(8,128)S(1)}, f32[3,64,8,128]{3,2,1,0:T(8,128)}, u32[]{:S(2)}) %copy-start) | copy-done | bytes 786456
  1.8 0.0 copy-start.1
  1.8 1.1 %copy-done.1 = f32[3,64,8,128]{3,2,1,0:T(8,128)S(1)} copy-done((f32[3,64,8,128]{3,2,1,0:T(8,128)S(1)}, f32[3,64,8,128]{3,2,1,0:T(8,128)}, u32[]{:S(2)}) %copy-start.1) | copy-done | bytes 786456
  2.9 0.0 copy-start.2
  2.9 1.1 %copy-done.2 = f32[3,64,8,128]{3,2,1,0:T(8,128)S(1)} copy-done((f32[3,64,8,128]{3,2,1,0:T(8,128)S(1)}, f32[3,64,8,128]{3,2,1,0:T(8,128)}, u32[]{:S(2)}) %copy-start.2) | copy-done | bytes 786456
  4.0 0.0 copy-start.3
  4.0 1.0 %copy-done.3 = bf16[4,2,2,64,256]{4,3,2,1,0:T(8,128)(2,1)S(1)} copy-done((bf16[4,2,2,64,256]{4,3,2,1,0:T(8,128)(2,1)S(1)}, bf16[4,2,2,64,256]{4,3,2,1,0:T(8,128)(2,1)}, u32[]{:S(2)}) %copy-start.3) | copy-done | bytes 524312
  5.1 0.0 copy-start.4
  5.1 1.0 %copy-done.4 = bf16[4,2,128,256]{3,2,1,0:T(8,128)(2,1)S(1)} copy-done((bf16[4,2,128,256]{3,2,1,0:T(8,128)(2,1)S(1)}, bf16[4,2,128,256]{3,2,1,0:T(8,128)(2,1)}, u32[]{:S(2)}) %copy-start.4) | copy-done | bytes 524312
  6.1 0.0 copy-start.5
  6.1 0.9 %copy-done.5 = f32[64,8,128]{2,1,0:T(8,128)S(1)} copy-done((f32[64,8,128]{2,1,0:T(8,128)S(1)}, f32[64,8,128]{2,1,0:T(8,128)}, u32[]{:S(2)}) %copy-start.5) | copy-done | bytes 262168
  7.1 0.0 copy-start.6
  7.1 0.9 %copy-done.6 = f32[64,8,128]{2,1,0:T(8,128)S(1)} copy-done((f32[64,8,128]{2,1,0:T(8,128)S(1)}, f32[64,8,128]{2,1,0:T(8,128)}, u32[]{:S(2)}) %copy-start.6) | copy-done | bytes 262168
  8.0 0.0 copy-start.7
  8.0 0.9 %copy-done.7 = f32[64,8,128]{2,1,0:T(8,128)S(1)} copy-done((f32[64,8,128]{2,1,0:T(8,128)S(1)}, f32[64,8,128]{2,1,0:T(8,128)}, u32[]{:S(2)}) %copy-start.7) | copy-done | bytes 262168
  9.0 0.0 copy-start.8
  9.0 0.9 %copy-done.8 = bf16[4,2,2,32,256]{4,3,2,1,0:T(8,128)(2,1)S(1)} copy-done((bf16[4,2,2,32,256]{4,3,2,1,0:T(8,128)(2,1)S(1)}, bf16[4,2,2,32,256]{4,3,2,1,0:T(8,128)(2,1)}, u32[]{:S(2)}) %copy-start.8) | copy-done | bytes 262168
  9.9 0.0 copy-start.9
  9.9 0.7 copy-done.9
  10.6 0.0 copy-start.10
  10.6 0.7 copy-done.10
  11.4 0.0 copy-start.11
  11.4 0.7 copy-done.11
  12.1 0.0 copy-start.12
  12.1 0.7 copy-done.12
  12.8 0.0 copy-start.13
  12.8 0.7 copy-done.13
  13.4 64.0 %shard_map.158 = (f32[5,512,128]{2,1,0:T(8,128)S(1)}, f32[4,128]{1,0:T(4,128)S(1)}) custom-call(bf16[4,2,128,256]{3,2,1,0:T(8,128)(2,1)S(1)} %copy-done.4, bf16[4,2,2,32,256]{4,3,2,1,0:T(8,128)(2,1)S(1)} %copy-done.8, bf16[4,2,2,64,256]{4,3,2,1,0:T(8,128)(2,1)S(1)} %copy-done.3, f32[512,128]{1,0:T(8,128)S(1)} %bitcast.16, f32[3,512,128]{2,1,0:T(8,128)S(1)} %bitcast.13, ...), custom_call_target="tpu_custom_call" | custom-call | tf_op jit(solution)/shard_map/pallas_call | solution.py:712
  77.5 1.1 %copy.19 = f32[5,64,8,128]{3,2,1,0:T(8,128)} copy(f32[5,64,8,128]{3,2,1,0:T(8,128)S(1)} %bitcast.12) | data formatting | bytes 2621440
  78.5 0.6 copy.20
Async XLA Ops:
  0.6 1.1 %copy-start = (f32[3,64,8,128]{3,2,1,0:T(8,128)S(1)}, f32[3,64,8,128]{3,2,1,0:T(8,128)}, u32[]{:S(2)}) copy-start(f32[3,64,8,128]{3,2,1,0:T(8,128)} %param.16) | copy-start | bytes 2359300
  1.8 1.1 %copy-start.1 = (f32[3,64,8,128]{3,2,1,0:T(8,128)S(1)}, f32[3,64,8,128]{3,2,1,0:T(8,128)}, u32[]{:S(2)}) copy-start(f32[3,64,8,128]{3,2,1,0:T(8,128)} %param.18) | copy-start | bytes 2359300
  2.9 1.1 %copy-start.2 = (f32[3,64,8,128]{3,2,1,0:T(8,128)S(1)}, f32[3,64,8,128]{3,2,1,0:T(8,128)}, u32[]{:S(2)}) copy-start(f32[3,64,8,128]{3,2,1,0:T(8,128)} %param.19) | copy-start | bytes 2359300
  4.0 1.0 %copy-start.3 = (bf16[4,2,2,64,256]{4,3,2,1,0:T(8,128)(2,1)S(1)}, bf16[4,2,2,64,256]{4,3,2,1,0:T(8,128)(2,1)}, u32[]{:S(2)}) copy-start(bf16[4,2,2,64,256]{4,3,2,1,0:T(8,128)(2,1)} %constant.8.clone.taken_hbm) | copy-start | bytes 1572868
  5.1 1.0 %copy-start.4 = (bf16[4,2,128,256]{3,2,1,0:T(8,128)(2,1)S(1)}, bf16[4,2,128,256]{3,2,1,0:T(8,128)(2,1)}, u32[]{:S(2)}) copy-start(bf16[4,2,128,256]{3,2,1,0:T(8,128)(2,1)} %constant.6.clone.own_hbm) | copy-start | bytes 1572868
  6.1 0.9 %copy-start.5 = (f32[64,8,128]{2,1,0:T(8,128)S(1)}, f32[64,8,128]{2,1,0:T(8,128)}, u32[]{:S(2)}) copy-start(f32[64,8,128]{2,1,0:T(8,128)} %param.15) | copy-start | bytes 786436
  7.1 0.9 %copy-start.6 = (f32[64,8,128]{2,1,0:T(8,128)S(1)}, f32[64,8,128]{2,1,0:T(8,128)}, u32[]{:S(2)}) copy-start(f32[64,8,128]{2,1,0:T(8,128)} %param.17) | copy-start | bytes 786436
  8.0 0.9 %copy-start.7 = (f32[64,8,128]{2,1,0:T(8,128)S(1)}, f32[64,8,128]{2,1,0:T(8,128)}, u32[]{:S(2)}) copy-start(f32[64,8,128]{2,1,0:T(8,128)} %param.20) | copy-start | bytes 786436
  9.0 0.9 %copy-start.8 = (bf16[4,2,2,32,256]{4,3,2,1,0:T(8,128)(2,1)S(1)}, bf16[4,2,2,32,256]{4,3,2,1,0:T(8,128)(2,1)}, u32[]{:S(2)}) copy-start(bf16[4,2,2,32,256]{4,3,2,1,0:T(8,128)(2,1)} %constant.7.clone.sent_hbm) | copy-start | bytes 786436
  9.9 0.7 copy-start.9
  10.6 0.7 copy-start.10
  11.4 0.7 copy-start.11
  12.1 0.7 copy-start.12
  12.8 0.7 copy-start.13

commit v2 on v1

--- a/solution.py
+++ b/solution.py
@@ -27,6 +27,7 @@
 BLOCKS = PLANES // 8
 SLOTS = 2 * BLOCKS
 TILE_ROWS = 8 * FIELDS
+SHARE = (24, 16)
 HALF = LINES // 2
 ENTRY_ROWS = 32
 OBSERVERS = 512
@@ -148,6 +149,17 @@
     return [np.stack(pair, axis=1) for pair in zip(deriv, smooth)]
 
 
+def azimuth_rows():
+    gap = np.arange(NAZ)
+    line = FK * (np.power(FL, gap) + np.power(FL, NAZ - gap)) / (1.0 - FL**NAZ)
+    line[0] = FK * (1.0 + 2.0 * FL**NAZ / (1.0 - FL**NAZ)) + E0
+    for shift, value in ((1, E1), (2, E2)):
+        line[shift] += value
+        line[-shift] += value
+    rows = np.arange(ROWS)
+    return line[(gap[None, :] - rows[:, None]) % NAZ].astype(np.float32)
+
+
 def two_terms(value):
     high = value.astype(BF16)
     low = (value - high.astype(F32)).astype(BF16)
@@ -173,12 +185,13 @@
     azim_hbm,
     volume_hbm,
     radial_hbm,
-    area_ref,
-    observer_ref,
-    bin_ref,
-    weight_ref,
-    table_ref,
-    state_hbm,
+    area_hbm,
+    observer_hbm,
+    bin_hbm,
+    weight_hbm,
+    table_hbm,
+    azimuth_hbm,
+    final,
     signal_ref,
     own,
     sent,
@@ -190,12 +203,17 @@
     azim_metric,
     volume,
     radial,
+    area_ref,
+    observer_ref,
+    bin_ref,
+    weight_ref,
+    table_ref,
+    azimuth_ref,
     azim_flux,
     base,
     ratio,
     cells,
     lined,
-    final,
     edge_send,
     edge_recv,
     moment_send,
@@ -210,8 +228,9 @@
     part_recv,
     owner_send,
     owner_recv,
+    plane_send,
+    plane_recv,
     load_sem,
-    store_sem,
     edge_send_sem,
     edge_recv_sem,
     moment_send_sem,
@@ -224,13 +243,14 @@
     part_recv_sem,
     owner_send_sem,
     owner_recv_sem,
+    plane_send_sem,
+    plane_recv_sem,
 ):
     me_a = lax.axis_index("axial")
     me_z = lax.axis_index("azim")
     core = lax.rem(me_z, 2)
     chip = me_z // 2
     twin = me_z + 1 - 2 * core
-    reducer = core == 0
     after = lax.rem(me_z + 1, AZIM)
     before = lax.rem(me_z + AZIM - 1, AZIM)
 
@@ -242,6 +262,12 @@
         pltpu.make_async_copy(azim_hbm, azim_metric, load_sem.at[4]),
         pltpu.make_async_copy(volume_hbm, volume, load_sem.at[5]),
         pltpu.make_async_copy(radial_hbm, radial, load_sem.at[6]),
+        pltpu.make_async_copy(area_hbm, area_ref, load_sem.at[15]),
+        pltpu.make_async_copy(observer_hbm, observer_ref, load_sem.at[16]),
+        pltpu.make_async_copy(bin_hbm, bin_ref, load_sem.at[17]),
+        pltpu.make_async_copy(weight_hbm, weight_ref, load_sem.at[18]),
+        pltpu.make_async_copy(table_hbm, table_ref, load_sem.at[19]),
+        pltpu.make_async_copy(azimuth_hbm, azimuth_ref, load_sem.at[20]),
     ]
     for which in range(2):
         loads.append(
@@ -281,91 +307,103 @@
 
     for load in loads:
         load.wait()
-    pl.semaphore_wait(barrier, PEERS)
-
-    def send_moments(which, slot):
-        target = 2 * slot
-
-        @pl.when(target != me_z)
-        def _():
-            pltpu.make_async_remote_copy(
-                src_ref=moment_send.at[which, slot],
-                dst_ref=moment_recv.at[which, me_z],
-                send_sem=moment_send_sem.at[which],
-                recv_sem=moment_recv_sem.at[which],
-                device_id=(me_a, target),
-                device_id_type=MESH,
-            ).start()
-
-        @pl.when(target == me_z)
-        def _():
-            pltpu.make_async_copy(
-                moment_send.at[which, slot], moment_recv.at[which, me_z], moment_recv_sem.at[which]
-            ).start()
+
+    def send_moments(which):
+        def piece(step, carry):
+            target = lax.rem(me_z + step, AZIM)
+            slot, part = target // 2, lax.rem(target, 2)
+            for share in range(2):
+                rows = pl.ds(share * SHARE[0], SHARE[share])
+                source = moment_send.at[which, slot, rows]
+                dest = moment_recv.at[which, me_z, pl.ds(0, SHARE[share])]
+
+                @pl.when(jnp.logical_and(part == share, step > 0))
+                def _():
+                    pltpu.make_async_remote_copy(
+                        src_ref=source,
+                        dst_ref=dest,
+                        send_sem=moment_send_sem.at[which],
+                        recv_sem=moment_recv_sem.at[which],
+                        device_id=(me_a, target),
+                        device_id_type=MESH,
+                    ).start()
+
+                @pl.when(jnp.logical_and(part == share, step == 0))
+                def _():
+                    pltpu.make_async_copy(source, dest, moment_recv_sem.at[which]).start()
+
+            return carry
+
+        lax.fori_loop(0, AZIM, piece, 0)
 
     def wait_moment_sends(which):
-        @pl.when(reducer)
-        def _():
-            part = moment_send.at[which, pl.ds(0, SLOTS - 1)]
-            pltpu.make_async_copy(part, part, moment_send_sem.at[which]).wait()
-
-        @pl.when(jnp.logical_not(reducer))
-        def _():
-            part = moment_send.at[which]
-            pltpu.make_async_copy(part, part, moment_send_sem.at[which]).wait()
+        for share in range(2):
+
+            @pl.when(core == share)
+            def _():
+                part = moment_send.at[which, pl.ds(0, SLOTS - 1)]
+                pltpu.make_async_copy(part, part, moment_send_sem.at[which]).wait()
+                part = moment_send.at[which, SLOTS - 1, pl.ds(0, SHARE[1 - share])]
+                pltpu.make_async_copy(part, part, moment_send_sem.at[which]).wait()
 
     def reduce_moments(which, root):
         factor = root**ROWS
         wrap = 1.0 / (1.0 - root**NAZ)
-
-        @pl.when(reducer)
-        def _():
-            part = moment_recv.at[which]
-            pltpu.make_async_copy(part, part, moment_recv_sem.at[which]).wait()
-            side = lax.rem(chip, 2)
-
-            def place(step):
-                return step + side * (AZIM - 1 - 2 * step)
-
-            def gather(step, total):
-                return factor * total + moment_recv[which, place(step)]
-
-            first = lax.fori_loop(0, AZIM, gather, jnp.zeros((TILE_ROWS, LANES), F32)) * wrap
-
-            def hand_out(step, now):
-                other = place(step)
-                start_send[which, other] = now
-
-                @pl.when(other != me_z)
-                def _():
+        side = lax.rem(chip, 2)
+
+        def place(step):
+            return step + side * (AZIM - 1 - 2 * step)
+
+        for share in range(2):
+            rows = pl.ds(0, SHARE[share])
+            there = pl.ds(share * SHARE[0], SHARE[share])
+
+            @pl.when(core == share)
+            def _():
+                part = moment_recv.at[which, :, rows]
+                pltpu.make_async_copy(part, part, moment_recv_sem.at[which]).wait()
+
+                def gather(step, total):
+                    return factor * total + moment_recv[which, place(step), rows]
+
+                first = lax.fori_loop(0, AZIM, gather, jnp.zeros((SHARE[share], LANES), F32), unroll=8) * wrap
+
+                def follow(step, now):
+                    other = place(step)
+                    start_send[which, other, rows] = now
+                    return factor * now + moment_recv[which, other, rows]
+
+                lax.fori_loop(0, AZIM, follow, first, unroll=8)
+
+                pltpu.make_async_copy(
+                    start_send.at[which, me_z, rows], start_recv.at[which, chip, there], start_recv_sem.at[which]
+                ).start()
+
+                def hand_out(step, carry):
+                    other = lax.rem(me_z + step, AZIM)
                     pltpu.make_async_remote_copy(
-                        src_ref=start_send.at[which, other],
-                        dst_ref=start_recv.at[which, chip],
+                        src_ref=start_send.at[which, other, rows],
+                        dst_ref=start_recv.at[which, chip, there],
                         send_sem=start_send_sem.at[which],
                         recv_sem=start_recv_sem.at[which],
                         device_id=(me_a, other),
                         device_id_type=MESH,
                     ).start()
-
-                @pl.when(other == me_z)
-                def _():
-                    pltpu.make_async_copy(
-                        start_send.at[which, other], start_recv.at[which, chip], start_recv_sem.at[which]
-                    ).start()
-
-                return factor * now + moment_recv[which, other]
-
-            lax.fori_loop(0, AZIM, hand_out, first)
+                    return carry
+
+                lax.fori_loop(1, AZIM, hand_out, 0)
 
     def wait_starts(which):
         part = start_recv.at[which]
         pltpu.make_async_copy(part, part, start_recv_sem.at[which]).wait()
 
     def wait_start_sends(which):
-        @pl.when(reducer)
-        def _():
-            part = start_send.at[which, pl.ds(0, AZIM - 1)]
-            pltpu.make_async_copy(part, part, start_send_sem.at[which]).wait()
+        for share in range(2):
+
+            @pl.when(core == share)
+            def _():
+                part = start_send.at[which, pl.ds(0, AZIM - 1), pl.ds(0, SHARE[share])]
+                pltpu.make_async_copy(part, part, start_send_sem.at[which]).wait()
 
     def moments_of(values, root):
         up = root * values[0]
@@ -497,11 +535,11 @@
                         keep_cells(0, row, field, group, parts[field])
         for field in range(FIELDS):
             keep_moments(0, group, field, flux[field], DL)
-        for quarter in range(4):
-            send_moments(0, 4 * group + quarter)
         return carry
 
     lax.fori_loop(0, BLOCKS // 2, flux_group, 0)
+    pl.semaphore_wait(barrier, PEERS)
+    send_moments(0)
     for copy in halo_copies(0, deriv_halo, azim_flux, 1):
         copy.start()
     send_edges(0)
@@ -553,26 +591,115 @@
     send_edges(1)
     own_part(1)
     add_edges(1)
-    for copy in halo_copies(1, filter_halo, lined, 2):
-        copy.start()
+
+    plane_send[...] = lined[:, 0] + lined[:, 2 * PLANES]
+
+    def plane_copy(step):
+        other = lax.rem(me_z + step, AZIM)
+        return pltpu.make_async_remote_copy(
+            src_ref=plane_send,
+            dst_ref=plane_recv.at[AZIM - step],
+            send_sem=plane_send_sem,
+            recv_sem=plane_recv_sem,
+            device_id=(me_a, other),
+            device_id_type=MESH,
+        )
+
+    def send_plane(step, carry):
+        plane_copy(step).start()
+        return carry
+
+    lax.fori_loop(1, AZIM, send_plane, 0)
+    plane_recv[0] = plane_send[...]
 
     def moment_group(group, carry):
         for field in range(FIELDS):
             at = pl.ds(pl.multiple_of(field * PLANES + group * 16, 16), 16)
             keep_moments(1, group, field, [lined[row, at] for row in range(ROWS)], FL)
-        for quarter in range(4):
-            send_moments(1, 4 * group + quarter)
         return carry
 
     lax.fori_loop(0, BLOCKS // 2, moment_group, 0)
+    send_moments(1)
+    for copy in halo_copies(1, filter_halo, lined, 2):
+        copy.start()
+    pltpu.make_async_copy(
+        plane_recv.at[pl.ds(1, AZIM - 1)], plane_recv.at[pl.ds(1, AZIM - 1)], plane_recv_sem
+    ).wait()
+    filtered = jnp.dot(
+        azimuth_ref[...],
+        plane_recv[...].reshape(NAZ, LANES),
+        preferred_element_type=F32,
+        precision=lax.Precision.HIGHEST,
+    )
+    source = area_ref[...] * (filtered - 1.0)
+    picks = weight_ref[...]
+    low_half = jnp.take_along_axis(
+        jnp.broadcast_to(table_ref[pl.ds(0, 1)], (ENTRY_ROWS, LANES)), picks & 127, axis=1
+    )
+    high_half = jnp.take_along_axis(
+        jnp.broadcast_to(table_ref[pl.ds(1, 1)], (ENTRY_ROWS, LANES)), picks & 127, axis=1
+    )
+    weights = jnp.where(picks < LANES, low_half, high_half)
+    values = weights * jnp.concatenate([source] * 4, axis=0)
+    high, low = two_terms(values)
+    partial[pl.ds(0, ENTRY_ROWS)] = high.astype(F32)
+    partial[pl.ds(ENTRY_ROWS, ENTRY_ROWS)] = low.astype(F32)
+
+    def bin_row(row, carry):
+        same = lax.broadcasted_iota(jnp.int32, (TIME_BINS, LANES), 0) == bin_ref[pl.ds(row, 1)]
+        at = pl.multiple_of(row * LANES, LANES)
+        bin_hot[pl.ds(0, TIME_BINS), pl.ds(at, LANES)] = jnp.where(same, partial[pl.ds(row, 1)], 0.0).astype(BF16)
+        bin_hot[pl.ds(TIME_BINS, TIME_BINS), pl.ds(at, LANES)] = jnp.where(
+            same, partial[pl.ds(ENTRY_ROWS + row, 1)], 0.0
+        ).astype(BF16)
+        return carry
+
+    lax.fori_loop(0, ENTRY_ROWS, bin_row, 0)
+
+    total = dot_last(observer_hot[...], bin_hot[...])
+    partial[...] = total[:, :TIME_BINS] + total[:, TIME_BINS:]
+
+    mine = me_a * 2 + core
+
+    def part_copy(step):
+        other = lax.rem(mine + step, 8)
+        other_z = me_z - core + lax.rem(other, 2)
+        return pltpu.make_async_remote_copy(
+            src_ref=partial.at[pl.ds(pl.multiple_of(other * 64, 64), 64)],
+            dst_ref=part_recv.at[step - 1],
+            send_sem=part_send_sem.at[step - 1],
+            recv_sem=part_recv_sem.at[step - 1],
+            device_id=(other // 2, other_z),
+            device_id_type=MESH,
+        )
+
+    for step in range(1, 8):
+        part_copy(step).start()
     reduce_moments(1, FL)
+    total = partial[pl.ds(pl.multiple_of(mine * 64, 64), 64)]
+    for step in range(1, 8):
+        part_copy(step).wait_recv()
+        total = total + part_recv[step - 1]
+    for owner in range(16):
+        owner_send[owner, pl.ds(0, 4)] = total[4 * owner : 4 * owner + 4]
+        owner_send[owner, pl.ds(4, 4)] = jnp.zeros((4, LANES), F32)
+
+    def owner_copy(step):
+        other = lax.rem(chip + step, 16)
+        return pltpu.make_async_remote_copy(
+            src_ref=owner_send.at[other],
+            dst_ref=owner_recv.at[step - 1],
+            send_sem=owner_send_sem.at[step - 1],
+            recv_sem=owner_recv_sem.at[step - 1],
+            device_id=(me_a, 2 * other + core),
+            device_id_type=MESH,
+        )
+
+    for step in range(1, 16):
+        owner_copy(step).start()
     wait_starts(1)
     for copy in halo_copies(1, filter_halo, lined, 2):
         copy.wait_recv()
-
-    def store_copy(group):
-        planes = pl.ds(pl.multiple_of(group * 128, 128), 128)
-        return pltpu.make_async_copy(final.at[:, planes], state_hbm.at[:, planes], store_sem.at[group])
 
     def final_group(group, carry):
         for field in range(FIELDS):
@@ -593,91 +720,14 @@
                 final[field, pl.ds(group * 128 + row, 16, stride=ROWS)] = result
         return carry
 
-    def final_step(group, carry):
-        final_group(group, carry)
-        store_copy(group).start()
-        return carry
-
-    lax.fori_loop(0, BLOCKS // 2, final_step, 0)
-
-    source = area_ref[...] * (final[2, pl.ds(0, ROWS)] + final[0, pl.ds(0, ROWS)] - 1.0)
-    picks = weight_ref[...]
-    low_half = jnp.take_along_axis(
-        jnp.broadcast_to(table_ref[pl.ds(0, 1)], (ENTRY_ROWS, LANES)), picks & 127, axis=1
-    )
-    high_half = jnp.take_along_axis(
-        jnp.broadcast_to(table_ref[pl.ds(1, 1)], (ENTRY_ROWS, LANES)), picks & 127, axis=1
-    )
-    weights = jnp.where(picks < LANES, low_half, high_half)
-    values = weights * jnp.concatenate([source] * 4, axis=0)
-    high, low = two_terms(values)
-    partial[pl.ds(0, ENTRY_ROWS)] = high.astype(F32)
-    partial[pl.ds(ENTRY_ROWS, ENTRY_ROWS)] = low.astype(F32)
-
-    def bin_row(row, carry):
-        same = lax.broadcasted_iota(jnp.int32, (TIME_BINS, LANES), 0) == bin_ref[pl.ds(row, 1)]
-        at = pl.multiple_of(row * LANES, LANES)
-        bin_hot[pl.ds(0, TIME_BINS), pl.ds(at, LANES)] = jnp.where(same, partial[pl.ds(row, 1)], 0.0).astype(BF16)
-        bin_hot[pl.ds(TIME_BINS, TIME_BINS), pl.ds(at, LANES)] = jnp.where(
-            same, partial[pl.ds(ENTRY_ROWS + row, 1)], 0.0
-        ).astype(BF16)
-        return carry
-
-    lax.fori_loop(0, ENTRY_ROWS, bin_row, 0)
-
-    def sum_rows(step, carry):
-        at = pl.ds(pl.multiple_of(step * 128, 128), 128)
-        total = dot_last(observer_hot[at], bin_hot[...])
-        partial[at] = total[:, :TIME_BINS] + total[:, TIME_BINS:]
-        return carry
-
-    lax.fori_loop(0, OBSERVERS // 128, sum_rows, 0)
-
-    mine = me_a * 2 + core
-
-    def part_copy(step):
-        other = lax.rem(mine + step, 8)
-        other_z = me_z - core + lax.rem(other, 2)
-        return pltpu.make_async_remote_copy(
-            src_ref=partial.at[pl.ds(pl.multiple_of(other * 64, 64), 64)],
-            dst_ref=part_recv.at[step - 1],
-            send_sem=part_send_sem.at[step - 1],
-            recv_sem=part_recv_sem.at[step - 1],
-            device_id=(other // 2, other_z),
-            device_id_type=MESH,
-        )
-
-    for step in range(1, 8):
-        part_copy(step).start()
-    total = partial[pl.ds(pl.multiple_of(mine * 64, 64), 64)]
-    for step in range(1, 8):
-        part_copy(step).wait_recv()
-        total = total + part_recv[step - 1]
-    for owner in range(16):
-        owner_send[owner, pl.ds(0, 4)] = total[4 * owner : 4 * owner + 4]
-        owner_send[owner, pl.ds(4, 4)] = jnp.zeros((4, LANES), F32)
-
-    def owner_copy(step):
-        other = lax.rem(chip + step, 16)
-        return pltpu.make_async_remote_copy(
-            src_ref=owner_send.at[other],
-            dst_ref=owner_recv.at[step - 1],
-            send_sem=owner_send_sem.at[step - 1],
-            recv_sem=owner_recv_sem.at[step - 1],
-            device_id=(me_a, 2 * other + core),
-            device_id_type=MESH,
-        )
-
-    for step in range(1, 16):
-        owner_copy(step).start()
+    lax.fori_loop(0, BLOCKS // 2, final_group, 0)
+
     result = owner_send[chip]
     for step in range(1, 16):
         owner_copy(step).wait_recv()
         result = result + owner_recv[step - 1]
     signal_ref[...] = result[:4]
 
-    for group in range(BLOCKS // 2):
-        store_copy(group).wait()
     for which, halo, source_ref, depth in ((0, deriv_halo, azim_flux, 1), (1, filter_halo, lined, 2)):
         wait_moment_sends(which)
         wait_start_sends(which)
@@ -688,6 +738,9 @@
         part_copy(step).wait_send()
     for step in range(1, 16):
         owner_copy(step).wait_send()
+    pltpu.make_async_copy(
+        plane_recv.at[pl.ds(1, AZIM - 1)], plane_recv.at[pl.ds(1, AZIM - 1)], plane_send_sem
+    ).wait()
 
 
 def per_device(
@@ -706,7 +759,7 @@
 ):
     own, sent, taken = both_tables()
     rows = PLANES * ROWS
-    hbm = pl.BlockSpec(memory_space=pl.ANY)
+    hbm = pl.BlockSpec(memory_space=pltpu.HBM)
     vmem = pl.BlockSpec(memory_space=pltpu.VMEM)
     dma = pltpu.SemaphoreType.DMA
     state, signals = pl.pallas_call(
@@ -715,8 +768,8 @@
             jax.ShapeDtypeStruct((FIELDS, rows, LANES), F32),
             jax.ShapeDtypeStruct((4, TIME_BINS), F32),
         ),
-        in_specs=[hbm] * 10 + [vmem] * 5,
-        out_specs=(hbm, vmem),
+        in_specs=[hbm] * 16,
+        out_specs=(vmem, vmem),
         scratch_shapes=[
             pltpu.VMEM((2, 2 * LANES, 2 * LANES), BF16),
             pltpu.VMEM((2, 2, 32, 2 * LANES), BF16),
@@ -728,17 +781,22 @@
             pltpu.VMEM((3, rows, LANES), F32),
             pltpu.VMEM((rows, LANES), F32),
             pltpu.VMEM((FIELDS, rows, LANES), F32),
+            pltpu.VMEM((ROWS, LANES), F32),
+            pltpu.VMEM((ENTRY_ROWS, LANES), jnp.int32),
+            pltpu.VMEM((ENTRY_ROWS, LANES), jnp.int32),
+            pltpu.VMEM((ENTRY_ROWS, LANES), jnp.int32),
+            pltpu.VMEM((2, LANES), F32),
+            pltpu.VMEM((ROWS, NAZ), F32),
             pltpu.VMEM((ROWS, SLAB, LANES), F32),
             pltpu.VMEM((ROWS, SLAB, LANES), F32),
             pltpu.VMEM((ROWS, PLANES, LANES), F32),
             pltpu.VMEM((2, LINES, 2 * LANES), BF16),
             pltpu.VMEM((ROWS, SLAB, LANES), F32),
-            pltpu.VMEM((FIELDS, rows, LANES), F32),
             pltpu.VMEM((2, 2, 8, HALF), F32),
             pltpu.VMEM((2, AXIAL, 8, HALF), F32),
             pltpu.VMEM((2, SLOTS, TILE_ROWS, LANES), F32),
-            pltpu.VMEM((2, AZIM, TILE_ROWS, LANES), F32),
-            pltpu.VMEM((2, AZIM, TILE_ROWS, LANES), F32),
+            pltpu.VMEM((2, AZIM, SHARE[0], LANES), F32),
+            pltpu.VMEM((2, AZIM, SHARE[0], LANES), F32),
             pltpu.VMEM((2, SLOTS, TILE_ROWS, LANES), F32),
             pltpu.VMEM((2, 1, SLAB, LANES), F32),
             pltpu.VMEM((2, 2, SLAB, LANES), F32),
@@ -748,8 +806,9 @@
             pltpu.VMEM((7, 64, TIME_BINS), F32),
             pltpu.VMEM((16, 8, TIME_BINS), F32),
             pltpu.VMEM((15, 8, TIME_BINS), F32),
-            dma((15,)),
-            dma((BLOCKS // 2,)),
+            pltpu.VMEM((ROWS, LANES), F32),
+            pltpu.VMEM((AZIM, ROWS, LANES), F32),
+            dma((21,)),
             dma((2, 3)),
             dma((2, 3)),
             dma((2,)),
@@ -762,9 +821,11 @@
             dma((7,)),
             dma((15,)),
             dma((15,)),
+            dma(()),
+            dma(()),
         ],
         compiler_params=pltpu.CompilerParams(
-            collective_id=0, has_side_effects=True, vmem_limit_bytes=48 * 1024 * 1024
+            collective_id=0, has_side_effects=True
         ),
     )(
         jnp.asarray(own),
@@ -782,6 +843,7 @@
         bin_ids.reshape(ENTRY_ROWS, LANES),
         weight_ids.reshape(ENTRY_ROWS, LANES),
         bin_weights.reshape(2, LANES),
+        jnp.asarray(azimuth_rows()),
     )
     return state.reshape(FIELDS, PLANES, ROWS, LANES), signals
 

time: 79.8 us -> 52.8 us (0.66)
  Pallas kernels: 64 us -> 49 us
  local copies, waits for them, and re-layouts: 14.4 us -> 3.04 us
    pallas_call x1, Pallas kernels: 64 us -> 49 us  [per_device(): pl.pallas_call(kernel, out_shape=(jax.ShapeDtypeStruct((FIELDS, rows, LAN...]
    unnamed x30 -> x4, local copies, waits for them, and re-layouts: 14.4 us -> 3.04 us
where the time goes in v2:
time: 52.8 us; the launch traced here: 52.7 us
  Pallas kernels  49 us (93%)
  local copies, waits for them, and re-layouts  3.04 us (6%)
  between operations  0.65 us (1%)
    pallas_call x1, Pallas kernels, per_device(): pl.pallas_call(kernel, out_shape=(jax.ShapeDtypeStruct((FIELDS, rows, LAN...  49 us
    unnamed x4, local copies, waits for them, and re-layouts  3.04 us

profile of v2, /device:TPU:1, one launch (start us, length us, event | category | flops | bytes accessed | tf_op | source)
XLA Modules:
  0.0 52.7 jit_solution(13237920157708711437)
XLA Ops:
  0.6 49.0 %shard_map.167 = (f32[5,512,128]{2,1,0:T(8,128)}, f32[4,128]{1,0:T(4,128)}) custom-call(bf16[4,2,128,256]{3,2,1,0:T(8,128)(2,1)} %constant.8.clone.own_hbm, bf16[4,2,2,32,256]{4,3,2,1,0:T(8,128)(2,1)} %constant.9.clone.sent_hbm, bf16[4,2,2,64,256]{4,3,2,1,0:T(8,128)(2,1)} %constant.10.clone.taken_hbm, f32[512,128]{1,0:T(8,128)} %bitcast.17, ...), custom_call_target="tpu_custom_call" | custom-call | tf_op jit(solution)/shard_map/pallas_call | solution.py:765
  49.6 0.0 copy-start
  49.6 2.5 %copy.20 = f32[5,64,8,128]{3,2,1,0:T(8,128)} copy(f32[5,64,8,128]{3,2,1,0:T(8,128)} %bitcast.12) | data formatting | bytes 2621440
  52.1 0.0 copy-done
  52.1 0.6 %copy.21 = f32[4,128]{1,0:T(4,128)} copy(f32[4,128]{1,0:T(4,128)S(1)} %copy-done) | data formatting | bytes 4096
Async XLA Ops:
  49.6 2.5 %copy-start = (f32[4,128]{1,0:T(4,128)S(1)}, f32[4,128]{1,0:T(4,128)}, u32[]{:S(2)}) copy-start(f32[4,128]{1,0:T(4,128)} %get-tuple-element.9) | copy-start | bytes 6148

commit v3 on v2

--- a/solution.py
+++ b/solution.py
@@ -90,6 +90,7 @@
             - np.power(root, (2 * n - m - k * w + 1).astype(np.float64))
         ) @ side[lo:hi, cols]
     t = np.arange(w)
+    full = np.stack([whole[d * w : (d + 1) * w].T for d in range(AXIAL)]).astype(np.float32)
     own = np.zeros((AXIAL, w, 2 * w), ml_dtypes.bfloat16)
     sent = np.zeros((AXIAL, 2, 32, 2 * w), ml_dtypes.bfloat16)
     taken = np.zeros((AXIAL, 2, 64, 2 * w), ml_dtypes.bfloat16)
@@ -137,7 +138,7 @@
             high, low = split(rows)
             pair = np.concatenate([high, low], axis=1)
             taken[d, half] = np.concatenate([pair, pair], axis=0)
-    return own, sent, taken
+    return own, sent, taken, full
 
 
 def both_tables():
@@ -151,13 +152,18 @@
 
 def azimuth_rows():
     gap = np.arange(NAZ)
+    slope = DK * (np.power(DL, gap) - np.power(DL, NAZ - gap)) / (1.0 - DL**NAZ)
+    slope[0] = 0.0
+    slope[1] += C1
+    slope[-1] -= C1
     line = FK * (np.power(FL, gap) + np.power(FL, NAZ - gap)) / (1.0 - FL**NAZ)
     line[0] = FK * (1.0 + 2.0 * FL**NAZ / (1.0 - FL**NAZ)) + E0
     for shift, value in ((1, E1), (2, E2)):
         line[shift] += value
         line[-shift] += value
     rows = np.arange(ROWS)
-    return line[(gap[None, :] - rows[:, None]) % NAZ].astype(np.float32)
+    at = (gap[None, :] - rows[:, None]) % NAZ
+    return np.stack([slope[at], line[at]]).astype(np.float32)
 
 
 def two_terms(value):
@@ -191,6 +197,7 @@
     weight_hbm,
     table_hbm,
     azimuth_hbm,
+    full_hbm,
     final,
     signal_ref,
     own,
@@ -209,6 +216,7 @@
     weight_ref,
     table_ref,
     azimuth_ref,
+    full,
     azim_flux,
     base,
     ratio,
@@ -230,7 +238,12 @@
     owner_recv,
     plane_send,
     plane_recv,
+    axial_send,
+    axial_recv,
+    panel_axial,
     load_sem,
+    early_sem,
+    late_sem,
     edge_send_sem,
     edge_recv_sem,
     moment_send_sem,
@@ -245,6 +258,8 @@
     owner_recv_sem,
     plane_send_sem,
     plane_recv_sem,
+    axial_send_sem,
+    axial_recv_sem,
 ):
     me_a = lax.axis_index("axial")
     me_z = lax.axis_index("azim")
@@ -254,20 +269,37 @@
     after = lax.rem(me_z + 1, AZIM)
     before = lax.rem(me_z + AZIM - 1, AZIM)
 
+    def early_loads(group):
+        part = pl.ds(pl.multiple_of(group * 128, 128), 128)
+        whole = slice(None)
+        return [
+            pltpu.make_async_copy(source.at[where], dest.at[where], early_sem.at[number, group])
+            for number, (source, dest, where) in enumerate(
+                (
+                    (density_hbm, density, (part,)),
+                    (velocity_hbm, velocity, (whole, part)),
+                    (pressure_hbm, pressure, (part,)),
+                    (volume_hbm, volume, (part,)),
+                    (azim_hbm, azim_metric, (whole, part)),
+                )
+            )
+        ]
+
+    def late_loads(group):
+        part = pl.ds(pl.multiple_of(group * 128, 128), 128)
+        return [
+            pltpu.make_async_copy(axial_hbm.at[:, part], axial_metric.at[:, part], late_sem.at[0, group]),
+            pltpu.make_async_copy(radial_hbm.at[:, part], radial.at[:, part], late_sem.at[1, group]),
+        ]
+
     loads = [
-        pltpu.make_async_copy(density_hbm, density, load_sem.at[0]),
-        pltpu.make_async_copy(velocity_hbm, velocity, load_sem.at[1]),
-        pltpu.make_async_copy(pressure_hbm, pressure, load_sem.at[2]),
-        pltpu.make_async_copy(axial_hbm, axial_metric, load_sem.at[3]),
-        pltpu.make_async_copy(azim_hbm, azim_metric, load_sem.at[4]),
-        pltpu.make_async_copy(volume_hbm, volume, load_sem.at[5]),
-        pltpu.make_async_copy(radial_hbm, radial, load_sem.at[6]),
-        pltpu.make_async_copy(area_hbm, area_ref, load_sem.at[15]),
-        pltpu.make_async_copy(observer_hbm, observer_ref, load_sem.at[16]),
-        pltpu.make_async_copy(bin_hbm, bin_ref, load_sem.at[17]),
-        pltpu.make_async_copy(weight_hbm, weight_ref, load_sem.at[18]),
-        pltpu.make_async_copy(table_hbm, table_ref, load_sem.at[19]),
-        pltpu.make_async_copy(azimuth_hbm, azimuth_ref, load_sem.at[20]),
+        pltpu.make_async_copy(area_hbm, area_ref, load_sem.at[0]),
+        pltpu.make_async_copy(observer_hbm, observer_ref, load_sem.at[1]),
+        pltpu.make_async_copy(bin_hbm, bin_ref, load_sem.at[2]),
+        pltpu.make_async_copy(weight_hbm, weight_ref, load_sem.at[3]),
+        pltpu.make_async_copy(table_hbm, table_ref, load_sem.at[4]),
+        pltpu.make_async_copy(azimuth_hbm, azimuth_ref, load_sem.at[5]),
+        pltpu.make_async_copy(full_hbm.at[me_a], full, load_sem.at[6]),
     ]
     for which in range(2):
         loads.append(
@@ -282,6 +314,12 @@
         )
         loads.append(pltpu.make_async_copy(sent_hbm.at[me_a, which], sent.at[which], load_sem.at[9 + 4 * which]))
         loads.append(pltpu.make_async_copy(taken_hbm.at[me_a, which], taken.at[which], load_sem.at[10 + 4 * which]))
+    for group in range(BLOCKS // 2):
+        for load in early_loads(group):
+            load.start()
+    for group in range(BLOCKS // 2):
+        for load in late_loads(group):
+            load.start()
     for load in loads:
         load.start()
 
@@ -305,36 +343,35 @@
     edge_recv[0, pl.ds(me_a, 1)] = jnp.zeros((1, 8, HALF), F32)
     edge_recv[1, pl.ds(me_a, 1)] = jnp.zeros((1, 8, HALF), F32)
 
-    for load in loads:
-        load.wait()
+
+    def moment_copy(which, slot, share):
+        return pltpu.make_async_remote_copy(
+            src_ref=moment_send.at[which, slot, pl.ds(share * SHARE[0], SHARE[share])],
+            dst_ref=moment_recv.at[which, me_z, pl.ds(0, SHARE[share])],
+            send_sem=moment_send_sem.at[which],
+            recv_sem=moment_recv_sem.at[which],
+            device_id=(me_a, 2 * slot + share),
+            device_id_type=MESH,
+        )
 
     def send_moments(which):
-        def piece(step, carry):
-            target = lax.rem(me_z + step, AZIM)
-            slot, part = target // 2, lax.rem(target, 2)
+        def to_chip(step, carry):
+            slot = lax.rem(chip + step, SLOTS)
             for share in range(2):
-                rows = pl.ds(share * SHARE[0], SHARE[share])
-                source = moment_send.at[which, slot, rows]
-                dest = moment_recv.at[which, me_z, pl.ds(0, SHARE[share])]
-
-                @pl.when(jnp.logical_and(part == share, step > 0))
-                def _():
-                    pltpu.make_async_remote_copy(
-                        src_ref=source,
-                        dst_ref=dest,
-                        send_sem=moment_send_sem.at[which],
-                        recv_sem=moment_recv_sem.at[which],
-                        device_id=(me_a, target),
-                        device_id_type=MESH,
-                    ).start()
-
-                @pl.when(jnp.logical_and(part == share, step == 0))
-                def _():
-                    pltpu.make_async_copy(source, dest, moment_recv_sem.at[which]).start()
-
+                moment_copy(which, slot, share).start()
             return carry
 
-        lax.fori_loop(0, AZIM, piece, 0)
+        lax.fori_loop(1, SLOTS, to_chip, 0)
+        for share in range(2):
+
+            @pl.when(core == share)
+            def _():
+                moment_copy(which, chip, 1 - share).start()
+                pltpu.make_async_copy(
+                    moment_send.at[which, chip, pl.ds(share * SHARE[0], SHARE[share])],
+                    moment_recv.at[which, me_z, pl.ds(0, SHARE[share])],
+                    moment_recv_sem.at[which],
+                ).start()
 
     def wait_moment_sends(which):
         for share in range(2):
@@ -506,42 +543,114 @@
         cells[which, pl.ds(at, 16), pl.ds(0, LANES)] = high
         cells[which, pl.ds(at, 16), pl.ds(LANES, LANES)] = low
 
-    def flux_group(group, carry):
+    def axial_copy(which, step):
+        return pltpu.make_async_remote_copy(
+            src_ref=axial_send.at[which],
+            dst_ref=axial_recv.at[which, me_a],
+            send_sem=axial_send_sem.at[which, step - 1],
+            recv_sem=axial_recv_sem.at[which, step - 1],
+            device_id=(lax.rem(me_a + step, AXIAL), me_z),
+            device_id_type=MESH,
+        )
+
+    def send_axial(which, value):
+        axial_send[which] = value
+        axial_recv[which, pl.ds(me_a, 1)] = value[None]
+        for step in range(1, AXIAL):
+            axial_copy(which, step).start()
+
+    def take_axial(which):
+        for step in range(1, AXIAL):
+            axial_copy(which, step).wait_recv()
+        line = jnp.concatenate([axial_recv[which, k] for k in range(AXIAL)], axis=1)
+        return jnp.dot(line, full[which], preferred_element_type=F32, precision=lax.Precision.HIGHEST)
+
+    def send_plane(which, value):
+        plane_send[which] = value
+        plane_recv[which, 0] = value
+
+        def piece(step, carry):
+            pltpu.make_async_remote_copy(
+                src_ref=plane_send.at[which],
+                dst_ref=plane_recv.at[which, AZIM - step],
+                send_sem=plane_send_sem.at[which],
+                recv_sem=plane_recv_sem.at[which],
+                device_id=(me_a, lax.rem(me_z + step, AZIM)),
+                device_id_type=MESH,
+            ).start()
+            return carry
+
+        lax.fori_loop(1, AZIM, piece, 0)
+
+    def plane_wait(which, sem):
+        part = plane_recv.at[which, pl.ds(1, AZIM - 1)]
+        pltpu.make_async_copy(part, part, sem.at[which]).wait()
+
+    def take_plane(which):
+        plane_wait(which, plane_recv_sem)
+        return jnp.dot(
+            azimuth_ref[which],
+            plane_recv[which].reshape(NAZ, LANES),
+            preferred_element_type=F32,
+            precision=lax.Precision.HIGHEST,
+        )
+
+    def flux_of(metric, at, rho, vel, prs, vol, heat):
+        grad = [metric[comp, at] for comp in range(3)]
+        contra = vol * (grad[0] * vel[0] + grad[1] * vel[1] + grad[2] * vel[2])
+        flow = rho * contra
+        push = vol * prs
+        return [flow] + [flow * vel[comp] + grad[comp] * push for comp in range(3)] + [heat * contra]
+
+    def cells_at(group, row):
+        at = pl.ds(group * 128 + row, 16, stride=ROWS)
+        rho, prs, vol = density[at], pressure[at], volume[at]
+        vel = [velocity[comp, at] for comp in range(3)]
+        energy = 2.5 * prs + 0.5 * rho * (vel[0] * vel[0] + vel[1] * vel[1] + vel[2] * vel[2])
+        return at, rho, vel, prs, vol, energy
+
+    def azim_group(group, carry):
+        for load in early_loads(group):
+            load.wait()
         flux = [[None] * ROWS for _ in range(FIELDS)]
         for row in range(ROWS):
-            at = pl.ds(group * 128 + row, 16, stride=ROWS)
-            rho, prs, vol = density[at], pressure[at], volume[at]
-            vel = [velocity[comp, at] for comp in range(3)]
-            energy = 2.5 * prs + 0.5 * rho * (vel[0] * vel[0] + vel[1] * vel[1] + vel[2] * vel[2])
+            at, rho, vel, prs, vol, energy = cells_at(group, row)
+            parts = flux_of(azim_metric, at, rho, vel, prs, vol, energy + prs)
+            for field in range(FIELDS):
+                flux[field][row] = parts[field]
+                azim_flux[row, pl.ds(pl.multiple_of(field * PLANES + group * 16, 16), 16)] = parts[field]
+        for field in range(FIELDS):
+            keep_moments(0, group, field, flux[field], DL)
+        return carry
+
+    lax.fori_loop(0, BLOCKS // 2, azim_group, 0)
+    pl.semaphore_wait(barrier, PEERS)
+    send_moments(0)
+    send_plane(0, azim_flux[:, 0] + azim_flux[:, 2 * PLANES])
+    for copy in halo_copies(0, deriv_halo, azim_flux, 1):
+        copy.start()
+
+    def axial_group(group, carry):
+        for load in late_loads(group):
+            load.wait()
+        for row in range(ROWS):
+            at, rho, vel, prs, vol, energy = cells_at(group, row)
             state = [rho, rho * vel[0], rho * vel[1], rho * vel[2], energy]
-            here = pl.ds(pl.multiple_of(group * 16, 16), 16)
-            ratio[row, here] = SECTION / vol
+            ratio[row, pl.ds(pl.multiple_of(group * 16, 16), 16)] = SECTION / vol
             for field in range(FIELDS):
                 base[row, pl.ds(pl.multiple_of(field * PLANES + group * 16, 16), 16)] = (
                     state[field] + SECTION * radial[field, at]
                 )
-            heat = energy + prs
-            for metric, azimuthal in ((axial_metric, False), (azim_metric, True)):
-                grad = [metric[comp, at] for comp in range(3)]
-                contra = vol * (grad[0] * vel[0] + grad[1] * vel[1] + grad[2] * vel[2])
-                flow = rho * contra
-                push = vol * prs
-                parts = [flow] + [flow * vel[comp] + grad[comp] * push for comp in range(3)] + [heat * contra]
-                for field in range(FIELDS):
-                    if azimuthal:
-                        flux[field][row] = parts[field]
-                        azim_flux[row, pl.ds(pl.multiple_of(field * PLANES + group * 16, 16), 16)] = parts[field]
-                    else:
-                        keep_cells(0, row, field, group, parts[field])
-        for field in range(FIELDS):
-            keep_moments(0, group, field, flux[field], DL)
+            parts = flux_of(axial_metric, at, rho, vel, prs, vol, energy + prs)
+            for field in range(FIELDS):
+                keep_cells(0, row, field, group, parts[field])
+            panel_axial[group, pl.ds(row, 1)] = parts[0][:1] + parts[2][:1]
         return carry
 
-    lax.fori_loop(0, BLOCKS // 2, flux_group, 0)
-    pl.semaphore_wait(barrier, PEERS)
-    send_moments(0)
-    for copy in halo_copies(0, deriv_halo, azim_flux, 1):
-        copy.start()
+    lax.fori_loop(0, BLOCKS // 2, axial_group, 0)
+    send_axial(0, panel_axial[0])
+    for load in loads:
+        load.wait()
     send_edges(0)
 
     ids = observer_ref[...]
@@ -564,7 +673,10 @@
 
     own_part(0)
     reduce_moments(0, DL)
+    change = take_axial(0) + take_plane(0)
+    send_axial(1, base[:, 0] + base[:, 2 * PLANES] - ratio[:, 0] * change)
     add_edges(0)
+    send_plane(1, take_axial(1))
     wait_starts(0)
     for copy in halo_copies(0, deriv_halo, azim_flux, 1):
         copy.wait_recv()
@@ -592,26 +704,6 @@
     own_part(1)
     add_edges(1)
 
-    plane_send[...] = lined[:, 0] + lined[:, 2 * PLANES]
-
-    def plane_copy(step):
-        other = lax.rem(me_z + step, AZIM)
-        return pltpu.make_async_remote_copy(
-            src_ref=plane_send,
-            dst_ref=plane_recv.at[AZIM - step],
-            send_sem=plane_send_sem,
-            recv_sem=plane_recv_sem,
-            device_id=(me_a, other),
-            device_id_type=MESH,
-        )
-
-    def send_plane(step, carry):
-        plane_copy(step).start()
-        return carry
-
-    lax.fori_loop(1, AZIM, send_plane, 0)
-    plane_recv[0] = plane_send[...]
-
     def moment_group(group, carry):
         for field in range(FIELDS):
             at = pl.ds(pl.multiple_of(field * PLANES + group * 16, 16), 16)
@@ -622,16 +714,7 @@
     send_moments(1)
     for copy in halo_copies(1, filter_halo, lined, 2):
         copy.start()
-    pltpu.make_async_copy(
-        plane_recv.at[pl.ds(1, AZIM - 1)], plane_recv.at[pl.ds(1, AZIM - 1)], plane_recv_sem
-    ).wait()
-    filtered = jnp.dot(
-        azimuth_ref[...],
-        plane_recv[...].reshape(NAZ, LANES),
-        preferred_element_type=F32,
-        precision=lax.Precision.HIGHEST,
-    )
-    source = area_ref[...] * (filtered - 1.0)
+    source = area_ref[...] * (take_plane(1) - 1.0)
     picks = weight_ref[...]
     low_half = jnp.take_along_axis(
         jnp.broadcast_to(table_ref[pl.ds(0, 1)], (ENTRY_ROWS, LANES)), picks & 127, axis=1
@@ -738,9 +821,10 @@
         part_copy(step).wait_send()
     for step in range(1, 16):
         owner_copy(step).wait_send()
-    pltpu.make_async_copy(
-        plane_recv.at[pl.ds(1, AZIM - 1)], plane_recv.at[pl.ds(1, AZIM - 1)], plane_send_sem
-    ).wait()
+    for which in range(2):
+        plane_wait(which, plane_send_sem)
+        for step in range(1, AXIAL):
+            axial_copy(which, step).wait_send()
 
 
 def per_device(
@@ -757,7 +841,7 @@
     weight_ids,
     bin_weights,
 ):
-    own, sent, taken = both_tables()
+    own, sent, taken, full = both_tables()
     rows = PLANES * ROWS
     hbm = pl.BlockSpec(memory_space=pltpu.HBM)
     vmem = pl.BlockSpec(memory_space=pltpu.VMEM)
@@ -768,7 +852,7 @@
             jax.ShapeDtypeStruct((FIELDS, rows, LANES), F32),
             jax.ShapeDtypeStruct((4, TIME_BINS), F32),
         ),
-        in_specs=[hbm] * 16,
+        in_specs=[hbm] * 17,
         out_specs=(vmem, vmem),
         scratch_shapes=[
             pltpu.VMEM((2, 2 * LANES, 2 * LANES), BF16),
@@ -786,7 +870,8 @@
             pltpu.VMEM((ENTRY_ROWS, LANES), jnp.int32),
             pltpu.VMEM((ENTRY_ROWS, LANES), jnp.int32),
             pltpu.VMEM((2, LANES), F32),
-            pltpu.VMEM((ROWS, NAZ), F32),
+            pltpu.VMEM((2, ROWS, NAZ), F32),
+            pltpu.VMEM((2, NA, LANES), F32),
             pltpu.VMEM((ROWS, SLAB, LANES), F32),
             pltpu.VMEM((ROWS, SLAB, LANES), F32),
             pltpu.VMEM((ROWS, PLANES, LANES), F32),
@@ -806,9 +891,14 @@
             pltpu.VMEM((7, 64, TIME_BINS), F32),
             pltpu.VMEM((16, 8, TIME_BINS), F32),
             pltpu.VMEM((15, 8, TIME_BINS), F32),
-            pltpu.VMEM((ROWS, LANES), F32),
-            pltpu.VMEM((AZIM, ROWS, LANES), F32),
-            dma((21,)),
+            pltpu.VMEM((2, ROWS, LANES), F32),
+            pltpu.VMEM((2, AZIM, ROWS, LANES), F32),
+            pltpu.VMEM((2, ROWS, LANES), F32),
+            pltpu.VMEM((2, AXIAL, ROWS, LANES), F32),
+            pltpu.VMEM((BLOCKS // 2, ROWS, LANES), F32),
+            dma((15,)),
+            dma((5, BLOCKS // 2)),
+            dma((2, BLOCKS // 2)),
             dma((2, 3)),
             dma((2, 3)),
             dma((2,)),
@@ -821,8 +911,10 @@
             dma((7,)),
             dma((15,)),
             dma((15,)),
-            dma(()),
-            dma(()),
+            dma((2,)),
+            dma((2,)),
+            dma((2, 3)),
+            dma((2, 3)),
         ],
         compiler_params=pltpu.CompilerParams(
             collective_id=0, has_side_effects=True
@@ -844,6 +936,7 @@
         weight_ids.reshape(ENTRY_ROWS, LANES),
         bin_weights.reshape(2, LANES),
         jnp.asarray(azimuth_rows()),
+        jnp.asarray(full),
     )
     return state.reshape(FIELDS, PLANES, ROWS, LANES), signals
 

time: 52.8 us -> 51.5 us (0.975)
  Pallas kernels: 49 us -> 47.6 us
    pallas_call x1, Pallas kernels: 49 us -> 47.6 us  [per_device(): pl.pallas_call(kernel, out_shape=(jax.ShapeDtypeStruct((FIELDS, rows, LAN...]
where the time goes in v3:
time: 51.5 us; the launch traced here: 51.3 us
  Pallas kernels  47.6 us (92%)
  local copies, waits for them, and re-layouts  3.04 us (6%)
  between operations  0.65 us (1%)
    pallas_call x1, Pallas kernels, per_device(): pl.pallas_call(kernel, out_shape=(jax.ShapeDtypeStruct((FIELDS, rows, LAN...  47.6 us
    unnamed x4, local copies, waits for them, and re-layouts  3.04 us

profile of v3, /device:TPU:1, one launch (start us, length us, event | category | flops | bytes accessed | tf_op | source)
XLA Modules:
  0.0 51.3 jit_solution(1078747672189720763)
XLA Ops:
  0.6 47.6 %shard_map.176 = (f32[5,512,128]{2,1,0:T(8,128)}, f32[4,128]{1,0:T(4,128)}) custom-call(bf16[4,2,128,256]{3,2,1,0:T(8,128)(2,1)} %constant.10.clone.own_hbm, bf16[4,2,2,32,256]{4,3,2,1,0:T(8,128)(2,1)} %constant.11.clone.sent_hbm, bf16[4,2,2,64,256]{4,3,2,1,0:T(8,128)(2,1)} %constant.12.clone.taken_hbm, f32[512,128]{1,0:T(8,128)} %bitcast.17, ...), custom_call_target="tpu_custom_call" | custom-call | tf_op jit(solution)/shard_map/pallas_call | solution.py:849
  48.3 0.0 copy-start
  48.3 2.5 %copy.21 = f32[5,64,8,128]{3,2,1,0:T(8,128)} copy(f32[5,64,8,128]{3,2,1,0:T(8,128)} %bitcast.12) | data formatting | bytes 2621440
  50.7 0.0 copy-done
  50.7 0.6 %copy.22 = f32[4,128]{1,0:T(4,128)} copy(f32[4,128]{1,0:T(4,128)S(1)} %copy-done) | data formatting | bytes 4096
Async XLA Ops:
  48.3 2.5 %copy-start = (f32[4,128]{1,0:T(4,128)S(1)}, f32[4,128]{1,0:T(4,128)}, u32[]{:S(2)}) copy-start(f32[4,128]{1,0:T(4,128)} %get-tuple-element.9) | copy-start | bytes 6148

commit v4 on v3

--- a/solution.py
+++ b/solution.py
@@ -180,6 +180,63 @@
     return lax.dot_general(left, right, (((0,), (0,)), ((), ())), preferred_element_type=F32)
 
 
+def start_of(starts, group, field, side):
+    return jnp.concatenate(
+        [starts[4 * group + 2 * half + side, pl.ds(8 * field, 8)] for half in range(2)], axis=0
+    )
+
+
+def finish_kernel(
+    lined_hbm, halo_hbm, start_hbm, signal_hbm, state_hbm, result_hbm, lined, halo, starts, final, load_sem, store_sem
+):
+    signal_copy = pltpu.make_async_copy(signal_hbm, result_hbm, store_sem.at[BLOCKS // 2])
+    signal_copy.start()
+
+    def loads(group):
+        slots = pl.ds(pl.multiple_of(4 * group, 4), 4)
+        planes = pl.ds(pl.multiple_of(16 * group, 16), 16)
+        return [
+            pltpu.make_async_copy(start_hbm.at[slots], starts.at[slots], load_sem.at[group, 0]),
+            pltpu.make_async_copy(lined_hbm.at[:, :, planes], lined.at[:, :, planes], load_sem.at[group, 1]),
+            pltpu.make_async_copy(halo_hbm.at[:, :, planes], halo.at[:, :, planes], load_sem.at[group, 2]),
+        ]
+
+    def store(group):
+        planes = pl.ds(pl.multiple_of(group * 128, 128), 128)
+        return pltpu.make_async_copy(final.at[:, planes], state_hbm.at[:, planes], store_sem.at[group])
+
+    for group in range(BLOCKS // 2):
+        for load in loads(group):
+            load.start()
+
+    def final_group(group, carry):
+        for load in loads(group):
+            load.wait()
+        planes = pl.ds(pl.multiple_of(group * 16, 16), 16)
+        for field in range(FIELDS):
+            value = [halo[row, field, planes] for row in range(2)]
+            value += [lined[row, field, planes] for row in range(ROWS)]
+            value += [halo[2 + row, field, planes] for row in range(2)]
+            up = [start_of(starts, group, field, 0)]
+            for row in range(ROWS - 1):
+                up.append(FL * (value[row + 2] + up[-1]))
+            down = [start_of(starts, group, field, 1)]
+            for row in range(ROWS - 1, 0, -1):
+                down.append(FL * (value[row + 2] + down[-1]))
+            down = down[::-1]
+            for row in range(ROWS):
+                near = E1 * (value[row + 1] + value[row + 3]) + E2 * (value[row] + value[row + 4])
+                result = FK * (up[row] + down[row]) + (FK + E0) * value[row + 2] + near
+                final[field, pl.ds(group * 128 + row, 16, stride=ROWS)] = result
+        store(group).start()
+        return carry
+
+    lax.fori_loop(0, BLOCKS // 2, final_group, 0)
+    for group in range(BLOCKS // 2):
+        store(group).wait()
+    signal_copy.wait()
+
+
 def kernel(
     own_hbm,
     sent_hbm,
@@ -198,7 +255,9 @@
     table_hbm,
     azimuth_hbm,
     full_hbm,
-    final,
+    lined_hbm,
+    filter_halo,
+    start_hbm,
     signal_ref,
     own,
     sent,
@@ -229,7 +288,6 @@
     start_send,
     start_recv,
     deriv_halo,
-    filter_halo,
     observer_hot,
     bin_hot,
     partial,
@@ -241,6 +299,7 @@
     axial_send,
     axial_recv,
     panel_axial,
+    keep_sem,
     load_sem,
     early_sem,
     late_sem,
@@ -323,6 +382,7 @@
     for load in loads:
         load.start()
 
+    starts = (start_recv, start_hbm)
     barrier = pltpu.get_barrier_semaphore()
 
     def greet_azim(step, carry):
@@ -413,14 +473,14 @@
                 lax.fori_loop(0, AZIM, follow, first, unroll=8)
 
                 pltpu.make_async_copy(
-                    start_send.at[which, me_z, rows], start_recv.at[which, chip, there], start_recv_sem.at[which]
+                    start_send.at[which, me_z, rows], starts[which].at[chip, there], start_recv_sem.at[which]
                 ).start()
 
                 def hand_out(step, carry):
                     other = lax.rem(me_z + step, AZIM)
                     pltpu.make_async_remote_copy(
                         src_ref=start_send.at[which, other, rows],
-                        dst_ref=start_recv.at[which, chip, there],
+                        dst_ref=starts[which].at[chip, there],
                         send_sem=start_send_sem.at[which],
                         recv_sem=start_recv_sem.at[which],
                         device_id=(me_a, other),
@@ -431,7 +491,7 @@
                 lax.fori_loop(1, AZIM, hand_out, 0)
 
     def wait_starts(which):
-        part = start_recv.at[which]
+        part = starts[which]
         pltpu.make_async_copy(part, part, start_recv_sem.at[which]).wait()
 
     def wait_start_sends(which):
@@ -456,11 +516,6 @@
         for half in range(2):
             for side, value in ((0, up), (1, down)):
                 moment_send[which, 4 * group + 2 * half + side, pl.ds(8 * field, 8)] = value[8 * half : 8 * half + 8]
-
-    def start_of(which, group, field, side):
-        return jnp.concatenate(
-            [start_recv[which, 4 * group + 2 * half + side, pl.ds(8 * field, 8)] for half in range(2)], axis=0
-        )
 
     def halo_copies(which, halo, source, depth):
         return (
@@ -686,10 +741,10 @@
             at = pl.ds(pl.multiple_of(field * PLANES + group * 16, 16), 16)
             here = pl.ds(pl.multiple_of(group * 16, 16), 16)
             flux = [deriv_halo[0, 0, at]] + [azim_flux[row, at] for row in range(ROWS)] + [deriv_halo[1, 0, at]]
-            up = [start_of(0, group, field, 0)]
+            up = [start_of(start_recv, group, field, 0)]
             for row in range(ROWS - 1):
                 up.append(DL * (flux[row + 1] + up[-1]))
-            down = [start_of(0, group, field, 1)]
+            down = [start_of(start_recv, group, field, 1)]
             for row in range(ROWS - 1, 0, -1):
                 down.append(DL * (flux[row + 1] + down[-1]))
             down = down[::-1]
@@ -703,6 +758,9 @@
     send_edges(1)
     own_part(1)
     add_edges(1)
+
+    keep = pltpu.make_async_copy(lined, lined_hbm, keep_sem)
+    keep.start()
 
     def moment_group(group, carry):
         for field in range(FIELDS):
@@ -784,32 +842,12 @@
     for copy in halo_copies(1, filter_halo, lined, 2):
         copy.wait_recv()
 
-    def final_group(group, carry):
-        for field in range(FIELDS):
-            at = pl.ds(pl.multiple_of(field * PLANES + group * 16, 16), 16)
-            value = [filter_halo[0, 0, at], filter_halo[0, 1, at]]
-            value += [lined[row, at] for row in range(ROWS)]
-            value += [filter_halo[1, 0, at], filter_halo[1, 1, at]]
-            up = [start_of(1, group, field, 0)]
-            for row in range(ROWS - 1):
-                up.append(FL * (value[row + 2] + up[-1]))
-            down = [start_of(1, group, field, 1)]
-            for row in range(ROWS - 1, 0, -1):
-                down.append(FL * (value[row + 2] + down[-1]))
-            down = down[::-1]
-            for row in range(ROWS):
-                near = E1 * (value[row + 1] + value[row + 3]) + E2 * (value[row] + value[row + 4])
-                result = FK * (up[row] + down[row]) + (FK + E0) * value[row + 2] + near
-                final[field, pl.ds(group * 128 + row, 16, stride=ROWS)] = result
-        return carry
-
-    lax.fori_loop(0, BLOCKS // 2, final_group, 0)
-
     result = owner_send[chip]
     for step in range(1, 16):
         owner_copy(step).wait_recv()
         result = result + owner_recv[step - 1]
     signal_ref[...] = result[:4]
+    keep.wait()
 
     for which, halo, source_ref, depth in ((0, deriv_halo, azim_flux, 1), (1, filter_halo, lined, 2)):
         wait_moment_sends(which)
@@ -846,14 +884,16 @@
     hbm = pl.BlockSpec(memory_space=pltpu.HBM)
     vmem = pl.BlockSpec(memory_space=pltpu.VMEM)
     dma = pltpu.SemaphoreType.DMA
-    state, signals = pl.pallas_call(
+    lined, halo, starts, partial_signals = pl.pallas_call(
         kernel,
         out_shape=(
-            jax.ShapeDtypeStruct((FIELDS, rows, LANES), F32),
+            jax.ShapeDtypeStruct((ROWS, SLAB, LANES), F32),
+            jax.ShapeDtypeStruct((2, 2, SLAB, LANES), F32),
+            jax.ShapeDtypeStruct((SLOTS, TILE_ROWS, LANES), F32),
             jax.ShapeDtypeStruct((4, TIME_BINS), F32),
         ),
         in_specs=[hbm] * 17,
-        out_specs=(vmem, vmem),
+        out_specs=(hbm, hbm, hbm, vmem),
         scratch_shapes=[
             pltpu.VMEM((2, 2 * LANES, 2 * LANES), BF16),
             pltpu.VMEM((2, 2, 32, 2 * LANES), BF16),
@@ -882,9 +922,8 @@
             pltpu.VMEM((2, SLOTS, TILE_ROWS, LANES), F32),
             pltpu.VMEM((2, AZIM, SHARE[0], LANES), F32),
             pltpu.VMEM((2, AZIM, SHARE[0], LANES), F32),
-            pltpu.VMEM((2, SLOTS, TILE_ROWS, LANES), F32),
+            pltpu.VMEM((SLOTS, TILE_ROWS, LANES), F32),
             pltpu.VMEM((2, 1, SLAB, LANES), F32),
-            pltpu.VMEM((2, 2, SLAB, LANES), F32),
             pltpu.VMEM((OBSERVERS, ENTRY_ROWS * LANES), BF16),
             pltpu.VMEM((2 * TIME_BINS, ENTRY_ROWS * LANES), BF16),
             pltpu.VMEM((OBSERVERS, TIME_BINS), F32),
@@ -896,6 +935,7 @@
             pltpu.VMEM((2, ROWS, LANES), F32),
             pltpu.VMEM((2, AXIAL, ROWS, LANES), F32),
             pltpu.VMEM((BLOCKS // 2, ROWS, LANES), F32),
+            dma(()),
             dma((15,)),
             dma((5, BLOCKS // 2)),
             dma((2, BLOCKS // 2)),
@@ -938,6 +978,28 @@
         jnp.asarray(azimuth_rows()),
         jnp.asarray(full),
     )
+    state, signals = pl.pallas_call(
+        finish_kernel,
+        out_shape=(
+            jax.ShapeDtypeStruct((FIELDS, rows, LANES), F32),
+            jax.ShapeDtypeStruct((4, TIME_BINS), F32),
+        ),
+        in_specs=[hbm] * 4,
+        out_specs=(hbm, hbm),
+        scratch_shapes=[
+            pltpu.VMEM((ROWS, FIELDS, PLANES, LANES), F32),
+            pltpu.VMEM((4, FIELDS, PLANES, LANES), F32),
+            pltpu.VMEM((SLOTS, TILE_ROWS, LANES), F32),
+            pltpu.VMEM((FIELDS, rows, LANES), F32),
+            dma((BLOCKS // 2, 3)),
+            dma((BLOCKS // 2 + 1,)),
+        ],
+    )(
+        lined.reshape(ROWS, FIELDS, PLANES, LANES),
+        halo.reshape(4, FIELDS, PLANES, LANES),
+        starts,
+        partial_signals,
+    )
     return state.reshape(FIELDS, PLANES, ROWS, LANES), signals
 
 

time: 51.5 us -> 50.5 us (0.981)
  local copies, waits for them, and re-layouts: 3.04 us -> 0 us
  Pallas kernels: 47.6 us -> 49.2 us
    unnamed x4 -> x0, local copies, waits for them, and re-layouts: 3.04 us -> none
    pallas_call x1 -> x2, Pallas kernels: 47.6 us -> 49.2 us  [the longest x1 46.5 us: per_device(): pl.pallas_call(kernel, out_shape=(jax.ShapeDtypeStruct((ROWS, SLAB, LANES...]
where the time goes in v4:
time: 50.5 us; the launch traced here: 49.9 us
  Pallas kernels  49.2 us (97%)
  between operations  0.64 us (1%)
    pallas_call x1, Pallas kernels, per_device(): pl.pallas_call(kernel, out_shape=(jax.ShapeDtypeStruct((ROWS, SLAB, LANES...  46.5 us
    pallas_call x1, Pallas kernels, per_device(): pl.pallas_call(finish_kernel, out_shape=(jax.ShapeDtypeStruct((FIELDS, ro...  2.67 us

profile of v4, /device:TPU:1, one launch (start us, length us, event | category | flops | bytes accessed | tf_op | source)
XLA Modules:
  0.0 49.9 jit_solution(3467472767886644579)
XLA Ops:
  0.6 46.5 %shard_map.176 = (f32[8,320,128]{2,1,0:T(8,128)}, f32[2,2,320,128]{3,2,1,0:T(8,128)}, f32[16,40,128]{2,1,0:T(8,128)}, f32[4,128]{1,0:T(4,128)}) custom-call(bf16[4,2,128,256]{3,2,1,0:T(8,128)(2,1)} %constant.10.clone.own_hbm, bf16[4,2,2,32,256]{4,3,2,1,0:T(8,128)(2,1)} %constant.11.clone.sent_hbm, bf16[4,2,2,64,256]{4,3,2,1,0:T(8,128)(2,1)} %constant.12.clone.taken_hbm, ...), custom_call_target="tpu_custom_call" | custom-call | tf_op jit(solution)/shard_map/pallas_call | solution.py:887
  47.2 2.7 %shard_map.177 = (f32[5,512,128]{2,1,0:T(8,128)}, f32[4,128]{1,0:T(4,128)}) custom-call(f32[8,5,64,128]{3,2,1,0:T(8,128)} %bitcast.14, f32[4,5,64,128]{3,2,1,0:T(8,128)} %bitcast.19, f32[16,40,128]{2,1,0:T(8,128)} %get-tuple-element.10.start_hbm, f32[4,128]{1,0:T(4,128)} %get-tuple-element.11.signal_hbm), custom_call_target="tpu_custom_call" | custom-call | tf_op jit(solution)/shard_map/pallas_call | solution.py:981

commit v5 on v4

--- a/solution.py
+++ b/solution.py
@@ -28,6 +28,8 @@
 SLOTS = 2 * BLOCKS
 TILE_ROWS = 8 * FIELDS
 SHARE = (24, 16)
+STEPS = (2, 1, 3, 0)
+AWAY = tuple((dz, dy) for dz in STEPS[:3] for dy in STEPS[:3]) + ((2, 0), (0, 2), (1, 0), (3, 0), (0, 1), (0, 3))
 HALF = LINES // 2
 ENTRY_ROWS = 32
 OBSERVERS = 512
@@ -187,10 +189,24 @@
 
 
 def finish_kernel(
-    lined_hbm, halo_hbm, start_hbm, signal_hbm, state_hbm, result_hbm, lined, halo, starts, final, load_sem, store_sem
+    lined_hbm,
+    halo_hbm,
+    start_hbm,
+    part_hbm,
+    state_hbm,
+    signal_hbm,
+    lined,
+    halo,
+    starts,
+    final,
+    parts,
+    signals,
+    load_sem,
+    store_sem,
+    part_sem,
 ):
-    signal_copy = pltpu.make_async_copy(signal_hbm, result_hbm, store_sem.at[BLOCKS // 2])
-    signal_copy.start()
+    part_copy = pltpu.make_async_copy(part_hbm, parts, part_sem.at[0])
+    signal_copy = pltpu.make_async_copy(signals, signal_hbm, part_sem.at[1])
 
     def loads(group):
         slots = pl.ds(pl.multiple_of(4 * group, 4), 4)
@@ -208,6 +224,8 @@
     for group in range(BLOCKS // 2):
         for load in loads(group):
             load.start()
+        if group == 0:
+            part_copy.start()
 
     def final_group(group, carry):
         for load in loads(group):
@@ -231,7 +249,11 @@
         store(group).start()
         return carry
 
-    lax.fori_loop(0, BLOCKS // 2, final_group, 0)
+    final_group(0, 0)
+    part_copy.wait()
+    signals[...] = jnp.sum(parts[...], axis=0)[:4]
+    signal_copy.start()
+    lax.fori_loop(1, BLOCKS // 2, final_group, 0)
     for group in range(BLOCKS // 2):
         store(group).wait()
     signal_copy.wait()
@@ -258,7 +280,7 @@
     lined_hbm,
     filter_halo,
     start_hbm,
-    signal_ref,
+    owner_hbm,
     own,
     sent,
     taken,
@@ -293,13 +315,13 @@
     partial,
     part_recv,
     owner_send,
-    owner_recv,
     plane_send,
     plane_recv,
     axial_send,
     axial_recv,
     panel_axial,
     keep_sem,
+    owner_sem,
     load_sem,
     early_sem,
     late_sem,
@@ -328,6 +350,13 @@
     after = lax.rem(me_z + 1, AZIM)
     before = lax.rem(me_z + AZIM - 1, AZIM)
 
+    def chip_at(step):
+        return 4 * lax.rem(chip // 4 + step[0], 4) + lax.rem(chip + step[1], 4)
+
+    def group_at(step):
+        away = jnp.where(step == 0, STEPS[0], jnp.where(step == 1, STEPS[1], jnp.where(step == 2, STEPS[2], 0)))
+        return lax.rem(chip // 4 + away, 4)
+
     def early_loads(group):
         part = pl.ds(pl.multiple_of(group * 128, 128), 128)
         whole = slice(None)
@@ -373,8 +402,8 @@
         )
         loads.append(pltpu.make_async_copy(sent_hbm.at[me_a, which], sent.at[which], load_sem.at[9 + 4 * which]))
         loads.append(pltpu.make_async_copy(taken_hbm.at[me_a, which], taken.at[which], load_sem.at[10 + 4 * which]))
-    for group in range(BLOCKS // 2):
-        for load in early_loads(group):
+    for step in range(BLOCKS // 2):
+        for load in early_loads(group_at(step)):
             load.start()
     for group in range(BLOCKS // 2):
         for load in late_loads(group):
@@ -383,6 +412,7 @@
         load.start()
 
     starts = (start_recv, start_hbm)
+
     barrier = pltpu.get_barrier_semaphore()
 
     def greet_azim(step, carry):
@@ -414,17 +444,20 @@
             device_id_type=MESH,
         )
 
-    def send_moments(which):
-        def to_chip(step, carry):
-            slot = lax.rem(chip + step, SLOTS)
+    def send_moments(which, step):
+        row = 4 * group_at(step)
+        for turn in STEPS[:3]:
             for share in range(2):
-                moment_copy(which, slot, share).start()
-            return carry
-
-        lax.fori_loop(1, SLOTS, to_chip, 0)
+                moment_copy(which, row + lax.rem(chip + turn, 4), share).start()
+
+        @pl.when(step < 3)
+        def _():
+            for share in range(2):
+                moment_copy(which, row + lax.rem(chip, 4), share).start()
+
         for share in range(2):
 
-            @pl.when(core == share)
+            @pl.when(jnp.logical_and(step == 3, core == share))
             def _():
                 moment_copy(which, chip, 1 - share).start()
                 pltpu.make_async_copy(
@@ -476,8 +509,7 @@
                     start_send.at[which, me_z, rows], starts[which].at[chip, there], start_recv_sem.at[which]
                 ).start()
 
-                def hand_out(step, carry):
-                    other = lax.rem(me_z + step, AZIM)
+                def hand_out(other):
                     pltpu.make_async_remote_copy(
                         src_ref=start_send.at[which, other, rows],
                         dst_ref=starts[which].at[chip, there],
@@ -486,9 +518,11 @@
                         device_id=(me_a, other),
                         device_id_type=MESH,
                     ).start()
-                    return carry
-
-                lax.fori_loop(1, AZIM, hand_out, 0)
+
+                for step in AWAY:
+                    for half in range(2):
+                        hand_out(2 * chip_at(step) + half)
+                hand_out(twin)
 
     def wait_starts(which):
         part = starts[which]
@@ -561,7 +595,7 @@
             return carry
 
         lax.fori_loop(0, 2, piece, 0)
-        for step in range(1, AXIAL):
+        for step in STEPS[:3]:
             edge_copy(which, step).start()
 
     def own_part(which):
@@ -611,7 +645,7 @@
     def send_axial(which, value):
         axial_send[which] = value
         axial_recv[which, pl.ds(me_a, 1)] = value[None]
-        for step in range(1, AXIAL):
+        for step in STEPS[:3]:
             axial_copy(which, step).start()
 
     def take_axial(which):
@@ -624,18 +658,20 @@
         plane_send[which] = value
         plane_recv[which, 0] = value
 
-        def piece(step, carry):
+        def piece(other):
             pltpu.make_async_remote_copy(
                 src_ref=plane_send.at[which],
-                dst_ref=plane_recv.at[which, AZIM - step],
+                dst_ref=plane_recv.at[which, lax.rem(me_z - other + AZIM, AZIM)],
                 send_sem=plane_send_sem.at[which],
                 recv_sem=plane_recv_sem.at[which],
-                device_id=(me_a, lax.rem(me_z + step, AZIM)),
+                device_id=(me_a, other),
                 device_id_type=MESH,
             ).start()
-            return carry
-
-        lax.fori_loop(1, AZIM, piece, 0)
+
+        for step in AWAY:
+            for half in range(2):
+                piece(2 * chip_at(step) + half)
+        piece(twin)
 
     def plane_wait(which, sem):
         part = plane_recv.at[which, pl.ds(1, AZIM - 1)]
@@ -664,7 +700,8 @@
         energy = 2.5 * prs + 0.5 * rho * (vel[0] * vel[0] + vel[1] * vel[1] + vel[2] * vel[2])
         return at, rho, vel, prs, vol, energy
 
-    def azim_group(group, carry):
+    def azim_group(step, carry):
+        group = group_at(step)
         for load in early_loads(group):
             load.wait()
         flux = [[None] * ROWS for _ in range(FIELDS)]
@@ -676,11 +713,15 @@
                 azim_flux[row, pl.ds(pl.multiple_of(field * PLANES + group * 16, 16), 16)] = parts[field]
         for field in range(FIELDS):
             keep_moments(0, group, field, flux[field], DL)
+
+        @pl.when(step == 0)
+        def _():
+            pl.semaphore_wait(barrier, PEERS)
+
+        send_moments(0, step)
         return carry
 
     lax.fori_loop(0, BLOCKS // 2, azim_group, 0)
-    pl.semaphore_wait(barrier, PEERS)
-    send_moments(0)
     send_plane(0, azim_flux[:, 0] + azim_flux[:, 2 * PLANES])
     for copy in halo_copies(0, deriv_halo, azim_flux, 1):
         copy.start()
@@ -762,16 +803,15 @@
     keep = pltpu.make_async_copy(lined, lined_hbm, keep_sem)
     keep.start()
 
-    def moment_group(group, carry):
+    def moment_group(step, carry):
+        group = group_at(step)
         for field in range(FIELDS):
             at = pl.ds(pl.multiple_of(field * PLANES + group * 16, 16), 16)
             keep_moments(1, group, field, [lined[row, at] for row in range(ROWS)], FL)
+        send_moments(1, step)
         return carry
 
     lax.fori_loop(0, BLOCKS // 2, moment_group, 0)
-    send_moments(1)
-    for copy in halo_copies(1, filter_halo, lined, 2):
-        copy.start()
     source = area_ref[...] * (take_plane(1) - 1.0)
     picks = weight_ref[...]
     low_half = jnp.take_along_axis(
@@ -816,6 +856,8 @@
 
     for step in range(1, 8):
         part_copy(step).start()
+    for copy in halo_copies(1, filter_halo, lined, 2):
+        copy.start()
     reduce_moments(1, FL)
     total = partial[pl.ds(pl.multiple_of(mine * 64, 64), 64)]
     for step in range(1, 8):
@@ -829,7 +871,7 @@
         other = lax.rem(chip + step, 16)
         return pltpu.make_async_remote_copy(
             src_ref=owner_send.at[other],
-            dst_ref=owner_recv.at[step - 1],
+            dst_ref=owner_hbm.at[step],
             send_sem=owner_send_sem.at[step - 1],
             recv_sem=owner_recv_sem.at[step - 1],
             device_id=(me_a, 2 * other + core),
@@ -838,15 +880,15 @@
 
     for step in range(1, 16):
         owner_copy(step).start()
+    own_copy = pltpu.make_async_copy(owner_send.at[chip], owner_hbm.at[0], owner_sem)
+    own_copy.start()
     wait_starts(1)
     for copy in halo_copies(1, filter_halo, lined, 2):
         copy.wait_recv()
 
-    result = owner_send[chip]
+    own_copy.wait()
     for step in range(1, 16):
         owner_copy(step).wait_recv()
-        result = result + owner_recv[step - 1]
-    signal_ref[...] = result[:4]
     keep.wait()
 
     for which, halo, source_ref, depth in ((0, deriv_halo, azim_flux, 1), (1, filter_halo, lined, 2)):
@@ -882,18 +924,17 @@
     own, sent, taken, full = both_tables()
     rows = PLANES * ROWS
     hbm = pl.BlockSpec(memory_space=pltpu.HBM)
-    vmem = pl.BlockSpec(memory_space=pltpu.VMEM)
     dma = pltpu.SemaphoreType.DMA
-    lined, halo, starts, partial_signals = pl.pallas_call(
+    lined, halo, starts, parts = pl.pallas_call(
         kernel,
         out_shape=(
             jax.ShapeDtypeStruct((ROWS, SLAB, LANES), F32),
             jax.ShapeDtypeStruct((2, 2, SLAB, LANES), F32),
             jax.ShapeDtypeStruct((SLOTS, TILE_ROWS, LANES), F32),
-            jax.ShapeDtypeStruct((4, TIME_BINS), F32),
+            jax.ShapeDtypeStruct((16, 8, TIME_BINS), F32),
         ),
         in_specs=[hbm] * 17,
-        out_specs=(hbm, hbm, hbm, vmem),
+        out_specs=(hbm, hbm, hbm, hbm),
         scratch_shapes=[
             pltpu.VMEM((2, 2 * LANES, 2 * LANES), BF16),
             pltpu.VMEM((2, 2, 32, 2 * LANES), BF16),
@@ -929,12 +970,12 @@
             pltpu.VMEM((OBSERVERS, TIME_BINS), F32),
             pltpu.VMEM((7, 64, TIME_BINS), F32),
             pltpu.VMEM((16, 8, TIME_BINS), F32),
-            pltpu.VMEM((15, 8, TIME_BINS), F32),
             pltpu.VMEM((2, ROWS, LANES), F32),
             pltpu.VMEM((2, AZIM, ROWS, LANES), F32),
             pltpu.VMEM((2, ROWS, LANES), F32),
             pltpu.VMEM((2, AXIAL, ROWS, LANES), F32),
             pltpu.VMEM((BLOCKS // 2, ROWS, LANES), F32),
+            dma(()),
             dma(()),
             dma((15,)),
             dma((5, BLOCKS // 2)),
@@ -991,14 +1032,17 @@
             pltpu.VMEM((4, FIELDS, PLANES, LANES), F32),
             pltpu.VMEM((SLOTS, TILE_ROWS, LANES), F32),
             pltpu.VMEM((FIELDS, rows, LANES), F32),
+            pltpu.VMEM((16, 8, TIME_BINS), F32),
+            pltpu.VMEM((4, TIME_BINS), F32),
             dma((BLOCKS // 2, 3)),
-            dma((BLOCKS // 2 + 1,)),
+            dma((BLOCKS // 2,)),
+            dma((2,)),
         ],
     )(
         lined.reshape(ROWS, FIELDS, PLANES, LANES),
         halo.reshape(4, FIELDS, PLANES, LANES),
         starts,
-        partial_signals,
+        parts,
     )
     return state.reshape(FIELDS, PLANES, ROWS, LANES), signals
 

time: 50.5 us -> 49.6 us (0.982)
    pallas_call x1, Pallas kernels: 46.5 us -> 45.8 us  [per_device(): pl.pallas_call(kernel, out_shape=(jax.ShapeDtypeStruct((ROWS, SLAB, LANES...]
where the time goes in v5:
time: 49.6 us; the launch traced here: 49.4 us
  Pallas kernels  48.8 us (98%)
  between operations  0.64 us (1%)
    pallas_call x1, Pallas kernels, per_device(): pl.pallas_call(kernel, out_shape=(jax.ShapeDtypeStruct((ROWS, SLAB, LANES...  45.8 us
    pallas_call x1, Pallas kernels, per_device(): pl.pallas_call(finish_kernel, out_shape=(jax.ShapeDtypeStruct((FIELDS, ro...  2.97 us

profile of v5, /device:TPU:1, one launch (start us, length us, event | category | flops | bytes accessed | tf_op | source)
XLA Modules:
  0.0 49.4 jit_solution(11855960426443244726)
XLA Ops:
  0.6 45.8 %shard_map.176 = (f32[8,320,128]{2,1,0:T(8,128)}, f32[2,2,320,128]{3,2,1,0:T(8,128)}, f32[16,40,128]{2,1,0:T(8,128)}, f32[16,8,128]{2,1,0:T(8,128)}) custom-call(bf16[4,2,128,256]{3,2,1,0:T(8,128)(2,1)} %constant.10.clone.own_hbm, bf16[4,2,2,32,256]{4,3,2,1,0:T(8,128)(2,1)} %constant.11.clone.sent_hbm, bf16[4,2,2,64,256]{4,3,2,1,0:T(8,128)(2,1)} %constant.12.clone.taken_hbm, ...), custom_call_target="tpu_custom_call" | custom-call | tf_op jit(solution)/shard_map/pallas_call | solution.py:928
  46.5 3.0 %shard_map.177 = (f32[5,512,128]{2,1,0:T(8,128)}, f32[4,128]{1,0:T(4,128)}) custom-call(f32[8,5,64,128]{3,2,1,0:T(8,128)} %bitcast.14, f32[4,5,64,128]{3,2,1,0:T(8,128)} %bitcast.19, f32[16,40,128]{2,1,0:T(8,128)} %get-tuple-element.10.start_hbm, f32[16,8,128]{2,1,0:T(8,128)} %get-tuple-element.11.part_hbm), custom_call_target="tpu_custom_call" | custom-call | tf_op jit(solution)/shard_map/pallas_call | solution.py:1022

commit v6 on v5

--- a/solution.py
+++ b/solution.py
@@ -23,14 +23,14 @@
 NA = AXIAL * LANES
 NAZ = AZIM * ROWS
 SLAB = FIELDS * PLANES
-LINES = ROWS * SLAB
 BLOCKS = PLANES // 8
 SLOTS = 2 * BLOCKS
 TILE_ROWS = 8 * FIELDS
-SHARE = (24, 16)
+PARTS = ((0, 3), (3, 2))
+PART_OF = (0, 0, 0, 1, 1)
+SHARE = (((0, 16), (16, 8)), ((24, 8), (32, 8)))
 STEPS = (2, 1, 3, 0)
 AWAY = tuple((dz, dy) for dz in STEPS[:3] for dy in STEPS[:3]) + ((2, 0), (0, 2), (1, 0), (3, 0), (0, 1), (0, 3))
-HALF = LINES // 2
 ENTRY_ROWS = 32
 OBSERVERS = 512
 TIME_BINS = 128
@@ -93,12 +93,9 @@
         ) @ side[lo:hi, cols]
     t = np.arange(w)
     full = np.stack([whole[d * w : (d + 1) * w].T for d in range(AXIAL)]).astype(np.float32)
-    own = np.zeros((AXIAL, w, 2 * w), ml_dtypes.bfloat16)
     sent = np.zeros((AXIAL, 2, 32, 2 * w), ml_dtypes.bfloat16)
     taken = np.zeros((AXIAL, 2, 64, 2 * w), ml_dtypes.bfloat16)
     for d in range(AXIAL):
-        high, low = split(whole[d * w : (d + 1) * w, d * w : (d + 1) * w].T)
-        own[d] = np.concatenate([high, low], axis=1)
         for half in range(2):
             rows = np.zeros((16, w))
             base = half * 4
@@ -140,7 +137,7 @@
             high, low = split(rows)
             pair = np.concatenate([high, low], axis=1)
             taken[d, half] = np.concatenate([pair, pair], axis=0)
-    return own, sent, taken, full
+    return sent, taken, full
 
 
 def both_tables():
@@ -260,7 +257,6 @@
 
 
 def kernel(
-    own_hbm,
     sent_hbm,
     taken_hbm,
     density_hbm,
@@ -301,10 +297,14 @@
     azim_flux,
     base,
     ratio,
-    cells,
-    lined,
-    edge_send,
-    edge_recv,
+    cells_a,
+    cells_b,
+    lined_a,
+    lined_b,
+    edge_send_a,
+    edge_send_b,
+    edge_recv_a,
+    edge_recv_b,
     moment_send,
     moment_recv,
     start_send,
@@ -390,18 +390,8 @@
         pltpu.make_async_copy(full_hbm.at[me_a], full, load_sem.at[6]),
     ]
     for which in range(2):
-        loads.append(
-            pltpu.make_async_copy(
-                own_hbm.at[me_a, which], own.at[which, pl.ds(0, LANES)], load_sem.at[7 + 4 * which]
-            )
-        )
-        loads.append(
-            pltpu.make_async_copy(
-                own_hbm.at[me_a, which], own.at[which, pl.ds(LANES, LANES)], load_sem.at[8 + 4 * which]
-            )
-        )
-        loads.append(pltpu.make_async_copy(sent_hbm.at[me_a, which], sent.at[which], load_sem.at[9 + 4 * which]))
-        loads.append(pltpu.make_async_copy(taken_hbm.at[me_a, which], taken.at[which], load_sem.at[10 + 4 * which]))
+        loads.append(pltpu.make_async_copy(sent_hbm.at[me_a, which], sent.at[which], load_sem.at[7 + 2 * which]))
+        loads.append(pltpu.make_async_copy(taken_hbm.at[me_a, which], taken.at[which], load_sem.at[8 + 2 * which]))
     for step in range(BLOCKS // 2):
         for load in early_loads(group_at(step)):
             load.start()
@@ -412,6 +402,8 @@
         load.start()
 
     starts = (start_recv, start_hbm)
+    cells, lined = (cells_a, cells_b), (lined_a, lined_b)
+    edge_send, edge_recv = (edge_send_a, edge_send_b), (edge_recv_a, edge_recv_b)
 
     barrier = pltpu.get_barrier_semaphore()
 
@@ -430,53 +422,58 @@
 
     lax.fori_loop(1, AXIAL, greet_axial, 0)
 
-    edge_recv[0, pl.ds(me_a, 1)] = jnp.zeros((1, 8, HALF), F32)
-    edge_recv[1, pl.ds(me_a, 1)] = jnp.zeros((1, 8, HALF), F32)
-
-
-    def moment_copy(which, slot, share):
+    for part in range(2):
+        for which in range(2):
+            edge_recv[part][which, pl.ds(me_a, 1)] = jnp.zeros((1, 8, 4 * PLANES * PARTS[part][1]), F32)
+
+    def moment_source(which, part, slot, share):
+        first, rows = SHARE[part][share]
+        return moment_send.at[which, slot, pl.ds(first, rows)]
+
+    def moment_copy(which, part, slot, share):
         return pltpu.make_async_remote_copy(
-            src_ref=moment_send.at[which, slot, pl.ds(share * SHARE[0], SHARE[share])],
-            dst_ref=moment_recv.at[which, me_z, pl.ds(0, SHARE[share])],
-            send_sem=moment_send_sem.at[which],
-            recv_sem=moment_recv_sem.at[which],
+            src_ref=moment_source(which, part, slot, share),
+            dst_ref=moment_recv.at[which, part, me_z, pl.ds(0, SHARE[part][share][1])],
+            send_sem=moment_send_sem.at[which, part],
+            recv_sem=moment_recv_sem.at[which, part],
             device_id=(me_a, 2 * slot + share),
             device_id_type=MESH,
         )
 
-    def send_moments(which, step):
+    def send_moments(which, part, step):
         row = 4 * group_at(step)
         for turn in STEPS[:3]:
             for share in range(2):
-                moment_copy(which, row + lax.rem(chip + turn, 4), share).start()
+                moment_copy(which, part, row + lax.rem(chip + turn, 4), share).start()
 
         @pl.when(step < 3)
         def _():
             for share in range(2):
-                moment_copy(which, row + lax.rem(chip, 4), share).start()
+                moment_copy(which, part, row + lax.rem(chip, 4), share).start()
 
         for share in range(2):
 
             @pl.when(jnp.logical_and(step == 3, core == share))
             def _():
-                moment_copy(which, chip, 1 - share).start()
+                moment_copy(which, part, chip, 1 - share).start()
                 pltpu.make_async_copy(
-                    moment_send.at[which, chip, pl.ds(share * SHARE[0], SHARE[share])],
-                    moment_recv.at[which, me_z, pl.ds(0, SHARE[share])],
-                    moment_recv_sem.at[which],
+                    moment_source(which, part, chip, share),
+                    moment_recv.at[which, part, me_z, pl.ds(0, SHARE[part][share][1])],
+                    moment_recv_sem.at[which, part],
                 ).start()
 
-    def wait_moment_sends(which):
+    def wait_moment_sends(which, part):
         for share in range(2):
 
             @pl.when(core == share)
             def _():
-                part = moment_send.at[which, pl.ds(0, SLOTS - 1)]
-                pltpu.make_async_copy(part, part, moment_send_sem.at[which]).wait()
-                part = moment_send.at[which, SLOTS - 1, pl.ds(0, SHARE[1 - share])]
-                pltpu.make_async_copy(part, part, moment_send_sem.at[which]).wait()
-
-    def reduce_moments(which, root):
+                rows = pl.ds(8 * PARTS[part][0], 8 * PARTS[part][1])
+                sent_rows = moment_send.at[which, pl.ds(0, SLOTS - 1), rows]
+                pltpu.make_async_copy(sent_rows, sent_rows, moment_send_sem.at[which, part]).wait()
+                sent_rows = moment_source(which, part, SLOTS - 1, 1 - share)
+                pltpu.make_async_copy(sent_rows, sent_rows, moment_send_sem.at[which, part]).wait()
+
+    def reduce_moments(which, part, root):
         factor = root**ROWS
         wrap = 1.0 / (1.0 - root**NAZ)
         side = lax.rem(chip, 2)
@@ -485,36 +482,32 @@
             return step + side * (AZIM - 1 - 2 * step)
 
         for share in range(2):
-            rows = pl.ds(0, SHARE[share])
-            there = pl.ds(share * SHARE[0], SHARE[share])
+            first_row, count = SHARE[part][share]
+            rows, there = pl.ds(0, count), pl.ds(first_row, count)
 
             @pl.when(core == share)
             def _():
-                part = moment_recv.at[which, :, rows]
-                pltpu.make_async_copy(part, part, moment_recv_sem.at[which]).wait()
+                arrived = moment_recv.at[which, part, :, rows]
+                pltpu.make_async_copy(arrived, arrived, moment_recv_sem.at[which, part]).wait()
 
                 def gather(step, total):
-                    return factor * total + moment_recv[which, place(step), rows]
-
-                first = lax.fori_loop(0, AZIM, gather, jnp.zeros((SHARE[share], LANES), F32), unroll=8) * wrap
+                    return factor * total + moment_recv[which, part, place(step), rows]
+
+                first = lax.fori_loop(0, AZIM, gather, jnp.zeros((count, LANES), F32), unroll=8) * wrap
 
                 def follow(step, now):
                     other = place(step)
-                    start_send[which, other, rows] = now
-                    return factor * now + moment_recv[which, other, rows]
+                    start_send[which, part, other, rows] = now
+                    return factor * now + moment_recv[which, part, other, rows]
 
                 lax.fori_loop(0, AZIM, follow, first, unroll=8)
-
-                pltpu.make_async_copy(
-                    start_send.at[which, me_z, rows], starts[which].at[chip, there], start_recv_sem.at[which]
-                ).start()
 
                 def hand_out(other):
                     pltpu.make_async_remote_copy(
-                        src_ref=start_send.at[which, other, rows],
+                        src_ref=start_send.at[which, part, other, rows],
                         dst_ref=starts[which].at[chip, there],
-                        send_sem=start_send_sem.at[which],
-                        recv_sem=start_recv_sem.at[which],
+                        send_sem=start_send_sem.at[which, part],
+                        recv_sem=start_recv_sem.at[which, part],
                         device_id=(me_a, other),
                         device_id_type=MESH,
                     ).start()
@@ -523,18 +516,23 @@
                     for half in range(2):
                         hand_out(2 * chip_at(step) + half)
                 hand_out(twin)
-
-    def wait_starts(which):
-        part = starts[which]
-        pltpu.make_async_copy(part, part, start_recv_sem.at[which]).wait()
-
-    def wait_start_sends(which):
+                pltpu.make_async_copy(
+                    start_send.at[which, part, me_z, rows],
+                    starts[which].at[chip, there],
+                    start_recv_sem.at[which, part],
+                ).start()
+
+    def wait_starts(which, part):
+        arrived = starts[which].at[:, pl.ds(8 * PARTS[part][0], 8 * PARTS[part][1])]
+        pltpu.make_async_copy(arrived, arrived, start_recv_sem.at[which, part]).wait()
+
+    def wait_start_sends(which, part):
         for share in range(2):
 
             @pl.when(core == share)
             def _():
-                part = start_send.at[which, pl.ds(0, AZIM - 1), pl.ds(0, SHARE[share])]
-                pltpu.make_async_copy(part, part, start_send_sem.at[which]).wait()
+                gone = start_send.at[which, part, pl.ds(0, AZIM - 1), pl.ds(0, SHARE[part][share][1])]
+                pltpu.make_async_copy(gone, gone, start_send_sem.at[which, part]).wait()
 
     def moments_of(values, root):
         up = root * values[0]
@@ -551,86 +549,93 @@
             for side, value in ((0, up), (1, down)):
                 moment_send[which, 4 * group + 2 * half + side, pl.ds(8 * field, 8)] = value[8 * half : 8 * half + 8]
 
-    def halo_copies(which, halo, source, depth):
-        return (
-            pltpu.make_async_remote_copy(
-                src_ref=source.at[pl.ds(ROWS - depth, depth)],
-                dst_ref=halo.at[0],
-                send_sem=halo_send_sem.at[which, 0],
-                recv_sem=halo_recv_sem.at[which, 0],
-                device_id=(me_a, after),
-                device_id_type=MESH,
-            ),
-            pltpu.make_async_remote_copy(
-                src_ref=source.at[pl.ds(0, depth)],
-                dst_ref=halo.at[1],
-                send_sem=halo_send_sem.at[which, 1],
-                recv_sem=halo_recv_sem.at[which, 1],
-                device_id=(me_a, before),
-                device_id_type=MESH,
-            ),
-        )
-
-    def edge_copy(which, step):
+    def halo_copies(which):
+        copies = []
+        for part in range(2):
+            if which == 1:
+                source, halo, depth = lined[part], filter_halo, 2
+                there = pl.ds(PLANES * PARTS[part][0], PLANES * PARTS[part][1])
+            else:
+                source, halo, depth = azim_flux, deriv_halo, 1
+                there = pl.ds(0, SLAB)
+                if part == 1:
+                    break
+            for side, other, rows in ((0, after, pl.ds(ROWS - depth, depth)), (1, before, pl.ds(0, depth))):
+                copies.append(
+                    pltpu.make_async_remote_copy(
+                        src_ref=source.at[rows],
+                        dst_ref=halo.at[side, :, there],
+                        send_sem=halo_send_sem.at[which, part, side],
+                        recv_sem=halo_recv_sem.at[which, part, side],
+                        device_id=(me_a, other),
+                        device_id_type=MESH,
+                    )
+                )
+        return copies
+
+    def edge_copy(which, part, step):
         other = lax.rem(me_a + step, AXIAL)
         down = jnp.where(other < me_a, 1, 0)
         return pltpu.make_async_remote_copy(
-            src_ref=edge_send.at[which, down],
-            dst_ref=edge_recv.at[which, me_a],
-            send_sem=edge_send_sem.at[which, step - 1],
-            recv_sem=edge_recv_sem.at[which, step - 1],
+            src_ref=edge_send[part].at[which, down],
+            dst_ref=edge_recv[part].at[which, me_a],
+            send_sem=edge_send_sem.at[which, part, step - 1],
+            recv_sem=edge_recv_sem.at[which, part, step - 1],
             device_id=(other, me_z),
             device_id_type=MESH,
         )
 
-    def send_edges(which):
+    def send_edges(which, part):
+        slab = PLANES * PARTS[part][1]
+
         def piece(step, carry):
-            at = pl.multiple_of(step * 640, 640)
-            total = dot_last(sent[which, 0], cells[which, pl.ds(at, 640)]) + dot_last(
-                sent[which, 1], cells[which, pl.ds(HALF + at, 640)]
+            at = pl.multiple_of(step * 2 * slab, 2 * slab)
+            total = dot_last(sent[which, 0], cells[part][which, pl.ds(at, 2 * slab)]) + dot_last(
+                sent[which, 1], cells[part][which, pl.ds(4 * slab + at, 2 * slab)]
             )
             total = total[:16] + total[16:]
-            edge_send[which, 0, :, pl.ds(at, 640)] = total[:8]
-            edge_send[which, 1, :, pl.ds(at, 640)] = total[8:]
+            edge_send[part][which, 0, :, pl.ds(at, 2 * slab)] = total[:8]
+            edge_send[part][which, 1, :, pl.ds(at, 2 * slab)] = total[8:]
             return carry
 
-        lax.fori_loop(0, 2, piece, 0)
+        lax.fori_loop(0, 2, piece, 0, unroll=True)
         for step in STEPS[:3]:
-            edge_copy(which, step).start()
-
-    def own_part(which):
-        def piece(row, carry):
-            at = pl.multiple_of(row * SLAB, SLAB)
-            total = jnp.dot(cells[which, pl.ds(at, SLAB)], own[which], preferred_element_type=F32)
-            lined[row] = total[:, :LANES] + total[:, LANES:]
+            edge_copy(which, part, step).start()
+
+    def own_part(which, part):
+        slab = PLANES * PARTS[part][1]
+
+        def piece(step, carry):
+            at = pl.multiple_of(step * 2 * slab, 2 * slab)
+            total = jnp.dot(cells[part][which, pl.ds(at, 2 * slab)], own[which], preferred_element_type=F32)
+            lined[part][pl.ds(2 * step, 2)] = (total[:, :LANES] + total[:, LANES:]).reshape(2, slab, LANES)
             return carry
 
-        lax.fori_loop(0, ROWS, piece, 0)
-
-    def add_edges(which):
+        lax.fori_loop(0, 4, piece, 0, unroll=True)
+
+    def add_edges(which, part):
+        slab = PLANES * PARTS[part][1]
         for step in range(1, AXIAL):
-            edge_copy(which, step).wait_recv()
+            edge_copy(which, part, step).wait_recv()
 
         def piece(step, carry):
-            at = pl.multiple_of(lax.rem(step, 2) * 640, 640)
-            received = edge_recv[which, :, :, pl.ds(at, 640)].reshape(32, 640)
+            at = pl.multiple_of(lax.rem(step, 2) * 2 * slab, 2 * slab)
+            received = edge_recv[part][which, :, :, pl.ds(at, 2 * slab)].reshape(32, 2 * slab)
             high, low = two_terms(received)
             total = dot_first(jnp.concatenate([high, low], axis=0), taken[which, step // 2])
-            total = (total[:, :LANES] + total[:, LANES:]).reshape(2, SLAB, LANES)
-            lined[pl.ds(2 * step, 2)] = lined[pl.ds(2 * step, 2)] + total
+            total = (total[:, :LANES] + total[:, LANES:]).reshape(2, slab, LANES)
+            lined[part][pl.ds(2 * step, 2)] = lined[part][pl.ds(2 * step, 2)] + total
             return carry
 
-        lax.fori_loop(0, 4, piece, 0)
-
-    def wait_edge_sends(which):
-        for step in range(1, AXIAL):
-            edge_copy(which, step).wait_send()
+        lax.fori_loop(0, 4, piece, 0, unroll=True)
 
     def keep_cells(which, row, field, group, value):
+        part = PART_OF[field]
+        first, count = PARTS[part]
         high, low = two_terms(value)
-        at = pl.multiple_of(row * SLAB + field * PLANES + group * 16, 16)
-        cells[which, pl.ds(at, 16), pl.ds(0, LANES)] = high
-        cells[which, pl.ds(at, 16), pl.ds(LANES, LANES)] = low
+        at = pl.multiple_of((row * count + field - first) * PLANES + group * 16, 16)
+        cells[part][which, pl.ds(at, 16), pl.ds(0, LANES)] = high
+        cells[part][which, pl.ds(at, 16), pl.ds(LANES, LANES)] = low
 
     def axial_copy(which, step):
         return pltpu.make_async_remote_copy(
@@ -718,12 +723,18 @@
         def _():
             pl.semaphore_wait(barrier, PEERS)
 
-        send_moments(0, step)
+        send_moments(0, 0, step)
         return carry
 
     lax.fori_loop(0, BLOCKS // 2, azim_group, 0)
+
+    def send_rest(step, carry):
+        send_moments(0, 1, step)
+        return carry
+
+    lax.fori_loop(0, BLOCKS // 2, send_rest, 0)
     send_plane(0, azim_flux[:, 0] + azim_flux[:, 2 * PLANES])
-    for copy in halo_copies(0, deriv_halo, azim_flux, 1):
+    for copy in halo_copies(0):
         copy.start()
 
     def axial_group(group, carry):
@@ -747,7 +758,8 @@
     send_axial(0, panel_axial[0])
     for load in loads:
         load.wait()
-    send_edges(0)
+    send_edges(0, 0)
+    send_edges(0, 1)
 
     ids = observer_ref[...]
     order = (
@@ -767,51 +779,85 @@
 
     lax.fori_loop(0, ENTRY_ROWS, hot_row, 0)
 
-    own_part(0)
-    reduce_moments(0, DL)
+    for which in range(2):
+        high, low = two_terms(full[which, pl.ds(pl.multiple_of(me_a * LANES, LANES), LANES)])
+        for top in range(2):
+            own[which, pl.ds(top * LANES, LANES), pl.ds(0, LANES)] = high
+            own[which, pl.ds(top * LANES, LANES), pl.ds(LANES, LANES)] = low
+    own_part(0, 0)
+    own_part(0, 1)
+    reduce_moments(0, 0, DL)
+    reduce_moments(0, 1, DL)
     change = take_axial(0) + take_plane(0)
     send_axial(1, base[:, 0] + base[:, 2 * PLANES] - ratio[:, 0] * change)
-    add_edges(0)
+    add_edges(0, 0)
+    add_edges(0, 1)
+
+    def section(part):
+        first, count = PARTS[part]
+
+        def section_group(group, carry):
+            here = pl.ds(pl.multiple_of(group * 16, 16), 16)
+            for field in range(first, first + count):
+                at = pl.ds(pl.multiple_of(field * PLANES + group * 16, 16), 16)
+                inside = pl.ds(pl.multiple_of((field - first) * PLANES + group * 16, 16), 16)
+                flux = [deriv_halo[0, 0, at]] + [azim_flux[row, at] for row in range(ROWS)] + [deriv_halo[1, 0, at]]
+                up = [start_of(start_recv, group, field, 0)]
+                for row in range(ROWS - 1):
+                    up.append(DL * (flux[row + 1] + up[-1]))
+                down = [start_of(start_recv, group, field, 1)]
+                for row in range(ROWS - 1, 0, -1):
+                    down.append(DL * (flux[row + 1] + down[-1]))
+                down = down[::-1]
+                for row in range(ROWS):
+                    deriv = DK * (down[row] - up[row]) + C1 * (flux[row + 2] - flux[row])
+                    value = base[row, at] - ratio[row, here] * (lined[part][row, inside] + deriv)
+                    keep_cells(1, row, field, group, value)
+            return carry
+
+        lax.fori_loop(0, BLOCKS // 2, section_group, 0)
+
+    def smoothed_moments(part):
+        first, count = PARTS[part]
+
+        def moment_group(step, carry):
+            group = group_at(step)
+            for field in range(first, first + count):
+                inside = pl.ds(pl.multiple_of((field - first) * PLANES + group * 16, 16), 16)
+                keep_moments(1, group, field, [lined[part][row, inside] for row in range(ROWS)], FL)
+            send_moments(1, part, step)
+            return carry
+
+        lax.fori_loop(0, BLOCKS // 2, moment_group, 0)
+
+    wait_starts(0, 0)
+    for copy in halo_copies(0):
+        copy.wait_recv()
+    section(0)
+    send_edges(1, 0)
+    wait_starts(0, 1)
+    section(1)
+    send_edges(1, 1)
     send_plane(1, take_axial(1))
-    wait_starts(0)
-    for copy in halo_copies(0, deriv_halo, azim_flux, 1):
-        copy.wait_recv()
-
-    def section_group(group, carry):
-        for field in range(FIELDS):
-            at = pl.ds(pl.multiple_of(field * PLANES + group * 16, 16), 16)
-            here = pl.ds(pl.multiple_of(group * 16, 16), 16)
-            flux = [deriv_halo[0, 0, at]] + [azim_flux[row, at] for row in range(ROWS)] + [deriv_halo[1, 0, at]]
-            up = [start_of(start_recv, group, field, 0)]
-            for row in range(ROWS - 1):
-                up.append(DL * (flux[row + 1] + up[-1]))
-            down = [start_of(start_recv, group, field, 1)]
-            for row in range(ROWS - 1, 0, -1):
-                down.append(DL * (flux[row + 1] + down[-1]))
-            down = down[::-1]
-            for row in range(ROWS):
-                deriv = DK * (down[row] - up[row]) + C1 * (flux[row + 2] - flux[row])
-                value = base[row, at] - ratio[row, here] * (lined[row, at] + deriv)
-                keep_cells(1, row, field, group, value)
-        return carry
-
-    lax.fori_loop(0, BLOCKS // 2, section_group, 0)
-    send_edges(1)
-    own_part(1)
-    add_edges(1)
-
-    keep = pltpu.make_async_copy(lined, lined_hbm, keep_sem)
-    keep.start()
-
-    def moment_group(step, carry):
-        group = group_at(step)
-        for field in range(FIELDS):
-            at = pl.ds(pl.multiple_of(field * PLANES + group * 16, 16), 16)
-            keep_moments(1, group, field, [lined[row, at] for row in range(ROWS)], FL)
-        send_moments(1, step)
-        return carry
-
-    lax.fori_loop(0, BLOCKS // 2, moment_group, 0)
+    own_part(1, 0)
+    own_part(1, 1)
+    add_edges(1, 0)
+    smoothed_moments(0)
+    add_edges(1, 1)
+    smoothed_moments(1)
+    for copy in halo_copies(1):
+        copy.start()
+    keeps = [
+        pltpu.make_async_copy(
+            lined[part],
+            lined_hbm.at[:, pl.ds(PLANES * PARTS[part][0], PLANES * PARTS[part][1])],
+            keep_sem.at[part],
+        )
+        for part in range(2)
+    ]
+    for keep in keeps:
+        keep.start()
+
     source = area_ref[...] * (take_plane(1) - 1.0)
     picks = weight_ref[...]
     low_half = jnp.take_along_axis(
@@ -856,9 +902,8 @@
 
     for step in range(1, 8):
         part_copy(step).start()
-    for copy in halo_copies(1, filter_halo, lined, 2):
-        copy.start()
-    reduce_moments(1, FL)
+    reduce_moments(1, 0, FL)
+    reduce_moments(1, 1, FL)
     total = partial[pl.ds(pl.multiple_of(mine * 64, 64), 64)]
     for step in range(1, 8):
         part_copy(step).wait_recv()
@@ -882,20 +927,24 @@
         owner_copy(step).start()
     own_copy = pltpu.make_async_copy(owner_send.at[chip], owner_hbm.at[0], owner_sem)
     own_copy.start()
-    wait_starts(1)
-    for copy in halo_copies(1, filter_halo, lined, 2):
+    for part in range(2):
+        wait_starts(1, part)
+    for copy in halo_copies(1):
         copy.wait_recv()
 
     own_copy.wait()
     for step in range(1, 16):
         owner_copy(step).wait_recv()
-    keep.wait()
-
-    for which, halo, source_ref, depth in ((0, deriv_halo, azim_flux, 1), (1, filter_halo, lined, 2)):
-        wait_moment_sends(which)
-        wait_start_sends(which)
-        wait_edge_sends(which)
-        for copy in halo_copies(which, halo, source_ref, depth):
+    for keep in keeps:
+        keep.wait()
+
+    for which in range(2):
+        for part in range(2):
+            wait_moment_sends(which, part)
+            wait_start_sends(which, part)
+            for step in range(1, AXIAL):
+                edge_copy(which, part, step).wait_send()
+        for copy in halo_copies(which):
             copy.wait_send()
     for step in range(1, 8):
         part_copy(step).wait_send()
@@ -921,8 +970,9 @@
     weight_ids,
     bin_weights,
 ):
-    own, sent, taken, full = both_tables()
+    sent, taken, full = both_tables()
     rows = PLANES * ROWS
+    slabs = [PLANES * count for _, count in PARTS]
     hbm = pl.BlockSpec(memory_space=pltpu.HBM)
     dma = pltpu.SemaphoreType.DMA
     lined, halo, starts, parts = pl.pallas_call(
@@ -933,7 +983,7 @@
             jax.ShapeDtypeStruct((SLOTS, TILE_ROWS, LANES), F32),
             jax.ShapeDtypeStruct((16, 8, TIME_BINS), F32),
         ),
-        in_specs=[hbm] * 17,
+        in_specs=[hbm] * 16,
         out_specs=(hbm, hbm, hbm, hbm),
         scratch_shapes=[
             pltpu.VMEM((2, 2 * LANES, 2 * LANES), BF16),
@@ -956,13 +1006,13 @@
             pltpu.VMEM((ROWS, SLAB, LANES), F32),
             pltpu.VMEM((ROWS, SLAB, LANES), F32),
             pltpu.VMEM((ROWS, PLANES, LANES), F32),
-            pltpu.VMEM((2, LINES, 2 * LANES), BF16),
-            pltpu.VMEM((ROWS, SLAB, LANES), F32),
-            pltpu.VMEM((2, 2, 8, HALF), F32),
-            pltpu.VMEM((2, AXIAL, 8, HALF), F32),
+            *[pltpu.VMEM((2, ROWS * slab, 2 * LANES), BF16) for slab in slabs],
+            *[pltpu.VMEM((ROWS, slab, LANES), F32) for slab in slabs],
+            *[pltpu.VMEM((2, 2, 8, 4 * slab), F32) for slab in slabs],
+            *[pltpu.VMEM((2, AXIAL, 8, 4 * slab), F32) for slab in slabs],
             pltpu.VMEM((2, SLOTS, TILE_ROWS, LANES), F32),
-            pltpu.VMEM((2, AZIM, SHARE[0], LANES), F32),
-            pltpu.VMEM((2, AZIM, SHARE[0], LANES), F32),
+            pltpu.VMEM((2, 2, AZIM, 16, LANES), F32),
+            pltpu.VMEM((2, 2, AZIM, 16, LANES), F32),
             pltpu.VMEM((SLOTS, TILE_ROWS, LANES), F32),
             pltpu.VMEM((2, 1, SLAB, LANES), F32),
             pltpu.VMEM((OBSERVERS, ENTRY_ROWS * LANES), BF16),
@@ -975,19 +1025,19 @@
             pltpu.VMEM((2, ROWS, LANES), F32),
             pltpu.VMEM((2, AXIAL, ROWS, LANES), F32),
             pltpu.VMEM((BLOCKS // 2, ROWS, LANES), F32),
+            dma((2,)),
             dma(()),
-            dma(()),
-            dma((15,)),
+            dma((11,)),
             dma((5, BLOCKS // 2)),
             dma((2, BLOCKS // 2)),
-            dma((2, 3)),
-            dma((2, 3)),
-            dma((2,)),
-            dma((2,)),
-            dma((2,)),
-            dma((2,)),
+            dma((2, 2, 3)),
+            dma((2, 2, 3)),
             dma((2, 2)),
             dma((2, 2)),
+            dma((2, 2)),
+            dma((2, 2)),
+            dma((2, 2, 2)),
+            dma((2, 2, 2)),
             dma((7,)),
             dma((7,)),
             dma((15,)),
@@ -1001,7 +1051,6 @@
             collective_id=0, has_side_effects=True
         ),
     )(
-        jnp.asarray(own),
         jnp.asarray(sent),
         jnp.asarray(taken),
         density.reshape(rows, LANES),

time: 49.6 us -> 46.5 us (0.938)
  Pallas kernels: 48.8 us -> 45.8 us
    pallas_call x1, Pallas kernels: 45.8 us -> 42.8 us  [per_device(): pl.pallas_call(kernel, out_shape=(jax.ShapeDtypeStruct((ROWS, SLAB, LANES...]
where the time goes in v6:
time: 46.5 us; the launch traced here: 46.4 us
  Pallas kernels  45.8 us (98%)
  between operations  0.64 us (1%)
    pallas_call x1, Pallas kernels, per_device(): pl.pallas_call(kernel, out_shape=(jax.ShapeDtypeStruct((ROWS, SLAB, LANES...  42.8 us
    pallas_call x1, Pallas kernels, per_device(): pl.pallas_call(finish_kernel, out_shape=(jax.ShapeDtypeStruct((FIELDS, ro...  2.97 us

profile of v6, /device:TPU:1, one launch (start us, length us, event | category | flops | bytes accessed | tf_op | source)
XLA Modules:
  0.0 46.4 jit_solution(9856493862355079873)
XLA Ops:
  0.6 42.8 %shard_map.167 = (f32[8,320,128]{2,1,0:T(8,128)}, f32[2,2,320,128]{3,2,1,0:T(8,128)}, f32[16,40,128]{2,1,0:T(8,128)}, f32[16,8,128]{2,1,0:T(8,128)}) custom-call(bf16[4,2,2,32,256]{4,3,2,1,0:T(8,128)(2,1)} %constant.8.clone.sent_hbm, bf16[4,2,2,64,256]{4,3,2,1,0:T(8,128)(2,1)} %constant.9.clone.taken_hbm, f32[512,128]{1,0:T(8,128)} %bitcast.20, ...), custom_call_target="tpu_custom_call" | custom-call | tf_op jit(solution)/shard_map/pallas_call | solution.py:978
  43.4 3.0 %shard_map.168 = (f32[5,512,128]{2,1,0:T(8,128)}, f32[4,128]{1,0:T(4,128)}) custom-call(f32[8,5,64,128]{3,2,1,0:T(8,128)} %bitcast.15, f32[4,5,64,128]{3,2,1,0:T(8,128)} %bitcast.19, f32[16,40,128]{2,1,0:T(8,128)} %get-tuple-element.10.start_hbm, f32[16,8,128]{2,1,0:T(8,128)} %get-tuple-element.11.part_hbm), custom_call_target="tpu_custom_call" | custom-call | tf_op jit(solution)/shard_map/pallas_call | solution.py:1071

commit v7 on v6

--- a/solution.py
+++ b/solution.py
@@ -186,71 +186,44 @@
 
 
 def finish_kernel(
-    lined_hbm,
-    halo_hbm,
-    start_hbm,
-    part_hbm,
-    state_hbm,
-    signal_hbm,
-    lined,
-    halo,
-    starts,
-    final,
-    parts,
-    signals,
-    load_sem,
-    store_sem,
-    part_sem,
+    near_hbm, start_hbm, part_hbm, state_hbm, signal_hbm, near, starts, final, parts, signals, load_sem, store_sem, part_sem
 ):
     part_copy = pltpu.make_async_copy(part_hbm, parts, part_sem.at[0])
     signal_copy = pltpu.make_async_copy(signals, signal_hbm, part_sem.at[1])
 
     def loads(group):
-        slots = pl.ds(pl.multiple_of(4 * group, 4), 4)
-        planes = pl.ds(pl.multiple_of(16 * group, 16), 16)
+        slots = pl.ds(4 * group, 4)
+        planes = pl.ds(16 * group, 16)
         return [
             pltpu.make_async_copy(start_hbm.at[slots], starts.at[slots], load_sem.at[group, 0]),
-            pltpu.make_async_copy(lined_hbm.at[:, :, planes], lined.at[:, :, planes], load_sem.at[group, 1]),
-            pltpu.make_async_copy(halo_hbm.at[:, :, planes], halo.at[:, :, planes], load_sem.at[group, 2]),
+            pltpu.make_async_copy(near_hbm.at[:, :, planes], near.at[:, :, planes], load_sem.at[group, 1]),
         ]
 
     def store(group):
-        planes = pl.ds(pl.multiple_of(group * 128, 128), 128)
+        planes = pl.ds(128 * group, 128)
         return pltpu.make_async_copy(final.at[:, planes], state_hbm.at[:, planes], store_sem.at[group])
 
     for group in range(BLOCKS // 2):
         for load in loads(group):
             load.start()
-        if group == 0:
-            part_copy.start()
-
-    def final_group(group, carry):
+    part_copy.start()
+
+    for group in range(BLOCKS // 2):
         for load in loads(group):
             load.wait()
-        planes = pl.ds(pl.multiple_of(group * 16, 16), 16)
+        planes = pl.ds(16 * group, 16)
         for field in range(FIELDS):
-            value = [halo[row, field, planes] for row in range(2)]
-            value += [lined[row, field, planes] for row in range(ROWS)]
-            value += [halo[2 + row, field, planes] for row in range(2)]
-            up = [start_of(starts, group, field, 0)]
-            for row in range(ROWS - 1):
-                up.append(FL * (value[row + 2] + up[-1]))
-            down = [start_of(starts, group, field, 1)]
-            for row in range(ROWS - 1, 0, -1):
-                down.append(FL * (value[row + 2] + down[-1]))
-            down = down[::-1]
+            up = FK * start_of(starts, group, field, 0)
+            down = FK * start_of(starts, group, field, 1)
             for row in range(ROWS):
-                near = E1 * (value[row + 1] + value[row + 3]) + E2 * (value[row] + value[row + 4])
-                result = FK * (up[row] + down[row]) + (FK + E0) * value[row + 2] + near
-                final[field, pl.ds(group * 128 + row, 16, stride=ROWS)] = result
+                result = near[row, field, planes] + (FL**row * up + FL ** (ROWS - 1 - row) * down)
+                final[field, pl.ds(128 * group + row, 16, stride=ROWS)] = result
         store(group).start()
-        return carry
-
-    final_group(0, 0)
-    part_copy.wait()
-    signals[...] = jnp.sum(parts[...], axis=0)[:4]
-    signal_copy.start()
-    lax.fori_loop(1, BLOCKS // 2, final_group, 0)
+        if group == 0:
+            part_copy.wait()
+            signals[...] = jnp.sum(parts[...], axis=0)[:4]
+            signal_copy.start()
+
     for group in range(BLOCKS // 2):
         store(group).wait()
     signal_copy.wait()
@@ -273,8 +246,7 @@
     table_hbm,
     azimuth_hbm,
     full_hbm,
-    lined_hbm,
-    filter_halo,
+    near_hbm,
     start_hbm,
     owner_hbm,
     own,
@@ -310,6 +282,8 @@
     start_send,
     start_recv,
     deriv_halo,
+    filter_halo,
+    near,
     observer_hot,
     bin_hot,
     partial,
@@ -395,11 +369,6 @@
     for step in range(BLOCKS // 2):
         for load in early_loads(group_at(step)):
             load.start()
-    for group in range(BLOCKS // 2):
-        for load in late_loads(group):
-            load.start()
-    for load in loads:
-        load.start()
 
     starts = (start_recv, start_hbm)
     cells, lined = (cells_a, cells_b), (lined_a, lined_b)
@@ -709,6 +678,8 @@
         group = group_at(step)
         for load in early_loads(group):
             load.wait()
+        for load in late_loads(group):
+            load.start()
         flux = [[None] * ROWS for _ in range(FIELDS)]
         for row in range(ROWS):
             at, rho, vel, prs, vol, energy = cells_at(group, row)
@@ -727,6 +698,9 @@
         return carry
 
     lax.fori_loop(0, BLOCKS // 2, azim_group, 0)
+
+    for load in loads:
+        load.start()
 
     def send_rest(step, carry):
         send_moments(0, 1, step)
@@ -775,6 +749,8 @@
         rows = lax.broadcasted_iota(jnp.int32, (OBSERVERS, LANES), 0)
         at = pl.multiple_of(row * LANES, LANES)
         observer_hot[:, pl.ds(at, LANES)] = jnp.where(rows == wanted, 1.0, 0.0).astype(BF16)
+        same = lax.broadcasted_iota(jnp.int32, (TIME_BINS, LANES), 0) == bin_ref[pl.ds(row, 1)]
+        bin_hot[pl.ds(0, TIME_BINS), pl.ds(at, LANES)] = jnp.where(same, 1.0, 0.0).astype(BF16)
         return carry
 
     lax.fori_loop(0, ENTRY_ROWS, hot_row, 0)
@@ -835,10 +811,10 @@
         copy.wait_recv()
     section(0)
     send_edges(1, 0)
+    send_plane(1, take_axial(1))
     wait_starts(0, 1)
     section(1)
     send_edges(1, 1)
-    send_plane(1, take_axial(1))
     own_part(1, 0)
     own_part(1, 1)
     add_edges(1, 0)
@@ -847,16 +823,6 @@
     smoothed_moments(1)
     for copy in halo_copies(1):
         copy.start()
-    keeps = [
-        pltpu.make_async_copy(
-            lined[part],
-            lined_hbm.at[:, pl.ds(PLANES * PARTS[part][0], PLANES * PARTS[part][1])],
-            keep_sem.at[part],
-        )
-        for part in range(2)
-    ]
-    for keep in keeps:
-        keep.start()
 
     source = area_ref[...] * (take_plane(1) - 1.0)
     picks = weight_ref[...]
@@ -873,12 +839,11 @@
     partial[pl.ds(ENTRY_ROWS, ENTRY_ROWS)] = low.astype(F32)
 
     def bin_row(row, carry):
-        same = lax.broadcasted_iota(jnp.int32, (TIME_BINS, LANES), 0) == bin_ref[pl.ds(row, 1)]
         at = pl.multiple_of(row * LANES, LANES)
-        bin_hot[pl.ds(0, TIME_BINS), pl.ds(at, LANES)] = jnp.where(same, partial[pl.ds(row, 1)], 0.0).astype(BF16)
-        bin_hot[pl.ds(TIME_BINS, TIME_BINS), pl.ds(at, LANES)] = jnp.where(
-            same, partial[pl.ds(ENTRY_ROWS + row, 1)], 0.0
-        ).astype(BF16)
+        mask = bin_hot[pl.ds(0, TIME_BINS), pl.ds(at, LANES)]
+        for term in range(2):
+            value = jnp.broadcast_to(partial[pl.ds(term * ENTRY_ROWS + row, 1)], (TIME_BINS, LANES)).astype(BF16)
+            bin_hot[pl.ds(term * TIME_BINS, TIME_BINS), pl.ds(at, LANES)] = mask * value
         return carry
 
     lax.fori_loop(0, ENTRY_ROWS, bin_row, 0)
@@ -927,16 +892,40 @@
         owner_copy(step).start()
     own_copy = pltpu.make_async_copy(owner_send.at[chip], owner_hbm.at[0], owner_sem)
     own_copy.start()
+    for copy in halo_copies(1):
+        copy.wait_recv()
+
+    def near_group(group, carry):
+        for field in range(FIELDS):
+            part = PART_OF[field]
+            at = pl.ds(pl.multiple_of(field * PLANES + group * 16, 16), 16)
+            inside = pl.ds(pl.multiple_of((field - PARTS[part][0]) * PLANES + group * 16, 16), 16)
+            value = [filter_halo[0, row, at] for row in range(2)]
+            value += [lined[part][row, inside] for row in range(ROWS)]
+            value += [filter_halo[1, row, at] for row in range(2)]
+            up = [None]
+            down = [None]
+            for row in range(ROWS - 1):
+                up.append(FL * value[row + 2] if row == 0 else FL * (value[row + 2] + up[-1]))
+                back = value[ROWS + 1 - row]
+                down.append(FL * back if row == 0 else FL * (back + down[-1]))
+            down = down[::-1]
+            for row in range(ROWS):
+                tails = up[row] if row == ROWS - 1 else down[row] if row == 0 else up[row] + down[row]
+                edges = E1 * (value[row + 1] + value[row + 3]) + E2 * (value[row] + value[row + 4])
+                near[row, at] = FK * tails + (FK + E0) * value[row + 2] + edges
+        return carry
+
+    lax.fori_loop(0, BLOCKS // 2, near_group, 0)
+    keep = pltpu.make_async_copy(near, near_hbm, keep_sem)
+    keep.start()
     for part in range(2):
         wait_starts(1, part)
-    for copy in halo_copies(1):
-        copy.wait_recv()
 
     own_copy.wait()
     for step in range(1, 16):
         owner_copy(step).wait_recv()
-    for keep in keeps:
-        keep.wait()
+    keep.wait()
 
     for which in range(2):
         for part in range(2):
@@ -975,16 +964,15 @@
     slabs = [PLANES * count for _, count in PARTS]
     hbm = pl.BlockSpec(memory_space=pltpu.HBM)
     dma = pltpu.SemaphoreType.DMA
-    lined, halo, starts, parts = pl.pallas_call(
+    near, starts, parts = pl.pallas_call(
         kernel,
         out_shape=(
             jax.ShapeDtypeStruct((ROWS, SLAB, LANES), F32),
-            jax.ShapeDtypeStruct((2, 2, SLAB, LANES), F32),
             jax.ShapeDtypeStruct((SLOTS, TILE_ROWS, LANES), F32),
             jax.ShapeDtypeStruct((16, 8, TIME_BINS), F32),
         ),
         in_specs=[hbm] * 16,
-        out_specs=(hbm, hbm, hbm, hbm),
+        out_specs=(hbm, hbm, hbm),
         scratch_shapes=[
             pltpu.VMEM((2, 2 * LANES, 2 * LANES), BF16),
             pltpu.VMEM((2, 2, 32, 2 * LANES), BF16),
@@ -1015,6 +1003,8 @@
             pltpu.VMEM((2, 2, AZIM, 16, LANES), F32),
             pltpu.VMEM((SLOTS, TILE_ROWS, LANES), F32),
             pltpu.VMEM((2, 1, SLAB, LANES), F32),
+            pltpu.VMEM((2, 2, SLAB, LANES), F32),
+            pltpu.VMEM((ROWS, SLAB, LANES), F32),
             pltpu.VMEM((OBSERVERS, ENTRY_ROWS * LANES), BF16),
             pltpu.VMEM((2 * TIME_BINS, ENTRY_ROWS * LANES), BF16),
             pltpu.VMEM((OBSERVERS, TIME_BINS), F32),
@@ -1025,7 +1015,7 @@
             pltpu.VMEM((2, ROWS, LANES), F32),
             pltpu.VMEM((2, AXIAL, ROWS, LANES), F32),
             pltpu.VMEM((BLOCKS // 2, ROWS, LANES), F32),
-            dma((2,)),
+            dma(()),
             dma(()),
             dma((11,)),
             dma((5, BLOCKS // 2)),
@@ -1074,11 +1064,10 @@
             jax.ShapeDtypeStruct((FIELDS, rows, LANES), F32),
             jax.ShapeDtypeStruct((4, TIME_BINS), F32),
         ),
-        in_specs=[hbm] * 4,
+        in_specs=[hbm] * 3,
         out_specs=(hbm, hbm),
         scratch_shapes=[
             pltpu.VMEM((ROWS, FIELDS, PLANES, LANES), F32),
-            pltpu.VMEM((4, FIELDS, PLANES, LANES), F32),
             pltpu.VMEM((SLOTS, TILE_ROWS, LANES), F32),
             pltpu.VMEM((FIELDS, rows, LANES), F32),
             pltpu.VMEM((16, 8, TIME_BINS), F32),
@@ -1088,8 +1077,7 @@
             dma((2,)),
         ],
     )(
-        lined.reshape(ROWS, FIELDS, PLANES, LANES),
-        halo.reshape(4, FIELDS, PLANES, LANES),
+        near.reshape(ROWS, FIELDS, PLANES, LANES),
         starts,
         parts,
     )

time: 46.5 us -> 46.2 us (level)
  Pallas kernels: 45.8 us -> 45.3 us
where the time goes in v7:
time: 46.2 us; the launch traced here: 46 us
  Pallas kernels  45.3 us (98%)
  between operations  0.64 us (1%)
    pallas_call x1, Pallas kernels, per_device(): pl.pallas_call(kernel, out_shape=(jax.ShapeDtypeStruct((ROWS, SLAB, LANES...  42.8 us
    pallas_call x1, Pallas kernels, per_device(): pl.pallas_call(finish_kernel, out_shape=(jax.ShapeDtypeStruct((FIELDS, ro...  2.57 us

profile of v7, /device:TPU:1, one launch (start us, length us, event | category | flops | bytes accessed | tf_op | source)
XLA Modules:
  0.0 46.0 jit_solution(2442772194796299497)
XLA Ops:
  0.6 42.8 %shard_map.167 = (f32[8,320,128]{2,1,0:T(8,128)}, f32[16,40,128]{2,1,0:T(8,128)}, f32[16,8,128]{2,1,0:T(8,128)}) custom-call(bf16[4,2,2,32,256]{4,3,2,1,0:T(8,128)(2,1)} %constant.8.clone.sent_hbm, bf16[4,2,2,64,256]{4,3,2,1,0:T(8,128)(2,1)} %constant.9.clone.taken_hbm, f32[512,128]{1,0:T(8,128)} %bitcast.18, f32[3,512,128]{2,1,0:T(8,128)} %bitcast.15, ...), custom_call_target="tpu_custom_call" | custom-call | tf_op jit(solution)/shard_map/pallas_call | solution.py:967
  43.4 2.6 %shard_map.168 = (f32[5,512,128]{2,1,0:T(8,128)}, f32[4,128]{1,0:T(4,128)}) custom-call(f32[8,5,64,128]{3,2,1,0:T(8,128)} %bitcast.14, f32[16,40,128]{2,1,0:T(8,128)} %get-tuple-element.8.start_hbm, f32[16,8,128]{2,1,0:T(8,128)} %get-tuple-element.9.part_hbm), custom_call_target="tpu_custom_call" | custom-call | tf_op jit(solution)/shard_map/pallas_call | solution.py:1061

commit v8 on v7

--- a/solution.py
+++ b/solution.py
@@ -177,6 +177,15 @@
 
 def dot_first(left, right):
     return lax.dot_general(left, right, (((0,), (0,)), ((), ())), preferred_element_type=F32)
+
+
+def near_tails(values, root):
+    up, down = [None], [None]
+    for row in range(ROWS - 1):
+        last, back = values[row], values[ROWS - 1 - row]
+        up.append(root * (last if up[-1] is None else last + up[-1]))
+        down.append(root * (back if down[-1] is None else back + down[-1]))
+    return list(zip(up, down[::-1]))
 
 
 def start_of(starts, group, field, side):
@@ -769,6 +778,21 @@
     add_edges(0, 0)
     add_edges(0, 1)
 
+    def near_section(group, carry):
+        here = pl.ds(pl.multiple_of(group * 16, 16), 16)
+        for field in range(FIELDS):
+            part = PART_OF[field]
+            at = pl.ds(pl.multiple_of(field * PLANES + group * 16, 16), 16)
+            inside = pl.ds(pl.multiple_of((field - PARTS[part][0]) * PLANES + group * 16, 16), 16)
+            flux = [deriv_halo[0, 0, at]] + [azim_flux[row, at] for row in range(ROWS)] + [deriv_halo[1, 0, at]]
+            tails = near_tails(flux[1:-1], DL)
+            for row in range(ROWS):
+                up, down = tails[row]
+                spread = down if up is None else -up if down is None else down - up
+                deriv = DK * spread + C1 * (flux[row + 2] - flux[row])
+                base[row, at] = base[row, at] - ratio[row, here] * (lined[part][row, inside] + deriv)
+        return carry
+
     def section(part):
         first, count = PARTS[part]
 
@@ -776,19 +800,11 @@
             here = pl.ds(pl.multiple_of(group * 16, 16), 16)
             for field in range(first, first + count):
                 at = pl.ds(pl.multiple_of(field * PLANES + group * 16, 16), 16)
-                inside = pl.ds(pl.multiple_of((field - first) * PLANES + group * 16, 16), 16)
-                flux = [deriv_halo[0, 0, at]] + [azim_flux[row, at] for row in range(ROWS)] + [deriv_halo[1, 0, at]]
-                up = [start_of(start_recv, group, field, 0)]
-                for row in range(ROWS - 1):
-                    up.append(DL * (flux[row + 1] + up[-1]))
-                down = [start_of(start_recv, group, field, 1)]
-                for row in range(ROWS - 1, 0, -1):
-                    down.append(DL * (flux[row + 1] + down[-1]))
-                down = down[::-1]
+                up = DK * start_of(start_recv, group, field, 0)
+                down = DK * start_of(start_recv, group, field, 1)
                 for row in range(ROWS):
-                    deriv = DK * (down[row] - up[row]) + C1 * (flux[row + 2] - flux[row])
-                    value = base[row, at] - ratio[row, here] * (lined[part][row, inside] + deriv)
-                    keep_cells(1, row, field, group, value)
+                    far = DL ** (ROWS - 1 - row) * down - DL**row * up
+                    keep_cells(1, row, field, group, base[row, at] - ratio[row, here] * far)
             return carry
 
         lax.fori_loop(0, BLOCKS // 2, section_group, 0)
@@ -806,9 +822,10 @@
 
         lax.fori_loop(0, BLOCKS // 2, moment_group, 0)
 
-    wait_starts(0, 0)
     for copy in halo_copies(0):
         copy.wait_recv()
+    lax.fori_loop(0, BLOCKS // 2, near_section, 0)
+    wait_starts(0, 0)
     section(0)
     send_edges(1, 0)
     send_plane(1, take_axial(1))
@@ -903,15 +920,10 @@
             value = [filter_halo[0, row, at] for row in range(2)]
             value += [lined[part][row, inside] for row in range(ROWS)]
             value += [filter_halo[1, row, at] for row in range(2)]
-            up = [None]
-            down = [None]
-            for row in range(ROWS - 1):
-                up.append(FL * value[row + 2] if row == 0 else FL * (value[row + 2] + up[-1]))
-                back = value[ROWS + 1 - row]
-                down.append(FL * back if row == 0 else FL * (back + down[-1]))
-            down = down[::-1]
+            ends = near_tails(value[2:-2], FL)
             for row in range(ROWS):
-                tails = up[row] if row == ROWS - 1 else down[row] if row == 0 else up[row] + down[row]
+                up, down = ends[row]
+                tails = down if up is None else up if down is None else up + down
                 edges = E1 * (value[row + 1] + value[row + 3]) + E2 * (value[row] + value[row + 4])
                 near[row, at] = FK * tails + (FK + E0) * value[row + 2] + edges
         return carry

time: 46.2 us -> 45.9 us (level)
  no operation moved by 1% of the time
where the time goes in v8:
time: 45.9 us; the launch traced here: 45.8 us
  Pallas kernels  45.1 us (98%)
  between operations  0.64 us (1%)
    pallas_call x1, Pallas kernels, per_device(): pl.pallas_call(kernel, out_shape=(jax.ShapeDtypeStruct((ROWS, SLAB, LANES...  42.5 us
    pallas_call x1, Pallas kernels, per_device(): pl.pallas_call(finish_kernel, out_shape=(jax.ShapeDtypeStruct((FIELDS, ro...  2.57 us

profile of v8, /device:TPU:1, one launch (start us, length us, event | category | flops | bytes accessed | tf_op | source)
XLA Modules:
  0.0 45.8 jit_solution(4012439071841475318)
XLA Ops:
  0.6 42.5 %shard_map.167 = (f32[8,320,128]{2,1,0:T(8,128)}, f32[16,40,128]{2,1,0:T(8,128)}, f32[16,8,128]{2,1,0:T(8,128)}) custom-call(bf16[4,2,2,32,256]{4,3,2,1,0:T(8,128)(2,1)} %constant.8.clone.sent_hbm, bf16[4,2,2,64,256]{4,3,2,1,0:T(8,128)(2,1)} %constant.9.clone.taken_hbm, f32[512,128]{1,0:T(8,128)} %bitcast.18, f32[3,512,128]{2,1,0:T(8,128)} %bitcast.15, ...), custom_call_target="tpu_custom_call" | custom-call | tf_op jit(solution)/shard_map/pallas_call | solution.py:979
  43.2 2.6 %shard_map.168 = (f32[5,512,128]{2,1,0:T(8,128)}, f32[4,128]{1,0:T(4,128)}) custom-call(f32[8,5,64,128]{3,2,1,0:T(8,128)} %bitcast.14, f32[16,40,128]{2,1,0:T(8,128)} %get-tuple-element.8.start_hbm, f32[16,8,128]{2,1,0:T(8,128)} %get-tuple-element.9.part_hbm), custom_call_target="tpu_custom_call" | custom-call | tf_op jit(solution)/shard_map/pallas_call | solution.py:1073

commit v9 on v8

--- a/solution.py
+++ b/solution.py
@@ -340,6 +340,19 @@
         away = jnp.where(step == 0, STEPS[0], jnp.where(step == 1, STEPS[1], jnp.where(step == 2, STEPS[2], 0)))
         return lax.rem(chip // 4 + away, 4)
 
+    barrier = pltpu.get_barrier_semaphore()
+
+    def greet(other_a, other_z):
+        pl.semaphore_signal(barrier, inc=1, device_id=(other_a, other_z), device_id_type=MESH)
+
+    for step in AWAY:
+        for half in range(2):
+            greet(me_a, 2 * chip_at(step) + half)
+    for step in STEPS[:3]:
+        greet(lax.rem(me_a + step, AXIAL), me_z)
+        greet(lax.rem(me_a + step, AXIAL), twin)
+    greet(me_a, twin)
+
     def early_loads(group):
         part = pl.ds(pl.multiple_of(group * 128, 128), 128)
         whole = slice(None)
@@ -383,22 +396,6 @@
     cells, lined = (cells_a, cells_b), (lined_a, lined_b)
     edge_send, edge_recv = (edge_send_a, edge_send_b), (edge_recv_a, edge_recv_b)
 
-    barrier = pltpu.get_barrier_semaphore()
-
-    def greet_azim(step, carry):
-        other = lax.rem(me_z + step, AZIM)
-        pl.semaphore_signal(barrier, inc=1, device_id=(me_a, other), device_id_type=MESH)
-        return carry
-
-    lax.fori_loop(1, AZIM, greet_azim, 0)
-
-    def greet_axial(step, carry):
-        other = lax.rem(me_a + step, AXIAL)
-        pl.semaphore_signal(barrier, inc=1, device_id=(other, me_z), device_id_type=MESH)
-        pl.semaphore_signal(barrier, inc=1, device_id=(other, twin), device_id_type=MESH)
-        return carry
-
-    lax.fori_loop(1, AXIAL, greet_axial, 0)
 
     for part in range(2):
         for which in range(2):
@@ -698,12 +695,6 @@
                 azim_flux[row, pl.ds(pl.multiple_of(field * PLANES + group * 16, 16), 16)] = parts[field]
         for field in range(FIELDS):
             keep_moments(0, group, field, flux[field], DL)
-
-        @pl.when(step == 0)
-        def _():
-            pl.semaphore_wait(barrier, PEERS)
-
-        send_moments(0, 0, step)
         return carry
 
     lax.fori_loop(0, BLOCKS // 2, azim_group, 0)
@@ -711,11 +702,14 @@
     for load in loads:
         load.start()
 
-    def send_rest(step, carry):
-        send_moments(0, 1, step)
-        return carry
-
-    lax.fori_loop(0, BLOCKS // 2, send_rest, 0)
+    pl.semaphore_wait(barrier, PEERS)
+    for part in range(2):
+
+        def send_part(step, carry, part=part):
+            send_moments(0, part, step)
+            return carry
+
+        lax.fori_loop(0, BLOCKS // 2, send_part, 0)
     send_plane(0, azim_flux[:, 0] + azim_flux[:, 2 * PLANES])
     for copy in halo_copies(0):
         copy.start()

time: 45.9 us -> 45.8 us (level)
  no operation moved by 1% of the time
where the time goes in v9:
time: 45.8 us; the launch traced here: 45.6 us
  Pallas kernels  45 us (98%)
  between operations  0.64 us (1%)
    pallas_call x1, Pallas kernels, per_device(): pl.pallas_call(kernel, out_shape=(jax.ShapeDtypeStruct((ROWS, SLAB, LANES...  42.4 us
    pallas_call x1, Pallas kernels, per_device(): pl.pallas_call(finish_kernel, out_shape=(jax.ShapeDtypeStruct((FIELDS, ro...  2.57 us

profile of v9, /device:TPU:1, one launch (start us, length us, event | category | flops | bytes accessed | tf_op | source)
XLA Modules:
  0.0 45.6 jit_solution(8069414644315184527)
XLA Ops:
  0.6 42.4 %shard_map.167 = (f32[8,320,128]{2,1,0:T(8,128)}, f32[16,40,128]{2,1,0:T(8,128)}, f32[16,8,128]{2,1,0:T(8,128)}) custom-call(bf16[4,2,2,32,256]{4,3,2,1,0:T(8,128)(2,1)} %constant.8.clone.sent_hbm, bf16[4,2,2,64,256]{4,3,2,1,0:T(8,128)(2,1)} %constant.9.clone.taken_hbm, f32[512,128]{1,0:T(8,128)} %bitcast.18, f32[3,512,128]{2,1,0:T(8,128)} %bitcast.15, ...), custom_call_target="tpu_custom_call" | custom-call | tf_op jit(solution)/shard_map/pallas_call | solution.py:973
  43.1 2.6 %shard_map.168 = (f32[5,512,128]{2,1,0:T(8,128)}, f32[4,128]{1,0:T(4,128)}) custom-call(f32[8,5,64,128]{3,2,1,0:T(8,128)} %bitcast.14, f32[16,40,128]{2,1,0:T(8,128)} %get-tuple-element.8.start_hbm, f32[16,8,128]{2,1,0:T(8,128)} %get-tuple-element.9.part_hbm), custom_call_target="tpu_custom_call" | custom-call | tf_op jit(solution)/shard_map/pallas_call | solution.py:1067

commit v10 on v9

--- a/solution.py
+++ b/solution.py
@@ -889,7 +889,7 @@
         owner_send[owner, pl.ds(4, 4)] = jnp.zeros((4, LANES), F32)
 
     def owner_copy(step):
-        other = lax.rem(chip + step, 16)
+        other = chip_at(AWAY[step - 1])
         return pltpu.make_async_remote_copy(
             src_ref=owner_send.at[other],
             dst_ref=owner_hbm.at[step],

time: 45.8 us -> 45.8 us (level)
  no operation moved by 1% of the time
where the time goes in v10:
time: 45.8 us; the launch traced here: 45.6 us
  Pallas kernels  45 us (98%)
  between operations  0.64 us (1%)
    pallas_call x1, Pallas kernels, per_device(): pl.pallas_call(kernel, out_shape=(jax.ShapeDtypeStruct((ROWS, SLAB, LANES...  42.4 us
    pallas_call x1, Pallas kernels, per_device(): pl.pallas_call(finish_kernel, out_shape=(jax.ShapeDtypeStruct((FIELDS, ro...  2.57 us

profile of v10, /device:TPU:1, one launch (start us, length us, event | category | flops | bytes accessed | tf_op | source)
XLA Modules:
  0.0 45.6 jit_solution(2211237626197339928)
XLA Ops:
  0.6 42.4 %shard_map.167 = (f32[8,320,128]{2,1,0:T(8,128)}, f32[16,40,128]{2,1,0:T(8,128)}, f32[16,8,128]{2,1,0:T(8,128)}) custom-call(bf16[4,2,2,32,256]{4,3,2,1,0:T(8,128)(2,1)} %constant.8.clone.sent_hbm, bf16[4,2,2,64,256]{4,3,2,1,0:T(8,128)(2,1)} %constant.9.clone.taken_hbm, f32[512,128]{1,0:T(8,128)} %bitcast.18, f32[3,512,128]{2,1,0:T(8,128)} %bitcast.15, ...), custom_call_target="tpu_custom_call" | custom-call | tf_op jit(solution)/shard_map/pallas_call | solution.py:973
  43.0 2.6 %shard_map.168 = (f32[5,512,128]{2,1,0:T(8,128)}, f32[4,128]{1,0:T(4,128)}) custom-call(f32[8,5,64,128]{3,2,1,0:T(8,128)} %bitcast.14, f32[16,40,128]{2,1,0:T(8,128)} %get-tuple-element.8.start_hbm, f32[16,8,128]{2,1,0:T(8,128)} %get-tuple-element.9.part_hbm), custom_call_target="tpu_custom_call" | custom-call | tf_op jit(solution)/shard_map/pallas_call | solution.py:1067

commit v11 on v10

--- a/solution.py
+++ b/solution.py
@@ -465,17 +465,15 @@
                 arrived = moment_recv.at[which, part, :, rows]
                 pltpu.make_async_copy(arrived, arrived, moment_recv_sem.at[which, part]).wait()
 
-                def gather(step, total):
-                    return factor * total + moment_recv[which, part, place(step), rows]
-
-                first = lax.fori_loop(0, AZIM, gather, jnp.zeros((count, LANES), F32), unroll=8) * wrap
-
                 def follow(step, now):
                     other = place(step)
                     start_send[which, part, other, rows] = now
                     return factor * now + moment_recv[which, part, other, rows]
 
-                lax.fori_loop(0, AZIM, follow, first, unroll=8)
+                first = lax.fori_loop(0, AZIM, follow, jnp.zeros((count, LANES), F32), unroll=8) * wrap
+                for step in range(AZIM):
+                    other = place(step)
+                    start_send[which, part, other, rows] = start_send[which, part, other, rows] + factor**step * first
 
                 def hand_out(other):
                     pltpu.make_async_remote_copy(

time: 45.8 us -> 45.8 us (level)
  no operation moved by 1% of the time
where the time goes in v11:
time: 45.8 us; the launch traced here: 45.6 us
  Pallas kernels  45 us (98%)
  between operations  0.64 us (1%)
    pallas_call x1, Pallas kernels, per_device(): pl.pallas_call(kernel, out_shape=(jax.ShapeDtypeStruct((ROWS, SLAB, LANES...  42.4 us
    pallas_call x1, Pallas kernels, per_device(): pl.pallas_call(finish_kernel, out_shape=(jax.ShapeDtypeStruct((FIELDS, ro...  2.57 us

profile of v11, /device:TPU:1, one launch (start us, length us, event | category | flops | bytes accessed | tf_op | source)
XLA Modules:
  0.0 45.6 jit_solution(536634808298075998)
XLA Ops:
  0.6 42.4 %shard_map.167 = (f32[8,320,128]{2,1,0:T(8,128)}, f32[16,40,128]{2,1,0:T(8,128)}, f32[16,8,128]{2,1,0:T(8,128)}) custom-call(bf16[4,2,2,32,256]{4,3,2,1,0:T(8,128)(2,1)} %constant.8.clone.sent_hbm, bf16[4,2,2,64,256]{4,3,2,1,0:T(8,128)(2,1)} %constant.9.clone.taken_hbm, f32[512,128]{1,0:T(8,128)} %bitcast.18, f32[3,512,128]{2,1,0:T(8,128)} %bitcast.15, ...), custom_call_target="tpu_custom_call" | custom-call | tf_op jit(solution)/shard_map/pallas_call | solution.py:971
  43.0 2.6 %shard_map.168 = (f32[5,512,128]{2,1,0:T(8,128)}, f32[4,128]{1,0:T(4,128)}) custom-call(f32[8,5,64,128]{3,2,1,0:T(8,128)} %bitcast.14, f32[16,40,128]{2,1,0:T(8,128)} %get-tuple-element.8.start_hbm, f32[16,8,128]{2,1,0:T(8,128)} %get-tuple-element.9.part_hbm), custom_call_target="tpu_custom_call" | custom-call | tf_op jit(solution)/shard_map/pallas_call | solution.py:1065
